TPU v7x, 128 devices: a whole 4x4x4 slice. The times are simulated.
128 devices in a mesh: row: 16 (over z, x), col: 8 (over y, core).
Axes of the slice: x: 4, y: 4, z: 4, core: 2. Of those that a mesh axis runs over, the one named last changes fastest.
Arguments:
- tokens: bfloat16 [8192, 4096], P('row'), may hold values from -6 to 6
- theta: bfloat16 [96, 1024, 128], P('col', 'row'), may hold values from -0.1875 to 0.1875
- log_sigma2: float32 [96, 1024, 128], P('col', 'row'), may hold values from -8 to -5
- block_rows: int32 [96, 8], P('col'), may hold values from 0 to 31, as said below
- noise: bfloat16 [8192, 12288], P('row', 'col'), may hold values from -6 to 6
- cotangent: bfloat16 [8192, 12288], P('row', 'col'), may hold values from -6 to 6
Outputs:
- output: bfloat16 [8192, 12288], P('row', 'col')
- grad_tokens: float32 [8192, 4096], P('row', 'col')
- grad_theta: float32 [96, 1024, 128], P('col', 'row')
- grad_logvar: float32 [96, 1024, 128], P('col', 'row')
Inputs may be any that keep to these rules, and one draw needn't show every extreme that they name: `block_rows`: each row lists 8 distinct block rows in increasing order; row n contains n modulo 32, the others are drawn uniformly.
All inputs are finite; a program needn't handle non-finite values.
Results may differ from a plain program's by a relative error of at most 0.014.
Values may be sent and summed in bfloat16 or wider, within the bound.
No kernel may reach another device: no remote copies, remote signals or barrier semaphores. Data moves between devices by JAX's collectives and lax.ppermute only.
A program may use at most 192 MiB of HBM per device.

v0:
```python
import math

import jax
import jax.numpy as jnp
from jax import lax
from jax.experimental import pallas as pl
from jax.experimental.pallas import tpu as pltpu
from jax.sharding import Mesh
from jax.sharding import PartitionSpec as P


ROW = ("z", "x")
COL = ("y", "core")
RING = 4
EPS = 1e-06
LANE = 128
f32, bf16 = jnp.float32, jnp.bfloat16
PARAMS = pltpu.CompilerParams(vmem_limit_bytes=60 * 1024 * 1024)
SM = pl.BlockSpec(memory_space=pltpu.SMEM)
VB = pl.BlockSpec(memory_space=pltpu.VMEM)
HB = pl.BlockSpec(memory_space=pl.ANY)
NT = (((1,), (1,)), ((), ()))

GATHER_SIGMA = (("x", "z", 0, 64),)
GATHER_THETA = (("z", "x", 0, 64),)
SCATTER_THETA = (("x", "z", 0, 64),)
SCATTER_VAR = (("z", "x", 0, 64),)
PLACE = {"z": 0, "x": 1, "y": 2, "core": 3}


def sds(shape, dtype):
    return jax.ShapeDtypeStruct(shape, dtype)


def at_block(index):
    return pl.ds(pl.multiple_of(index * LANE, LANE), LANE)


def sent(value, axis, step):
    n = lax.axis_size(axis)
    return lax.ppermute(value, axis, [(i, (i + step) % n) for i in range(n)])


def steps_of(value, axis):
    return [sent(value, axis, k) for k in range(1, RING)]


def steps_sent(values, axis):
    return [values[0]] + [sent(values[k], axis, k) for k in range(1, RING)]


def prep_kernel(paths_s, paths_t):
    def kernel(ls_ref, theta_ref, *outs):
        for n in range(theta_ref.shape[0]):
            at = slice(n * LANE, (n + 1) * LANE)
            for (_, _, lo, hi), o in zip(paths_s, outs):
                o[:, at] = jnp.exp(ls_ref[n, lo:hi]).astype(bf16)
            for (_, _, lo, hi), o in zip(paths_t, outs[len(paths_s) :]):
                o[:, at] = theta_ref[n, lo:hi]

    return kernel


def prep(ls, theta):
    c, _, b = theta.shape
    shapes = [sds((hi - lo, c * b), bf16) for _, _, lo, hi in GATHER_SIGMA + GATHER_THETA]
    outs = pl.pallas_call(
        prep_kernel(GATHER_SIGMA, GATHER_THETA), out_shape=shapes, compiler_params=PARAMS, name="prep"
    )(ls, theta)
    return outs[: len(GATHER_SIGMA)], outs[len(GATHER_SIGMA) :]


def gather(pieces, paths):
    blocks = [jnp.stack([p] + steps_of(p, path[0])) for p, path in zip(pieces, paths)]
    return [[b] + steps_of(b, path[1]) for b, path in zip(blocks, paths)]


def gather_copies(place, paths, groups, whole, sem):
    copies = []
    for (one, two, lo, hi), refs in zip(paths, groups):
        for k in range(RING):
            for j in range(RING):
                spot = {one: (place[PLACE[one]] - j) & 3, two: (place[PLACE[two]] - k) & 3}
                copies.append(pltpu.make_async_copy(refs[k].at[j], whole.at[spot["z"], spot["x"], lo:hi, :], sem))
    return copies


def chunked(refs, size):
    return [refs[i : i + size] for i in range(0, len(refs), size)]


def block_column(whole, n):
    blk = whole[:, :, :, at_block(n)]
    return blk.reshape(-1, LANE)


def scatter_copies(place, paths, held, groups, sem):
    copies = []
    for (one, _, lo, hi), refs in zip(paths, groups):
        for k in range(RING):
            spot = (place[PLACE[one]] + k) & 3
            src = held.at[spot, :, lo:hi, :] if one == "z" else held.at[:, spot, lo:hi, :]
            copies.append(pltpu.make_async_copy(src, refs[k], sem))
    return copies


def scatter_shapes(paths, ff):
    return [sds((RING, hi - lo, ff), bf16) for _, _, lo, hi in paths for _ in range(RING)]


def sum_kernel(paths):
    def kernel(place, *refs):
        ins, outs = refs[: RING * len(paths)], refs[RING * len(paths) :]
        for path, arrived, left in zip(paths, chunked(ins, RING), chunked(outs, RING)):
            own = place[PLACE[path[1]]]
            for k in range(RING):
                spot = (own + k) & 3
                total = arrived[0][spot].astype(f32)
                for r in arrived[1:]:
                    total = total + r[spot].astype(f32)
                left[k][...] = total.astype(bf16)

    return kernel


def scatter(parts, paths, place):
    ins = []
    for path, group in zip(paths, chunked(parts, RING)):
        ins += [group[0]] + [sent(group[k], path[0], k) for k in range(1, RING)]
    ff = parts[0].shape[2]
    shapes = [sds((hi - lo, ff), bf16) for _, _, lo, hi in paths for _ in range(RING)]
    mid = pl.pallas_call(
        sum_kernel(paths), out_shape=shapes, in_specs=[SM] + [VB] * len(ins), compiler_params=PARAMS
    )(place, *ins)
    arrived = []
    for path, group in zip(paths, chunked(mid, RING)):
        arrived += [group[0]] + [sent(group[k], path[1], k) for k in range(1, RING)]
    return arrived


def final_kernel(paths, scale, with_sigma):
    def kernel(*refs):
        ls = refs[0] if with_sigma else None
        ins, out = refs[int(with_sigma) : -1], refs[-1]
        for n in range(out.shape[0]):
            at = slice(n * LANE, (n + 1) * LANE)
            for (_, _, lo, hi), group in zip(paths, chunked(ins, RING)):
                total = group[0][:, at].astype(f32)
                for r in group[1:]:
                    total = total + r[:, at].astype(f32)
                if with_sigma:
                    total = total * jnp.exp(ls[n, lo:hi])
                out[n, lo:hi] = total * scale

    return kernel


def final(arrived, paths, shape, scale, ls):
    args = ([] if ls is None else [ls]) + list(arrived)
    return pl.pallas_call(
        final_kernel(paths, scale, ls is not None), out_shape=sds(shape, f32), compiler_params=PARAMS
    )(*args)


def early_kernel(rows, place, tok, cot, *refs):
    outs, (sq_out, sqt_out, tokt, held, sq, sqt, sems) = refs[:-7], refs[-7:]
    blocks = tok.shape[1] // LANE
    ks = rows.shape[1]
    for k in range(blocks):
        at = slice(k * LANE, (k + 1) * LANE)
        wide = tok[:, at].astype(f32)
        sq[:, at] = (wide * wide).astype(bf16)
        turned = tok[:, at].T
        tokt[k] = turned
        wide = turned.astype(f32)
        sqt[k] = (wide * wide).astype(bf16)
    saves = [pltpu.make_async_copy(sq, sq_out, sems.at[0]), pltpu.make_async_copy(sqt, sqt_out, sems.at[1])]
    for c in saves:
        c.start()

    def step(n, _):
        lhs = jnp.concatenate([tokt[rows[n, s]] for s in range(ks)], axis=0)
        part = jnp.dot(lhs, cot[:, at_block(n)], preferred_element_type=f32)
        held[:, :, :, at_block(n)] = part.astype(bf16).reshape(RING, RING, -1, LANE)
        return 0

    lax.fori_loop(0, cot.shape[1] // LANE, step, 0)
    copies = scatter_copies(place, SCATTER_THETA, held, chunked(outs, RING), sems.at[2])
    for c in copies:
        c.start()
    for c in saves + copies:
        c.wait()


def early(rows, place, tok, cot, own):
    t, d = tok.shape
    ff = cot.shape[1]
    shapes = scatter_shapes(SCATTER_THETA, ff) + [sds((t, d), bf16), sds((d // LANE, LANE, t), bf16)]
    outs = pl.pallas_call(
        early_kernel,
        out_shape=shapes,
        in_specs=[SM, SM, VB, VB],
        out_specs=[HB] * len(shapes),
        scratch_shapes=[
            pltpu.VMEM((d // LANE, LANE, t), bf16),
            pltpu.VMEM((RING, RING, own, ff), bf16),
            pltpu.VMEM((t, d), bf16),
            pltpu.VMEM((d // LANE, LANE, t), bf16),
            pltpu.SemaphoreType.DMA((3,)),
        ],
        compiler_params=PARAMS,
        name="early",
    )(rows, place, tok, cot)
    return outs[:-2], outs[-2], outs[-1]


def middle_kernel(rows, place, sq_in, sqt_in, noise, cot, *refs):
    n_in = RING * len(GATHER_SIGMA)
    sigma_refs, outs = refs[:n_in], refs[n_in:-9]
    gv_out, rn_out, sq, sqt, whole, held, gv, rn, sems = refs[-9:]
    ks = rows.shape[1]
    loads = gather_copies(place, GATHER_SIGMA, chunked(sigma_refs, RING), whole, sems.at[0])
    loads.append(pltpu.make_async_copy(sq_in, sq, sems.at[1]))
    late = pltpu.make_async_copy(sqt_in, sqt, sems.at[2])
    for c in loads:
        c.start()
    late.start()
    for c in loads:
        c.wait()

    def step(n, _):
        at = at_block(n)
        lhs = jnp.concatenate([sq[:, at_block(rows[n, s])] for s in range(ks)], axis=1)
        var = jnp.dot(lhs, block_column(whole, n), preferred_element_type=f32)
        root = jnp.sqrt(var + EPS)
        draw = noise[:, at].astype(f32)
        rn[:, at] = root * draw
        grad = (cot[:, at].astype(f32) * draw / (2.0 * root)).astype(bf16)
        gv[:, at] = grad

        @pl.when(n == 0)
        def _():
            late.wait()

        lhs = jnp.concatenate([sqt[rows[n, s]] for s in range(ks)], axis=0)
        part = jnp.dot(lhs, grad, preferred_element_type=f32)
        held[:, :, :, at] = part.astype(bf16).reshape(RING, RING, -1, LANE)
        return 0

    lax.fori_loop(0, cot.shape[1] // LANE, step, 0)
    copies = scatter_copies(place, SCATTER_VAR, held, chunked(outs, RING), sems.at[3])
    copies.append(pltpu.make_async_copy(gv, gv_out, sems.at[4]))
    copies.append(pltpu.make_async_copy(rn, rn_out, sems.at[5]))
    for c in copies:
        c.start()
    for c in copies:
        c.wait()


def middle(rows, place, sq, sqt, noise, cot, sigma, own):
    t, d = sq.shape
    ff = cot.shape[1]
    shapes = scatter_shapes(SCATTER_VAR, ff) + [sds((t, ff), bf16), sds((t, ff), f32)]
    refs = [r for group in sigma for r in group]
    outs = pl.pallas_call(
        middle_kernel,
        out_shape=shapes,
        in_specs=[SM, SM, HB, HB, VB, VB] + [HB] * len(refs),
        out_specs=[HB] * len(shapes),
        scratch_shapes=[
            pltpu.VMEM((t, d), bf16),
            pltpu.VMEM((d // LANE, LANE, t), bf16),
            pltpu.VMEM((RING, RING, own, ff), bf16),
            pltpu.VMEM((RING, RING, own, ff), bf16),
            pltpu.VMEM((t, ff), bf16),
            pltpu.VMEM((t, ff), f32),
            pltpu.SemaphoreType.DMA((6,)),
        ],
        compiler_params=PARAMS,
        name="middle",
    )(rows, place, sq, sqt, noise, cot, *refs)
    return outs[:-2], outs[-2], outs[-1]


def late_kernel(rows, place, tok, cot, gv, rn, *refs):
    n_s, n_t = RING * len(GATHER_SIGMA), RING * len(GATHER_THETA)
    sigma_refs, theta_refs = refs[:n_s], refs[n_s : n_s + n_t]
    out, away, home, sigma, theta, acc, sem = refs[n_s + n_t :]
    ks = rows.shape[1]
    loads = gather_copies(place, GATHER_SIGMA, chunked(sigma_refs, RING), sigma, sem)
    loads += gather_copies(place, GATHER_THETA, chunked(theta_refs, RING), theta, sem)
    for c in loads:
        c.start()
    acc[...] = jnp.zeros_like(acc)
    for c in loads:
        c.wait()

    def step(n, _):
        at = at_block(n)
        th = block_column(theta, n)
        sg = block_column(sigma, n)
        lhs = jnp.concatenate([tok[:, at_block(rows[n, s])] for s in range(ks)], axis=1)
        mean = jnp.dot(lhs, th, preferred_element_type=f32)
        out[:, at] = (mean + rn[:, at]).astype(bf16)
        first = lax.dot_general(cot[:, at], th, NT, preferred_element_type=f32)
        second = lax.dot_general(gv[:, at], sg, NT, preferred_element_type=f32)
        for s in range(ks):
            pick = at_block(rows[n, s])
            p = slice(s * LANE, (s + 1) * LANE)
            acc[:, pick] += first[:, p] + 2.0 * tok[:, pick].astype(f32) * second[:, p]
        return 0

    lax.fori_loop(0, cot.shape[1] // LANE, step, 0)
    w = away.shape[2]
    core = place[PLACE["core"]]
    for k in range(RING):
        y = (place[PLACE["y"]] + k) & 3
        home[k] = acc[:, pl.ds(pl.multiple_of((y * 2 + core) * w, w), w)].astype(bf16)
        away[k] = acc[:, pl.ds(pl.multiple_of((y * 2 + 1 - core) * w, w), w)].astype(bf16)


def late(rows, place, tok, cot, gv, rn, sigma, theta, own):
    t, d = tok.shape
    ff = cot.shape[1]
    w = d // (2 * RING)
    refs = [r for group in sigma + theta for r in group]
    return pl.pallas_call(
        late_kernel,
        out_shape=[sds((t, ff), bf16), sds((RING, t, w), bf16), sds((RING, t, w), bf16)],
        in_specs=[SM, SM] + [VB] * 4 + [HB] * len(refs),
        out_specs=[VB] * 3,
        scratch_shapes=[
            pltpu.VMEM((RING, RING, own, ff), bf16),
            pltpu.VMEM((RING, RING, own, ff), bf16),
            pltpu.VMEM((t, d), f32),
            pltpu.SemaphoreType.DMA(()),
        ],
        compiler_params=PARAMS,
        name="late",
    )(rows, place, tok, cot, gv, rn, *refs)


def pair_kernel(home, came, *outs):
    for k in range(RING):
        outs[k][...] = (home[k].astype(f32) + came[k].astype(f32)).astype(bf16)


def step(tokens, theta, log_sigma2, block_rows, noise, cotangent):
    place = jnp.stack([lax.axis_index(a) for a in ROW + COL]).astype(jnp.int32)
    own = theta.shape[1]
    sg, th = prep(log_sigma2, theta)
    sigma_in = gather(sg, GATHER_SIGMA)
    theta_in = gather(th, GATHER_THETA)
    parts_theta, sq, sqt = early(block_rows, place, tokens, cotangent, own)
    parts_var, gv, rn = middle(block_rows, place, sq, sqt, noise, cotangent, sigma_in, own)
    output, away, home = late(block_rows, place, tokens, cotangent, gv, rn, sigma_in, theta_in, own)
    tokens_all = tokens.shape[0] * lax.axis_size(ROW)
    width = block_rows.shape[1] * LANE
    inv_root = 1.0 / math.sqrt(tokens_all)
    got_theta = scatter(parts_theta, SCATTER_THETA, place)
    grad_theta = final(got_theta, SCATTER_THETA, theta.shape, inv_root, None)
    got_var = scatter(parts_var, SCATTER_VAR, place)
    grad_logvar = final(got_var, SCATTER_VAR, theta.shape, width * inv_root, log_sigma2)
    came = sent(away, "core", 1)
    t, w = home.shape[1:]
    pairs = pl.pallas_call(pair_kernel, out_shape=[sds((t, w), bf16)] * RING, compiler_params=PARAMS, name="pair")(
        home, came
    )
    arrived = steps_sent(pairs, "y")
    grad_tokens = arrived[0].astype(f32)
    for a in arrived[1:]:
        grad_tokens = grad_tokens + a.astype(f32)
    return (output, grad_tokens, grad_theta, grad_logvar)


def solution(mesh):
    finer = Mesh(mesh.devices.reshape(4, 4, 4, 2), ROW + COL)
    in_specs = (P(ROW, None), P(COL, ROW, None), P(COL, ROW, None), P(COL, None), P(ROW, COL), P(ROW, COL))
    out_specs = (P(ROW, COL), P(ROW, COL), P(COL, ROW, None), P(COL, ROW, None))
    return jax.shard_map(step, mesh=finer, in_specs=in_specs, out_specs=out_specs, check_vma=False)
```

profile of v0, /device:TPU:1, one launch (start us, length us, event | category | flops | bytes accessed | tf_op | source)
XLA Modules:
  0.0 222.1 jit_solution(17797154522962457600)
XLA Ops:
  0.6 1.9 prep.1
  2.5 2.0 collective-permute-start
  4.5 2.5 %collective-permute-start.1 = (bf16[64,1536]{1,0:T(8,128)(2,1)}, bf16[64,1536]{1,0:T(8,128)(2,1)S(1)}, u32[]{:S(2)}, u32[]{:S(2)}) collective-permute-start(bf16[64,1536]{1,0:T(8,128)(2,1)} %get-tuple-element.35), channel_id=1, source_target_pairs={{0,16},{8,24},{16,0},{24,8},{1,17},{9,25},{17,1},{25,9},{2,18},{10... | collective-permute-start | bytes 589832 | tf_op jit(solution)/shard_map/ppermute | solution.py:41
  7.0 1.2 collective-permute-start.2
  8.1 2.1 collective-permute-done
  10.2 5.5 %collective-permute-done.1 = bf16[64,1536]{1,0:T(8,128)(2,1)S(1)} collective-permute-done((bf16[64,1536]{1,0:T(8,128)(2,1)}, bf16[64,1536]{1,0:T(8,128)(2,1)S(1)}, u32[]{:S(2)}, u32[]{:S(2)}) %collective-permute-start.1) | collective-permute-done | bytes 196640 | tf_op jit(solution)/shard_map/ppermute | solution.py:41
  15.7 1.0 pad_maximum_fusion.refs_0_
  16.8 1.7 collective-permute-start.3
  18.5 3.3 %collective-permute-start.7 = (bf16[64,1536]{1,0:T(8,128)(2,1)}, bf16[64,1536]{1,0:T(8,128)(2,1)S(1)}, u32[]{:S(2)}, u32[]{:S(2)}) collective-permute-start(bf16[64,1536]{1,0:T(8,128)(2,1)} %get-tuple-element.38), channel_id=1, source_target_pairs={{0,64},{32,96},{64,0},{96,32},{1,65},{33,97},{65,1},{97,33},{2,66}... | collective-permute-start | bytes 589832 | tf_op jit(solution)/shard_map/ppermute | solution.py:41
  21.8 0.7 collective-permute-start.8
  22.5 0.7 collective-permute-start.6
  23.7 18.4 %collective-permute-done.7 = bf16[64,1536]{1,0:T(8,128)(2,1)S(1)} collective-permute-done((bf16[64,1536]{1,0:T(8,128)(2,1)}, bf16[64,1536]{1,0:T(8,128)(2,1)S(1)}, u32[]{:S(2)}, u32[]{:S(2)}) %collective-permute-start.7) | collective-permute-done | bytes 196640 | tf_op jit(solution)/shard_map/ppermute | solution.py:41
  42.1 2.6 %collective-permute-done.6 = bf16[64,1536]{1,0:T(8,128)(2,1)S(1)} collective-permute-done((bf16[64,1536]{1,0:T(8,128)(2,1)}, bf16[64,1536]{1,0:T(8,128)(2,1)S(1)}, u32[]{:S(2)}, u32[]{:S(2)}) %collective-permute-start.6) | collective-permute-done | bytes 196640 | tf_op jit(solution)/shard_map/ppermute | solution.py:41
  44.7 1.0 pad_maximum_fusion.1.refs_4_
  45.8 1.5 collective-permute-start.10
  47.3 3.4 %collective-permute-start.11 = (bf16[4,64,1536]{2,1,0:T(8,128)(2,1)S(1)}, bf16[4,64,1536]{2,1,0:T(8,128)(2,1)}, u32[]{:S(2)}, u32[]{:S(2)}) collective-permute-start(bf16[4,64,1536]{2,1,0:T(8,128)(2,1)S(1)} %pad_maximum_fusion.1.refs_4_), channel_id=1, source_target_pairs={{0,24},{8,0},{16,8},{24,16},{1,25},{9,1},{17,9},{25,17},{2,26},{10... | collective-permute-start | bytes 2359304 | tf_op jit(solution)/shard_map/ppermute | solution.py:41
  50.7 0.8 copy.12.rows
  52.1 12.8 %early.1 = (bf16[4,64,1536]{2,1,0:T(8,128)(2,1)}, bf16[4,64,1536]{2,1,0:T(8,128)(2,1)}, bf16[4,64,1536]{2,1,0:T(8,128)(2,1)}, bf16[4,64,1536]{2,1,0:T(8,128)(2,1...) custom-call(s32[12,8]{1,0:T(8,128)} %copy.12.rows, s32[4]{0:T(128)} %pad_add_fusion.place, ...), custom_call_target="tpu_custom_call" | custom-call | tf_op jit(solution)/shard_map/early/pallas_call | solution.py:199
  65.0 0.9 copy-done.3
  65.9 25.8 %middle.1 = (bf16[4,64,1536]{2,1,0:T(8,128)(2,1)}, bf16[4,64,1536]{2,1,0:T(8,128)(2,1)}, bf16[4,64,1536]{2,1,0:T(8,128)(2,1)}, bf16[4,64,1536]{2,1,0:T(8,128)(2,...) custom-call(s32[12,8]{1,0:T(8,128)} %copy.12.rows, s32[4]{0:T(128)} %pad_add_fusion.place, ...), custom_call_target="tpu_custom_call" | custom-call | tf_op jit(solution)/shard_map/middle/pallas_call | solution.py:265
  91.7 29.0 %late.1 = (bf16[512,1536]{1,0:T(8,128)(2,1)}, bf16[4,512,512]{2,1,0:T(8,128)(2,1)}, bf16[4,512,512]{2,1,0:T(8,128)(2,1)}) custom-call(s32[12,8]{1,0:T(8,128)} %copy.12.rows, s32[4]{0:T(128)} %pad_add_fusion.place, bf16[512,4096]{1,0:T(8,128)(2,1)} %tok.3, bf16[512,1536]{1,0:T(8,128)(2,1)} %cot.5, bf16[512,1536]{1,0:T(8,128)(2,1)} %get-tuple-element.36.gv, ...), custom_call_target="tpu_custom_call" | custom-call | tf_op jit(solution)/shard_map/late/pallas_call | solution.py:327
  120.8 3.4 %collective-permute-start.12 = (bf16[4,512,512]{2,1,0:T(8,128)(2,1)}, bf16[4,512,512]{2,1,0:T(8,128)(2,1)S(1)}, u32[]{:S(2)}, u32[]{:S(2)}) collective-permute-start(bf16[4,512,512]{2,1,0:T(8,128)(2,1)} %get-tuple-element.41), channel_id=1, source_target_pairs={{0,1},{1,0},{2,3},{3,2},{4,5},{5,4},{6,7},{7,6},{8,9},{9,8},{10,11... | collective-permute-start | bytes 6291464 | tf_op jit(solution)/shard_map/ppermute | solution.py:41
  124.3 3.3 %collective-permute-start.17 = (bf16[4,64,1536]{2,1,0:T(8,128)(2,1)}, bf16[4,64,1536]{2,1,0:T(8,128)(2,1)}, u32[]{:S(2)}, u32[]{:S(2)}) collective-permute-start(bf16[4,64,1536]{2,1,0:T(8,128)(2,1)} %get-tuple-element.48), channel_id=1, source_target_pairs={{0,16},{8,24},{16,0},{24,8},{1,17},{9,25},{17,1},{25,9},{2,18},{10... | collective-permute-start | bytes 2359304 | tf_op jit(solution)/shard_map/ppermute | solution.py:41
  127.5 15.4 %collective-permute-start.22 = (bf16[4,64,1536]{2,1,0:T(8,128)(2,1)}, bf16[4,64,1536]{2,1,0:T(8,128)(2,1)S(1)}, u32[]{:S(2)}, u32[]{:S(2)}) collective-permute-start(bf16[4,64,1536]{2,1,0:T(8,128)(2,1)} %get-tuple-element.55), channel_id=1, source_target_pairs={{0,32},{32,64},{64,96},{96,0},{1,33},{33,65},{65,97},{97,1},{2,34}... | collective-permute-start | bytes 2359304 | tf_op jit(solution)/shard_map/ppermute | solution.py:41
  142.9 1.4 collective-permute-done.16.refs_1_
  144.4 0.9 copy-done.7
  145.3 17.4 %collective-permute-start.23 = (bf16[4,64,1536]{2,1,0:T(8,128)(2,1)}, bf16[4,64,1536]{2,1,0:T(8,128)(2,1)S(1)}, u32[]{:S(2)}, u32[]{:S(2)}) collective-permute-start(bf16[4,64,1536]{2,1,0:T(8,128)(2,1)} %get-tuple-element.56), channel_id=1, source_target_pairs={{0,64},{32,96},{64,0},{96,32},{1,65},{33,97},{65,1},{97,33},{2,66}... | collective-permute-start | bytes 2359304 | tf_op jit(solution)/shard_map/ppermute | solution.py:41
  162.6 2.1 collective-permute-start.24
  164.7 3.1 %shard_map.93 = (bf16[64,1536]{1,0:T(8,128)(2,1)}, bf16[64,1536]{1,0:T(8,128)(2,1)}, bf16[64,1536]{1,0:T(8,128)(2,1)}, bf16[64,1536]{1,0:T(8,128)(2,1)}) custom-call(s32[4]{0:T(128)} %pad_add_fusion.place, bf16[4,64,1536]{2,1,0:T(8,128)(2,1)} %get-tuple-element.46.refs_0_, bf16[4,64,1536]{2,1,0:T(8,128)(2,1)} %copy-done.7, ...), custom_call_target="tpu_custom_call" | custom-call | tf_op jit(solution)/shard_map/pallas_call | solution.py:132
  167.8 12.7 %collective-permute-start.19 = (bf16[64,1536]{1,0:T(8,128)(2,1)}, bf16[64,1536]{1,0:T(8,128)(2,1)S(1)}, u32[]{:S(2)}, u32[]{:S(2)}) collective-permute-start(bf16[64,1536]{1,0:T(8,128)(2,1)} %get-tuple-element.51), channel_id=1, source_target_pairs={{0,32},{32,64},{64,96},{96,0},{1,33},{33,65},{65,97},{97,1},{2,34}... | collective-permute-start | bytes 589832 | tf_op jit(solution)/shard_map/ppermute | solution.py:41
  180.5 3.8 %collective-permute-start.20 = (bf16[64,1536]{1,0:T(8,128)(2,1)}, bf16[64,1536]{1,0:T(8,128)(2,1)S(1)}, u32[]{:S(2)}, u32[]{:S(2)}) collective-permute-start(bf16[64,1536]{1,0:T(8,128)(2,1)} %get-tuple-element.52), channel_id=1, source_target_pairs={{0,64},{32,96},{64,0},{96,32},{1,65},{33,97},{65,1},{97,33},{2,66}... | collective-permute-start | bytes 589832 | tf_op jit(solution)/shard_map/ppermute | solution.py:41
  184.3 3.7 %pair.1 = (bf16[512,512]{1,0:T(8,128)(2,1)}, bf16[512,512]{1,0:T(8,128)(2,1)}, bf16[512,512]{1,0:T(8,128)(2,1)}, bf16[512,512]{1,0:T(8,128)(2,1)}) custom-call(bf16[4,512,512]{2,1,0:T(8,128)(2,1)} %get-tuple-element.40.home, bf16[4,512,512]{2,1,0:T(8,128)(2,1)} %copy-done.4), custom_call_target="tpu_custom_call" | custom-call | tf_op jit(solution)/shard_map/pair/pallas_call | solution.py:366
  188.0 1.3 collective-permute-start.13
  189.3 2.6 %collective-permute-start.14 = (bf16[512,512]{1,0:T(8,128)(2,1)}, bf16[512,512]{1,0:T(8,128)(2,1)S(1)}, u32[]{:S(2)}, u32[]{:S(2)}) collective-permute-start(bf16[512,512]{1,0:T(8,128)(2,1)} %get-tuple-element.44), channel_id=1, source_target_pairs={{0,4},{2,6},{4,0},{6,2},{1,5},{3,7},{5,1},{7,3},{8,12},{10,14},{12... | collective-permute-start | bytes 1572872 | tf_op jit(solution)/shard_map/ppermute | solution.py:41
  191.9 2.9 %collective-permute-done.24.refs_3_ = bf16[4,64,1536]{2,1,0:T(8,128)(2,1)} collective-permute-done((bf16[4,64,1536]{2,1,0:T(8,128)(2,1)}, bf16[4,64,1536]{2,1,0:T(8,128)(2,1)}, u32[]{:S(2)}, u32[]{:S(2)}) %collective-permute-start.24) | collective-permute-done | bytes 786464 | tf_op jit(solution)/shard_map/ppermute | solution.py:41
  194.8 2.5 %collective-permute-start.15 = (bf16[512,512]{1,0:T(8,128)(2,1)}, bf16[512,512]{1,0:T(8,128)(2,1)S(1)}, u32[]{:S(2)}, u32[]{:S(2)}) collective-permute-start(bf16[512,512]{1,0:T(8,128)(2,1)} %get-tuple-element.45), channel_id=1, source_target_pairs={{0,6},{2,0},{4,2},{6,4},{1,7},{3,1},{5,3},{7,5},{8,14},{10,8},{12,... | collective-permute-start | bytes 1572872 | tf_op jit(solution)/shard_map/ppermute | solution.py:41
  197.4 3.1 %shard_map.95 = (bf16[64,1536]{1,0:T(8,128)(2,1)}, bf16[64,1536]{1,0:T(8,128)(2,1)}, bf16[64,1536]{1,0:T(8,128)(2,1)}, bf16[64,1536]{1,0:T(8,128)(2,1)}) custom-call(s32[4]{0:T(128)} %pad_add_fusion.place, bf16[4,64,1536]{2,1,0:T(8,128)(2,1)} %get-tuple-element.54.refs_0_, bf16[4,64,1536]{2,1,0:T(8,128)(2,1)} %copy-done.5, bf16[4,64,1536]{2,1,0:T(8,128)(2,1)} %copy-done.6, ...), custom_call_target="tpu_custom_call" | custom-call | tf_op jit(solution)/shard_map/pallas_call | solution.py:132
  200.5 3.8 %collective-permute-start.21 = (bf16[64,1536]{1,0:T(8,128)(2,1)}, bf16[64,1536]{1,0:T(8,128)(2,1)S(1)}, u32[]{:S(2)}, u32[]{:S(2)}) collective-permute-start(bf16[64,1536]{1,0:T(8,128)(2,1)} %get-tuple-element.53), channel_id=1, source_target_pairs={{0,96},{32,0},{64,32},{96,64},{1,97},{33,1},{65,33},{97,65},{2,98}... | collective-permute-start | bytes 589832 | tf_op jit(solution)/shard_map/ppermute | solution.py:41
  204.9 2.7 %collective-permute-done.21.refs_3_ = bf16[64,1536]{1,0:T(8,128)(2,1)S(1)} collective-permute-done((bf16[64,1536]{1,0:T(8,128)(2,1)}, bf16[64,1536]{1,0:T(8,128)(2,1)S(1)}, u32[]{:S(2)}, u32[]{:S(2)}) %collective-permute-start.21) | collective-permute-done | bytes 196640 | tf_op jit(solution)/shard_map/ppermute | solution.py:41
  207.6 1.9 collective-permute-start.26
  209.5 1.0 collective-permute-done.25.refs_2_
  210.5 1.5 collective-permute-start.27
  212.1 2.1 shard_map.94
  214.2 2.0 collective-permute-done.26.refs_3_
  216.2 1.8 collective-permute-done.27.refs_4_
  218.0 0.7 copy-done.14
  218.7 2.2 shard_map.96
  220.9 1.2 convert_add_fusion
  (56 shorter events, 1.8 us)
Async XLA Ops:
  0.6 50.1 %copy-start.15 = (s32[12,8]{0,1:T(8,128)S(1)}, s32[12,8]{0,1:T(8,128)}, u32[]{:S(2)}) copy-start(s32[12,8]{0,1:T(8,128)} %param.9) | copy-start | bytes 1156
  2.5 7.7 %collective-permute-start = (bf16[64,1536]{1,0:T(8,128)(2,1)}, bf16[64,1536]{1,0:T(8,128)(2,1)S(1)}, u32[]{:S(2)}, u32[]{:S(2)}) collective-permute-start(bf16[64,1536]{1,0:T(8,128)(2,1)} %get-tuple-element.35), channel_id=1, source_target_pairs={{0,8},{8,16},{16,24},{24,0},{1,9},{9,17},{17,25},{25,1},{2,10},{10... | collective-permute-start | bytes 589832 | tf_op jit(solution)/shard_map/ppermute | solution.py:41
  4.5 11.2 %collective-permute-start.1 = (bf16[64,1536]{1,0:T(8,128)(2,1)}, bf16[64,1536]{1,0:T(8,128)(2,1)S(1)}, u32[]{:S(2)}, u32[]{:S(2)}) collective-permute-start(bf16[64,1536]{1,0:T(8,128)(2,1)} %get-tuple-element.35), channel_id=1, source_target_pairs={{0,16},{8,24},{16,0},{24,8},{1,17},{9,25},{17,1},{25,9},{2,18},{10... | collective-permute-start | bytes 589832 | tf_op jit(solution)/shard_map/ppermute | solution.py:41
  7.0 8.7 %collective-permute-start.2 = (bf16[64,1536]{1,0:T(8,128)(2,1)}, bf16[64,1536]{1,0:T(8,128)(2,1)S(1)}, u32[]{:S(2)}, u32[]{:S(2)}) collective-permute-start(bf16[64,1536]{1,0:T(8,128)(2,1)} %get-tuple-element.35), channel_id=1, source_target_pairs={{0,24},{8,0},{16,8},{24,16},{1,25},{9,1},{17,9},{25,17},{2,26},{10... | collective-permute-start | bytes 589832 | tf_op jit(solution)/shard_map/ppermute | solution.py:41
  16.8 48.1 %copy-start = (bf16[4,64,1536]{2,1,0:T(8,128)(2,1)}, bf16[4,64,1536]{2,1,0:T(8,128)(2,1)S(1)}, u32[]{:S(2)}) copy-start(bf16[4,64,1536]{2,1,0:T(8,128)(2,1)S(1)} %pad_maximum_fusion.refs_0_) | copy-start | bytes 2359300
  16.8 33.9 %collective-permute-start.3 = (bf16[4,64,1536]{2,1,0:T(8,128)(2,1)S(1)}, bf16[4,64,1536]{2,1,0:T(8,128)(2,1)S(1)}, u32[]{:S(2)}, u32[]{:S(2)}) collective-permute-start(bf16[4,64,1536]{2,1,0:T(8,128)(2,1)S(1)} %pad_maximum_fusion.refs_0_), channel_id=1, source_target_pairs={{0,32},{32,64},{64,96},{96,0},{1,33},{33,65},{65,97},{97,1},{2,34}... | collective-permute-start | bytes 2359304 | tf_op jit(solution)/shard_map/ppermute | solution.py:41
  18.5 23.6 %collective-permute-start.7 = (bf16[64,1536]{1,0:T(8,128)(2,1)}, bf16[64,1536]{1,0:T(8,128)(2,1)S(1)}, u32[]{:S(2)}, u32[]{:S(2)}) collective-permute-start(bf16[64,1536]{1,0:T(8,128)(2,1)} %get-tuple-element.38), channel_id=1, source_target_pairs={{0,64},{32,96},{64,0},{96,32},{1,65},{33,97},{65,1},{97,33},{2,66}... | collective-permute-start | bytes 589832 | tf_op jit(solution)/shard_map/ppermute | solution.py:41
  21.8 20.3 %collective-permute-start.8 = (bf16[64,1536]{1,0:T(8,128)(2,1)}, bf16[64,1536]{1,0:T(8,128)(2,1)S(1)}, u32[]{:S(2)}, u32[]{:S(2)}) collective-permute-start(bf16[64,1536]{1,0:T(8,128)(2,1)} %get-tuple-element.38), channel_id=1, source_target_pairs={{0,96},{32,0},{64,32},{96,64},{1,97},{33,1},{65,33},{97,65},{2,98}... | collective-permute-start | bytes 589832 | tf_op jit(solution)/shard_map/ppermute | solution.py:41
  22.5 22.2 %collective-permute-start.6 = (bf16[64,1536]{1,0:T(8,128)(2,1)}, bf16[64,1536]{1,0:T(8,128)(2,1)S(1)}, u32[]{:S(2)}, u32[]{:S(2)}) collective-permute-start(bf16[64,1536]{1,0:T(8,128)(2,1)} %get-tuple-element.38), channel_id=1, source_target_pairs={{0,32},{32,64},{64,96},{96,0},{1,33},{33,65},{65,97},{97,1},{2,34}... | collective-permute-start | bytes 589832 | tf_op jit(solution)/shard_map/ppermute | solution.py:41
  23.2 41.7 %collective-permute-start.4 = (bf16[4,64,1536]{2,1,0:T(8,128)(2,1)S(1)}, bf16[4,64,1536]{2,1,0:T(8,128)(2,1)S(1)}, u32[]{:S(2)}, u32[]{:S(2)}) collective-permute-start(bf16[4,64,1536]{2,1,0:T(8,128)(2,1)S(1)} %pad_maximum_fusion.refs_0_), channel_id=1, source_target_pairs={{0,64},{32,96},{64,0},{96,32},{1,65},{33,97},{65,1},{97,33},{2,66}... | collective-permute-start | bytes 2359304 | tf_op jit(solution)/shard_map/ppermute | solution.py:41
  42.1 22.9 %collective-permute-start.5 = (bf16[4,64,1536]{2,1,0:T(8,128)(2,1)S(1)}, bf16[4,64,1536]{2,1,0:T(8,128)(2,1)}, u32[]{:S(2)}, u32[]{:S(2)}) collective-permute-start(bf16[4,64,1536]{2,1,0:T(8,128)(2,1)S(1)} %pad_maximum_fusion.refs_0_), channel_id=1, source_target_pairs={{0,96},{32,0},{64,32},{96,64},{1,97},{33,1},{65,33},{97,65},{2,98}... | collective-permute-start | bytes 2359304 | tf_op jit(solution)/shard_map/ppermute | solution.py:41
  45.8 19.1 %copy-start.1 = (bf16[4,64,1536]{2,1,0:T(8,128)(2,1)}, bf16[4,64,1536]{2,1,0:T(8,128)(2,1)S(1)}, u32[]{:S(2)}) copy-start(bf16[4,64,1536]{2,1,0:T(8,128)(2,1)S(1)} %pad_maximum_fusion.1.refs_4_) | copy-start | bytes 2359300
  45.8 45.9 %collective-permute-start.10 = (bf16[4,64,1536]{2,1,0:T(8,128)(2,1)S(1)}, bf16[4,64,1536]{2,1,0:T(8,128)(2,1)}, u32[]{:S(2)}, u32[]{:S(2)}) collective-permute-start(bf16[4,64,1536]{2,1,0:T(8,128)(2,1)S(1)} %pad_maximum_fusion.1.refs_4_), channel_id=1, source_target_pairs={{0,16},{8,24},{16,0},{24,8},{1,17},{9,25},{17,1},{25,9},{2,18},{10... | collective-permute-start | bytes 2359304 | tf_op jit(solution)/shard_map/ppermute | solution.py:41
  47.3 44.4 %collective-permute-start.11 = (bf16[4,64,1536]{2,1,0:T(8,128)(2,1)S(1)}, bf16[4,64,1536]{2,1,0:T(8,128)(2,1)}, u32[]{:S(2)}, u32[]{:S(2)}) collective-permute-start(bf16[4,64,1536]{2,1,0:T(8,128)(2,1)S(1)} %pad_maximum_fusion.1.refs_4_), channel_id=1, source_target_pairs={{0,24},{8,0},{16,8},{24,16},{1,25},{9,1},{17,9},{25,17},{2,26},{10... | collective-permute-start | bytes 2359304 | tf_op jit(solution)/shard_map/ppermute | solution.py:41
  50.7 14.2 %copy-start.2 = (bf16[4,64,1536]{2,1,0:T(8,128)(2,1)}, bf16[4,64,1536]{2,1,0:T(8,128)(2,1)S(1)}, u32[]{:S(2)}) copy-start(bf16[4,64,1536]{2,1,0:T(8,128)(2,1)S(1)} %collective-permute-done.3.refs_1_) | copy-start | bytes 2359300
  50.7 41.0 %collective-permute-start.9 = (bf16[4,64,1536]{2,1,0:T(8,128)(2,1)S(1)}, bf16[4,64,1536]{2,1,0:T(8,128)(2,1)}, u32[]{:S(2)}, u32[]{:S(2)}) collective-permute-start(bf16[4,64,1536]{2,1,0:T(8,128)(2,1)S(1)} %pad_maximum_fusion.1.refs_4_), channel_id=1, source_target_pairs={{0,8},{8,16},{16,24},{24,0},{1,9},{9,17},{17,25},{25,1},{2,10},{10... | collective-permute-start | bytes 2359304 | tf_op jit(solution)/shard_map/ppermute | solution.py:41
  64.9 0.9 copy-start.3
  91.7 32.4 %copy-start.16 = (bf16[4,64,1536]{2,1,0:T(8,128)(2,1)S(1)}, bf16[4,64,1536]{2,1,0:T(8,128)(2,1)}, u32[]{:S(2)}) copy-start(bf16[4,64,1536]{2,1,0:T(8,128)(2,1)} %get-tuple-element.47) | copy-start | bytes 2359300
  120.8 59.7 %collective-permute-start.12 = (bf16[4,512,512]{2,1,0:T(8,128)(2,1)}, bf16[4,512,512]{2,1,0:T(8,128)(2,1)S(1)}, u32[]{:S(2)}, u32[]{:S(2)}) collective-permute-start(bf16[4,512,512]{2,1,0:T(8,128)(2,1)} %get-tuple-element.41), channel_id=1, source_target_pairs={{0,1},{1,0},{2,3},{3,2},{4,5},{5,4},{6,7},{7,6},{8,9},{9,8},{10,11... | collective-permute-start | bytes 6291464 | tf_op jit(solution)/shard_map/ppermute | solution.py:41
  124.1 20.2 %collective-permute-start.16 = (bf16[4,64,1536]{2,1,0:T(8,128)(2,1)S(1)}, bf16[4,64,1536]{2,1,0:T(8,128)(2,1)S(1)}, u32[]{:S(2)}, u32[]{:S(2)}) collective-permute-start(bf16[4,64,1536]{2,1,0:T(8,128)(2,1)S(1)} %copy-done.16), channel_id=1, source_target_pairs={{0,8},{8,16},{16,24},{24,0},{1,9},{9,17},{17,25},{25,1},{2,10},{10... | collective-permute-start | bytes 2359304 | tf_op jit(solution)/shard_map/ppermute | solution.py:41
  124.3 38.4 %collective-permute-start.17 = (bf16[4,64,1536]{2,1,0:T(8,128)(2,1)}, bf16[4,64,1536]{2,1,0:T(8,128)(2,1)}, u32[]{:S(2)}, u32[]{:S(2)}) collective-permute-start(bf16[4,64,1536]{2,1,0:T(8,128)(2,1)} %get-tuple-element.48), channel_id=1, source_target_pairs={{0,16},{8,24},{16,0},{24,8},{1,17},{9,25},{17,1},{25,9},{2,18},{10... | collective-permute-start | bytes 2359304 | tf_op jit(solution)/shard_map/ppermute | solution.py:41
  127.5 37.2 %collective-permute-start.18 = (bf16[4,64,1536]{2,1,0:T(8,128)(2,1)}, bf16[4,64,1536]{2,1,0:T(8,128)(2,1)}, u32[]{:S(2)}, u32[]{:S(2)}) collective-permute-start(bf16[4,64,1536]{2,1,0:T(8,128)(2,1)} %get-tuple-element.49), channel_id=1, source_target_pairs={{0,24},{8,0},{16,8},{24,16},{1,25},{9,1},{17,9},{25,17},{2,26},{10... | collective-permute-start | bytes 2359304 | tf_op jit(solution)/shard_map/ppermute | solution.py:41
  127.5 60.4 %collective-permute-start.22 = (bf16[4,64,1536]{2,1,0:T(8,128)(2,1)}, bf16[4,64,1536]{2,1,0:T(8,128)(2,1)S(1)}, u32[]{:S(2)}, u32[]{:S(2)}) collective-permute-start(bf16[4,64,1536]{2,1,0:T(8,128)(2,1)} %get-tuple-element.55), channel_id=1, source_target_pairs={{0,32},{32,64},{64,96},{96,0},{1,33},{33,65},{65,97},{97,1},{2,34}... | collective-permute-start | bytes 2359304 | tf_op jit(solution)/shard_map/ppermute | solution.py:41
  144.4 0.9 copy-start.7
  145.3 44.0 %collective-permute-start.23 = (bf16[4,64,1536]{2,1,0:T(8,128)(2,1)}, bf16[4,64,1536]{2,1,0:T(8,128)(2,1)S(1)}, u32[]{:S(2)}, u32[]{:S(2)}) collective-permute-start(bf16[4,64,1536]{2,1,0:T(8,128)(2,1)} %get-tuple-element.56), channel_id=1, source_target_pairs={{0,64},{32,96},{64,0},{96,32},{1,65},{33,97},{65,1},{97,33},{2,66}... | collective-permute-start | bytes 2359304 | tf_op jit(solution)/shard_map/ppermute | solution.py:41
  162.6 32.2 %collective-permute-start.24 = (bf16[4,64,1536]{2,1,0:T(8,128)(2,1)}, bf16[4,64,1536]{2,1,0:T(8,128)(2,1)}, u32[]{:S(2)}, u32[]{:S(2)}) collective-permute-start(bf16[4,64,1536]{2,1,0:T(8,128)(2,1)} %get-tuple-element.57), channel_id=1, source_target_pairs={{0,96},{32,0},{64,32},{96,64},{1,97},{33,1},{65,33},{97,65},{2,98}... | collective-permute-start | bytes 2359304 | tf_op jit(solution)/shard_map/ppermute | solution.py:41
  167.8 32.7 %collective-permute-start.19 = (bf16[64,1536]{1,0:T(8,128)(2,1)}, bf16[64,1536]{1,0:T(8,128)(2,1)S(1)}, u32[]{:S(2)}, u32[]{:S(2)}) collective-permute-start(bf16[64,1536]{1,0:T(8,128)(2,1)} %get-tuple-element.51), channel_id=1, source_target_pairs={{0,32},{32,64},{64,96},{96,0},{1,33},{33,65},{65,97},{97,1},{2,34}... | collective-permute-start | bytes 589832 | tf_op jit(solution)/shard_map/ppermute | solution.py:41
  180.5 3.8 %copy-start.4 = (bf16[4,512,512]{2,1,0:T(8,128)(2,1)}, bf16[4,512,512]{2,1,0:T(8,128)(2,1)S(1)}, u32[]{:S(2)}) copy-start(bf16[4,512,512]{2,1,0:T(8,128)(2,1)S(1)} %collective-permute-done.12.came) | copy-start | bytes 6291460
  180.5 23.8 %collective-permute-start.20 = (bf16[64,1536]{1,0:T(8,128)(2,1)}, bf16[64,1536]{1,0:T(8,128)(2,1)S(1)}, u32[]{:S(2)}, u32[]{:S(2)}) collective-permute-start(bf16[64,1536]{1,0:T(8,128)(2,1)} %get-tuple-element.52), channel_id=1, source_target_pairs={{0,64},{32,96},{64,0},{96,32},{1,65},{33,97},{65,1},{97,33},{2,66}... | collective-permute-start | bytes 589832 | tf_op jit(solution)/shard_map/ppermute | solution.py:41
  187.9 9.4 %copy-start.5 = (bf16[4,64,1536]{2,1,0:T(8,128)(2,1)}, bf16[4,64,1536]{2,1,0:T(8,128)(2,1)S(1)}, u32[]{:S(2)}) copy-start(bf16[4,64,1536]{2,1,0:T(8,128)(2,1)S(1)} %collective-permute-done.22.refs_1_) | copy-start | bytes 2359300
  188.0 32.9 %collective-permute-start.13 = (bf16[512,512]{1,0:T(8,128)(2,1)}, bf16[512,512]{1,0:T(8,128)(2,1)S(1)}, u32[]{:S(2)}, u32[]{:S(2)}) collective-permute-start(bf16[512,512]{1,0:T(8,128)(2,1)} %get-tuple-element.43), channel_id=1, source_target_pairs={{0,2},{2,4},{4,6},{6,0},{1,3},{3,5},{5,7},{7,1},{8,10},{10,12},{12... | collective-permute-start | bytes 1572872 | tf_op jit(solution)/shard_map/ppermute | solution.py:41
  189.3 8.1 %copy-start.6 = (bf16[4,64,1536]{2,1,0:T(8,128)(2,1)}, bf16[4,64,1536]{2,1,0:T(8,128)(2,1)S(1)}, u32[]{:S(2)}) copy-start(bf16[4,64,1536]{2,1,0:T(8,128)(2,1)S(1)} %collective-permute-done.23.refs_2_) | copy-start | bytes 2359300
  189.3 31.6 %collective-permute-start.14 = (bf16[512,512]{1,0:T(8,128)(2,1)}, bf16[512,512]{1,0:T(8,128)(2,1)S(1)}, u32[]{:S(2)}, u32[]{:S(2)}) collective-permute-start(bf16[512,512]{1,0:T(8,128)(2,1)} %get-tuple-element.44), channel_id=1, source_target_pairs={{0,4},{2,6},{4,0},{6,2},{1,5},{3,7},{5,1},{7,3},{8,12},{10,14},{12... | collective-permute-start | bytes 1572872 | tf_op jit(solution)/shard_map/ppermute | solution.py:41
  194.8 26.1 %collective-permute-start.15 = (bf16[512,512]{1,0:T(8,128)(2,1)}, bf16[512,512]{1,0:T(8,128)(2,1)S(1)}, u32[]{:S(2)}, u32[]{:S(2)}) collective-permute-start(bf16[512,512]{1,0:T(8,128)(2,1)} %get-tuple-element.45), channel_id=1, source_target_pairs={{0,6},{2,0},{4,2},{6,4},{1,7},{3,1},{5,3},{7,5},{8,14},{10,8},{12,... | collective-permute-start | bytes 1572872 | tf_op jit(solution)/shard_map/ppermute | solution.py:41
  200.4 20.4 %copy-start.8 = (bf16[512,512]{1,0:T(8,128)(2,1)S(1)}, bf16[512,512]{1,0:T(8,128)(2,1)}, u32[]{:S(2)}) copy-start(bf16[512,512]{1,0:T(8,128)(2,1)} %get-tuple-element.42) | copy-start | bytes 1572868
  200.5 11.6 %copy-start.9 = (bf16[64,1536]{1,0:T(8,128)(2,1)}, bf16[64,1536]{1,0:T(8,128)(2,1)S(1)}, u32[]{:S(2)}) copy-start(bf16[64,1536]{1,0:T(8,128)(2,1)S(1)} %collective-permute-done.19.refs_1_) | copy-start | bytes 589828
  200.5 7.1 %collective-permute-start.21 = (bf16[64,1536]{1,0:T(8,128)(2,1)}, bf16[64,1536]{1,0:T(8,128)(2,1)S(1)}, u32[]{:S(2)}, u32[]{:S(2)}) collective-permute-start(bf16[64,1536]{1,0:T(8,128)(2,1)} %get-tuple-element.53), channel_id=1, source_target_pairs={{0,96},{32,0},{64,32},{96,64},{1,97},{33,1},{65,33},{97,65},{2,98}... | collective-permute-start | bytes 589832 | tf_op jit(solution)/shard_map/ppermute | solution.py:41
  204.3 7.8 %copy-start.10 = (bf16[64,1536]{1,0:T(8,128)(2,1)}, bf16[64,1536]{1,0:T(8,128)(2,1)S(1)}, u32[]{:S(2)}) copy-start(bf16[64,1536]{1,0:T(8,128)(2,1)S(1)} %collective-permute-done.20.refs_2_) | copy-start | bytes 589828
  204.3 6.2 %collective-permute-start.25 = (bf16[64,1536]{1,0:T(8,128)(2,1)}, bf16[64,1536]{1,0:T(8,128)(2,1)S(1)}, u32[]{:S(2)}, u32[]{:S(2)}) collective-permute-start(bf16[64,1536]{1,0:T(8,128)(2,1)} %get-tuple-element.59), channel_id=1, source_target_pairs={{0,8},{8,16},{16,24},{24,0},{1,9},{9,17},{17,25},{25,1},{2,10},{10... | collective-permute-start | bytes 589832 | tf_op jit(solution)/shard_map/ppermute | solution.py:41
  207.6 4.5 %copy-start.12 = (bf16[64,1536]{1,0:T(8,128)(2,1)}, bf16[64,1536]{1,0:T(8,128)(2,1)S(1)}, u32[]{:S(2)}) copy-start(bf16[64,1536]{1,0:T(8,128)(2,1)S(1)} %collective-permute-done.21.refs_3_) | copy-start | bytes 589828
  207.6 8.6 %collective-permute-start.26 = (bf16[64,1536]{1,0:T(8,128)(2,1)}, bf16[64,1536]{1,0:T(8,128)(2,1)S(1)}, u32[]{:S(2)}, u32[]{:S(2)}) collective-permute-start(bf16[64,1536]{1,0:T(8,128)(2,1)} %get-tuple-element.60), channel_id=1, source_target_pairs={{0,16},{8,24},{16,0},{24,8},{1,17},{9,25},{17,1},{25,9},{2,18},{10... | collective-permute-start | bytes 589832 | tf_op jit(solution)/shard_map/ppermute | solution.py:41
  210.5 7.5 %copy-start.11 = (bf16[64,1536]{1,0:T(8,128)(2,1)}, bf16[64,1536]{1,0:T(8,128)(2,1)S(1)}, u32[]{:S(2)}) copy-start(bf16[64,1536]{1,0:T(8,128)(2,1)S(1)} %collective-permute-done.25.refs_2_) | copy-start | bytes 589828
  210.5 7.4 %collective-permute-start.27 = (bf16[64,1536]{1,0:T(8,128)(2,1)}, bf16[64,1536]{1,0:T(8,128)(2,1)S(1)}, u32[]{:S(2)}, u32[]{:S(2)}) collective-permute-start(bf16[64,1536]{1,0:T(8,128)(2,1)} %get-tuple-element.61), channel_id=1, source_target_pairs={{0,24},{8,0},{16,8},{24,16},{1,25},{9,1},{17,9},{25,17},{2,26},{10... | collective-permute-start | bytes 589832 | tf_op jit(solution)/shard_map/ppermute | solution.py:41
  216.2 1.8 copy-start.13
  218.0 0.7 copy-start.14
where the time goes:
time: 224 us; the launch traced here: 222 us
  starting transfers between devices  89.9 us (40%)
  Pallas kernels  83.5 us (37%)
  waiting for transfers between devices  40.6 us (18%)
  other arithmetic  3.85 us (2%)
  local copies, waits for them, and re-layouts  3.37 us (2%)
    ppermute x28, starting transfers between devices, sent(): return lax.ppermute(value, axis, [(i, (i + step) % n) for i in range(n)])  89.9 us
    ppermute x28, waiting for transfers between devices, sent(): return lax.ppermute(value, axis, [(i, (i + step) % n) for i in range(n)])  40.6 us
    pallas_call x1, Pallas kernels, late(): pl.pallas_call(late_kernel, out_shape=[sds((t, ff), bf16), sds((RING, t,...  29 us
    pallas_call x1, Pallas kernels, middle(): pl.pallas_call(middle_kernel, out_shape=shapes, in_specs=[SM, SM, HB, HB,...  25.8 us
    pallas_call x1, Pallas kernels, early(): pl.pallas_call(early_kernel, out_shape=shapes, in_specs=[SM, SM, VB, VB],...  12.8 us
    pallas_call x2, Pallas kernels, scatter(): pl.pallas_call(sum_kernel(paths), out_shape=shapes, in_specs=[SM] + [VB]...  6.14 us
  transfers between devices with their start and end apart: 28, of which 10 were waited for; matrix products, arithmetic and copies ran while one was open for 1% of the time, Pallas kernels for 24%

commit v1 on v0

v1 whole, which is shorter than its diff:
```python
import math

import jax
import jax.numpy as jnp
from jax import lax
from jax.experimental import pallas as pl
from jax.experimental.pallas import tpu as pltpu
from jax.sharding import Mesh
from jax.sharding import PartitionSpec as P


ROW = ("z", "x")
COL = ("y", "core")
RING = 4
EPS = 1e-06
LANE = 128
f32, bf16 = jnp.float32, jnp.bfloat16
PARAMS = pltpu.CompilerParams(vmem_limit_bytes=60 * 1024 * 1024)
SM = pl.BlockSpec(memory_space=pltpu.SMEM)
VB = pl.BlockSpec(memory_space=pltpu.VMEM)
HB = pl.BlockSpec(memory_space=pl.ANY)
NT = (((1,), (1,)), ((), ()))

GATHER_SIGMA = (("x", "z", 0, 64),)
GATHER_THETA = (("z", "x", 0, 64),)
SCATTER_THETA = (("x", "z", 0, 64),)
SCATTER_VAR = (("z", "x", 0, 64),)
PLACE = {"z": 0, "x": 1, "y": 2, "core": 3}


def sds(shape, dtype):
    return jax.ShapeDtypeStruct(shape, dtype)


def at_block(index):
    return pl.ds(pl.multiple_of(index * LANE, LANE), LANE)


def sent(value, axis, step):
    n = lax.axis_size(axis)
    return lax.ppermute(value, axis, [(i, (i + step) % n) for i in range(n)])


def steps_of(value, axis):
    return [sent(value, axis, k) for k in range(1, RING)]


def steps_sent(values, axis):
    return [values[0]] + [sent(values[k], axis, k) for k in range(1, RING)]


def prep_kernel(paths_s, paths_t):
    def kernel(ls_ref, theta_ref, *outs):
        for n in range(theta_ref.shape[0]):
            at = slice(n * LANE, (n + 1) * LANE)
            for (_, _, lo, hi), o in zip(paths_s, outs):
                o[:, at] = jnp.exp(ls_ref[n, lo:hi]).astype(bf16)
            for (_, _, lo, hi), o in zip(paths_t, outs[len(paths_s) :]):
                o[:, at] = theta_ref[n, lo:hi]

    return kernel


def prep(ls, theta):
    c, _, b = theta.shape
    shapes = [sds((hi - lo, c * b), bf16) for _, _, lo, hi in GATHER_SIGMA + GATHER_THETA]
    outs = pl.pallas_call(
        prep_kernel(GATHER_SIGMA, GATHER_THETA), out_shape=shapes, compiler_params=PARAMS, name="prep"
    )(ls, theta)
    return outs[: len(GATHER_SIGMA)], outs[len(GATHER_SIGMA) :]


def gather(pieces, paths):
    blocks = [jnp.stack([p] + steps_of(p, path[0])) for p, path in zip(pieces, paths)]
    return [[b] + steps_of(b, path[1]) for b, path in zip(blocks, paths)]


def chunked(refs, size):
    return [refs[i : i + size] for i in range(0, len(refs), size)]


def block_column(whole, n):
    blk = whole[:, :, :, at_block(n)]
    return blk.reshape(-1, LANE)


def scatter_shapes(paths, ff):
    return [sds((RING, hi - lo, ff), bf16) for _, _, lo, hi in paths for _ in range(RING)]


def summed(arrived, spot):
    total = arrived[0][spot].astype(f32)
    for r in arrived[1:]:
        total = total + r[spot].astype(f32)
    return total.astype(bf16)


def scatter(parts, paths):
    ins = []
    for path, group in zip(paths, chunked(parts, RING)):
        ins += [group[0]] + [sent(group[k], path[0], k) for k in range(1, RING)]
    mid = [summed(group, k) for group in chunked(ins, RING) for k in range(RING)]
    arrived = []
    for path, group in zip(paths, chunked(mid, RING)):
        arrived += [group[0]] + [sent(group[k], path[1], k) for k in range(1, RING)]
    return arrived


def final_kernel(paths, scale, with_sigma):
    def kernel(*refs):
        ls = refs[0] if with_sigma else None
        ins, out = refs[int(with_sigma) : -1], refs[-1]
        for n in range(out.shape[0]):
            at = slice(n * LANE, (n + 1) * LANE)
            for (_, _, lo, hi), group in zip(paths, chunked(ins, RING)):
                total = group[0][:, at].astype(f32)
                for r in group[1:]:
                    total = total + r[:, at].astype(f32)
                if with_sigma:
                    total = total * jnp.exp(ls[n, lo:hi])
                out[n, lo:hi] = total * scale

    return kernel


def final(arrived, paths, shape, scale, ls):
    args = ([] if ls is None else [ls]) + list(arrived)
    return pl.pallas_call(
        final_kernel(paths, scale, ls is not None), out_shape=sds(shape, f32), compiler_params=PARAMS
    )(*args)


GROUPS = 2


def issue(copies):
    for c in copies:
        c.start()


def column_span(group, per):
    w = per * LANE
    return pl.ds(pl.multiple_of(group * w, w), w)


def gather_starts(place, paths, groups, whole, sems, per):
    for g in range(GROUPS):
        cols = slice(g * per * LANE, (g + 1) * per * LANE)
        for (one, two, lo, hi), refs in zip(paths, groups):
            for k in range(RING):
                for j in range(RING):
                    spot = {one: (place[PLACE[one]] - j) & 3, two: (place[PLACE[two]] - k) & 3}
                    pltpu.make_async_copy(
                        refs[k].at[j, :, cols], whole.at[spot["z"], spot["x"], lo:hi, cols], sems.at[g]
                    ).start()


def gather_wait(whole, sems, g, per):
    cols = column_span(g, per)
    part = whole.at[:, :, :, cols]
    pltpu.make_async_copy(part, part, sems.at[g]).wait()


def scatter_start(place, paths, held, groups, sem, cols):
    for (one, two, lo, hi), refs in zip(paths, groups):
        for k in range(RING):
            for j in range(RING):
                spot = {one: (place[PLACE[one]] + k) & 3, two: (place[PLACE[two]] + j) & 3}
                pltpu.make_async_copy(
                    held.at[spot["z"], spot["x"], lo:hi, cols], refs[k].at[j, :, cols], sem
                ).start()


def early_kernel(rows, tok, cot, *refs):
    outs, (sq_out, sqt_out, tokt, held, sq, sqt, sems) = refs[:-7], refs[-7:]
    place = [lax.axis_index(a) for a in ROW + COL]
    blocks = tok.shape[1] // LANE
    ks = rows.shape[1]
    per = cot.shape[1] // LANE // GROUPS
    for k in range(blocks):
        at = slice(k * LANE, (k + 1) * LANE)
        wide = tok[:, at].astype(f32)
        sq[:, at] = (wide * wide).astype(bf16)
        turned = tok[:, at].T
        tokt[k] = turned
        wide = turned.astype(f32)
        sqt[k] = (wide * wide).astype(bf16)
    saves = [pltpu.make_async_copy(sq, sq_out, sems.at[0]), pltpu.make_async_copy(sqt, sqt_out, sems.at[1])]
    issue(saves)

    def group(g, _):
        for u in range(per):
            n = g * per + u
            lhs = jnp.concatenate([tokt[rows[n, s]] for s in range(ks)], axis=0)
            part = jnp.dot(lhs, cot[:, at_block(n)], preferred_element_type=f32)
            held[:, :, :, at_block(n)] = part.astype(bf16).reshape(RING, RING, -1, LANE)
        scatter_start(place, SCATTER_THETA, held, chunked(outs, RING), sems.at[2], column_span(g, per))
        return 0

    lax.fori_loop(0, GROUPS, group, 0)
    for c in saves:
        c.wait()
    pltpu.make_async_copy(held, held, sems.at[2]).wait()


def early(rows, tok, cot, own):
    t, d = tok.shape
    ff = cot.shape[1]
    shapes = scatter_shapes(SCATTER_THETA, ff) + [sds((t, d), bf16), sds((d // LANE, LANE, t), bf16)]
    outs = pl.pallas_call(
        early_kernel,
        out_shape=shapes,
        in_specs=[SM, VB, VB],
        out_specs=[HB] * len(shapes),
        scratch_shapes=[
            pltpu.VMEM((d // LANE, LANE, t), bf16),
            pltpu.VMEM((RING, RING, own, ff), bf16),
            pltpu.VMEM((t, d), bf16),
            pltpu.VMEM((d // LANE, LANE, t), bf16),
            pltpu.SemaphoreType.DMA((3,)),
        ],
        compiler_params=PARAMS,
        name="early",
    )(rows, tok, cot)
    return outs[:-2], outs[-2], outs[-1]


def middle_kernel(rows, sq_in, sqt_in, noise_in, cot_in, *refs):
    n_in = RING * len(GATHER_SIGMA)
    sigma_refs, outs = refs[:n_in], refs[n_in:-14]
    gv_out, rn_out, sq, sqt, noise, cot, whole, held, gv, rn, s_sig, s_in, s_one, s_out = refs[-14:]
    place = [lax.axis_index(a) for a in ROW + COL]
    ks = rows.shape[1]
    per = noise.shape[1] // LANE // GROUPS
    first = pltpu.make_async_copy(sq_in, sq, s_one.at[0])
    second = pltpu.make_async_copy(sqt_in, sqt, s_one.at[1])
    first.start()
    gather_starts(place, GATHER_SIGMA, chunked(sigma_refs, RING), whole, s_sig, per)

    def loads(g):
        at = column_span(g, per)
        return [
            pltpu.make_async_copy(noise_in.at[:, at], noise.at[:, at], s_in.at[0, g]),
            pltpu.make_async_copy(cot_in.at[:, at], cot.at[:, at], s_in.at[1, g]),
        ]

    def saves(g):
        at = column_span(g, per)
        return [
            pltpu.make_async_copy(gv.at[:, at], gv_out.at[:, at], s_out.at[0, g]),
            pltpu.make_async_copy(rn.at[:, at], rn_out.at[:, at], s_out.at[1, g]),
        ]

    issue(loads(0))
    second.start()
    for g in range(1, GROUPS):
        issue(loads(g))
    first.wait()

    def group(g, _):
        gather_wait(whole, s_sig, g, per)
        for c in loads(g):
            c.wait()
        for u in range(per):
            n = g * per + u
            at = at_block(n)
            lhs = jnp.concatenate([sq[:, at_block(rows[n, s])] for s in range(ks)], axis=1)
            var = jnp.dot(lhs, block_column(whole, n), preferred_element_type=f32) + EPS
            inv = lax.rsqrt(var)
            draw = noise[:, at].astype(f32)
            rn[:, at] = var * inv * draw
            gv[:, at] = (cot[:, at].astype(f32) * draw * (0.5 * inv)).astype(bf16)

        @pl.when(g == 0)
        def _():
            second.wait()

        for u in range(per):
            n = g * per + u
            at = at_block(n)
            lhs = jnp.concatenate([sqt[rows[n, s]] for s in range(ks)], axis=0)
            part = jnp.dot(lhs, gv[:, at], preferred_element_type=f32)
            held[:, :, :, at] = part.astype(bf16).reshape(RING, RING, -1, LANE)
        issue(saves(g))
        scatter_start(place, SCATTER_VAR, held, chunked(outs, RING), s_one.at[2], column_span(g, per))
        return 0

    lax.fori_loop(0, GROUPS, group, 0)
    for g in range(GROUPS):
        for c in saves(g):
            c.wait()
    pltpu.make_async_copy(held, held, s_one.at[2]).wait()


def middle(rows, sq, sqt, noise, cot, sigma, own):
    t, d = sq.shape
    ff = cot.shape[1]
    shapes = scatter_shapes(SCATTER_VAR, ff) + [sds((t, ff), bf16), sds((t, ff), f32)]
    refs = [r for group in sigma for r in group]
    outs = pl.pallas_call(
        middle_kernel,
        out_shape=shapes,
        in_specs=[SM, HB, HB, HB, HB] + [HB] * len(refs),
        out_specs=[HB] * len(shapes),
        scratch_shapes=[
            pltpu.VMEM((t, d), bf16),
            pltpu.VMEM((d // LANE, LANE, t), bf16),
            pltpu.VMEM((t, ff), bf16),
            pltpu.VMEM((t, ff), bf16),
            pltpu.VMEM((RING, RING, own, ff), bf16),
            pltpu.VMEM((RING, RING, own, ff), bf16),
            pltpu.VMEM((t, ff), bf16),
            pltpu.VMEM((t, ff), f32),
            pltpu.SemaphoreType.DMA((GROUPS,)),
            pltpu.SemaphoreType.DMA((2, GROUPS)),
            pltpu.SemaphoreType.DMA((3,)),
            pltpu.SemaphoreType.DMA((2, GROUPS)),
        ],
        compiler_params=PARAMS,
        name="middle",
    )(rows, sq, sqt, noise, cot, *refs)
    return outs[:-2], outs[-2], outs[-1]


def late_kernel(rows, tok_in, cot_in, gv_in, rn_in, *refs):
    n_s, n_t = RING * len(GATHER_SIGMA), RING * len(GATHER_THETA)
    sigma_refs, theta_refs = refs[:n_s], refs[n_s : n_s + n_t]
    (out_out, away_out, home_out, tok, cot, gv, rn, out, both, sigma, theta, acc, s_w, s_in, s_one, s_out) = refs[n_s + n_t :]
    place = [lax.axis_index(a) for a in ROW + COL]
    ks = rows.shape[1]
    per = cot.shape[1] // LANE // GROUPS
    first = pltpu.make_async_copy(tok_in, tok, s_one.at[0])
    first.start()

    def loads(g):
        at = column_span(g, per)
        pairs = ((cot_in, cot), (gv_in, gv), (rn_in, rn))
        return [pltpu.make_async_copy(a.at[:, at], b.at[:, at], s_in.at[i, g]) for i, (a, b) in enumerate(pairs)]

    def save(g):
        at = column_span(g, per)
        return pltpu.make_async_copy(out.at[:, at], out_out.at[:, at], s_out.at[g])

    issue(loads(0))
    gather_starts(place, GATHER_THETA, chunked(theta_refs, RING), theta, s_w.at[0], per)
    gather_starts(place, GATHER_SIGMA, chunked(sigma_refs, RING), sigma, s_w.at[1], per)
    for g in range(1, GROUPS):
        issue(loads(g))
    acc[...] = jnp.zeros_like(acc)
    first.wait()

    def group(g, _):
        gather_wait(theta, s_w.at[0], g, per)
        gather_wait(sigma, s_w.at[1], g, per)
        for c in loads(g):
            c.wait()
        for u in range(per):
            n = g * per + u
            at = at_block(n)
            th = block_column(theta, n)
            sg = block_column(sigma, n)
            lhs = jnp.concatenate([tok[:, at_block(rows[n, s])] for s in range(ks)], axis=1)
            mean = jnp.dot(lhs, th, preferred_element_type=f32)
            out[:, at] = (mean + rn[:, at]).astype(bf16)
            for q in range(ks // 2):
                span = slice(q * 2 * LANE, (q + 1) * 2 * LANE)
                one = lax.dot_general(cot[:, at], th[span], NT, preferred_element_type=f32)
                two = lax.dot_general(gv[:, at], sg[span], NT, preferred_element_type=f32)
                for h in range(2):
                    pick = at_block(rows[n, 2 * q + h])
                    p = slice(h * LANE, (h + 1) * LANE)
                    acc[:, pick] += one[:, p] + 2.0 * tok[:, pick].astype(f32) * two[:, p]
        save(g).start()
        return 0

    lax.fori_loop(0, GROUPS, group, 0)
    w = away_out.shape[2]
    core = place[PLACE["core"]]
    ends = []
    for side, (ref, half) in enumerate(((away_out, 1 - core), (home_out, core))):
        for k in range(RING):
            y = (place[PLACE["y"]] + k) & 3
            both[side, k] = acc[:, pl.ds(pl.multiple_of((y * 2 + half) * w, w), w)].astype(bf16)
            ends.append(pltpu.make_async_copy(both.at[side, k], ref.at[k], s_one.at[1 + side * RING + k]))
            ends[-1].start()
    for c in [save(g) for g in range(GROUPS)] + ends:
        c.wait()


def late(rows, tok, cot, gv, rn, sigma, theta, own):
    t, d = tok.shape
    ff = cot.shape[1]
    w = d // (2 * RING)
    refs = [r for group in sigma + theta for r in group]
    shapes = [sds((t, ff), bf16), sds((RING, t, w), bf16), sds((RING, t, w), bf16)]
    return pl.pallas_call(
        late_kernel,
        out_shape=shapes,
        in_specs=[SM] + [HB] * (4 + len(refs)),
        out_specs=[HB] * 3,
        scratch_shapes=[
            pltpu.VMEM((t, d), bf16),
            pltpu.VMEM((t, ff), bf16),
            pltpu.VMEM((t, ff), bf16),
            pltpu.VMEM((t, ff), f32),
            pltpu.VMEM((t, ff), bf16),
            pltpu.VMEM((2, RING, t, w), bf16),
            pltpu.VMEM((RING, RING, own, ff), bf16),
            pltpu.VMEM((RING, RING, own, ff), bf16),
            pltpu.VMEM((t, d), f32),
            pltpu.SemaphoreType.DMA((2, GROUPS)),
            pltpu.SemaphoreType.DMA((3, GROUPS)),
            pltpu.SemaphoreType.DMA((1 + 2 * RING,)),
            pltpu.SemaphoreType.DMA((GROUPS,)),
        ],
        compiler_params=PARAMS,
        name="late",
    )(rows, tok, cot, gv, rn, *refs)


def step(tokens, theta, log_sigma2, block_rows, noise, cotangent):
    own = theta.shape[1]
    sg, th = prep(log_sigma2, theta)
    sigma_in = gather(sg, GATHER_SIGMA)
    theta_in = gather(th, GATHER_THETA)
    parts_theta, sq, sqt = early(block_rows, tokens, cotangent, own)
    parts_var, gv, rn = middle(block_rows, sq, sqt, noise, cotangent, sigma_in, own)
    output, away, home = late(block_rows, tokens, cotangent, gv, rn, sigma_in, theta_in, own)
    tokens_all = tokens.shape[0] * lax.axis_size(ROW)
    width = block_rows.shape[1] * LANE
    inv_root = 1.0 / math.sqrt(tokens_all)
    got_theta = scatter(parts_theta, SCATTER_THETA)
    grad_theta = final(got_theta, SCATTER_THETA, theta.shape, inv_root, None)
    got_var = scatter(parts_var, SCATTER_VAR)
    grad_logvar = final(got_var, SCATTER_VAR, theta.shape, width * inv_root, log_sigma2)
    came = sent(away, "core", 1)
    pairs = [(home[k].astype(f32) + came[k].astype(f32)).astype(bf16) for k in range(RING)]
    arrived = steps_sent(pairs, "y")
    grad_tokens = arrived[0].astype(f32)
    for a in arrived[1:]:
        grad_tokens = grad_tokens + a.astype(f32)
    return (output, grad_tokens, grad_theta, grad_logvar)


def solution(mesh):
    finer = Mesh(mesh.devices.reshape(4, 4, 4, 2), ROW + COL)
    in_specs = (P(ROW, None), P(COL, ROW, None), P(COL, ROW, None), P(COL, None), P(ROW, COL), P(ROW, COL))
    out_specs = (P(ROW, COL), P(ROW, COL), P(COL, ROW, None), P(COL, ROW, None))
    return jax.shard_map(step, mesh=finer, in_specs=in_specs, out_specs=out_specs, check_vma=False)
```

time: 224 us -> 213 us (0.951)
  the two profiles are of different devices: /device:TPU:1 before, /device:TPU:0 now
where the time goes in v1:
time: 213 us
  waiting for transfers between devices  73.6 us (35%)
  starting transfers between devices  70.4 us (33%)
  Pallas kernels  57.1 us (27%)
  other arithmetic  9.04 us (4%)
    ppermute x28, waiting for transfers between devices, sent(): return lax.ppermute(value, axis, [(i, (i + step) % n) for i in range(n)])  73.6 us
    ppermute x28, starting transfers between devices, sent(): return lax.ppermute(value, axis, [(i, (i + step) % n) for i in range(n)])  70.4 us
    pallas_call x1, Pallas kernels, late(): pl.pallas_call(late_kernel, out_shape=shapes, in_specs=[SM] + [HB] * (4 +...  24.8 us
    pallas_call x1, Pallas kernels, middle(): pl.pallas_call(middle_kernel, out_shape=shapes, in_specs=[SM, HB, HB, HB,...  15.3 us
    pallas_call x1, Pallas kernels, early(): pl.pallas_call(early_kernel, out_shape=shapes, in_specs=[SM, VB, VB], out...  10.9 us
    pallas_call x2, Pallas kernels, final(): pl.pallas_call(final_kernel(paths, scale, ls is not None), out_shape=sds(...  4.27 us
  transfers between devices with their start and end apart: 28, of which 12 were waited for; matrix products, arithmetic and copies ran while one was open for 3% of the time, Pallas kernels for 14%

profile of v1, /device:TPU:0, one launch (start us, length us, event | category | flops | bytes accessed | tf_op | source)
XLA Modules:
  0.0 212.7 jit_solution(4594306671648897012)
XLA Ops:
  0.6 1.9 prep.1
  2.5 1.6 collective-permute-start
  4.1 2.7 %collective-permute-start.1 = (bf16[64,1536]{1,0:T(8,128)(2,1)}, bf16[64,1536]{1,0:T(8,128)(2,1)S(1)}, u32[]{:S(2)}, u32[]{:S(2)}) collective-permute-start(bf16[64,1536]{1,0:T(8,128)(2,1)} %get-tuple-element.23), channel_id=1, source_target_pairs={{0,16},{8,24},{16,0},{24,8},{1,17},{9,25},{17,1},{25,9},{2,18},{10... | collective-permute-start | bytes 589832 | tf_op jit(solution)/shard_map/ppermute | solution.py:41
  6.8 1.4 collective-permute-start.2
  8.3 2.2 %collective-permute-done = bf16[64,1536]{1,0:T(8,128)(2,1)S(1)} collective-permute-done((bf16[64,1536]{1,0:T(8,128)(2,1)}, bf16[64,1536]{1,0:T(8,128)(2,1)S(1)}, u32[]{:S(2)}, u32[]{:S(2)}) %collective-permute-start) | collective-permute-done | bytes 196640 | tf_op jit(solution)/shard_map/ppermute | solution.py:41
  10.5 5.4 %collective-permute-done.1 = bf16[64,1536]{1,0:T(8,128)(2,1)S(1)} collective-permute-done((bf16[64,1536]{1,0:T(8,128)(2,1)}, bf16[64,1536]{1,0:T(8,128)(2,1)S(1)}, u32[]{:S(2)}, u32[]{:S(2)}) %collective-permute-start.1) | collective-permute-done | bytes 196640 | tf_op jit(solution)/shard_map/ppermute | solution.py:41
  15.9 1.0 pad_maximum_fusion.refs_0_
  16.9 2.0 collective-permute-start.3
  18.9 1.9 collective-permute-start.6
  20.8 1.7 collective-permute-start.7
  22.6 2.5 %collective-permute-start.8 = (bf16[64,1536]{1,0:T(8,128)(2,1)}, bf16[64,1536]{1,0:T(8,128)(2,1)S(1)}, u32[]{:S(2)}, u32[]{:S(2)}) collective-permute-start(bf16[64,1536]{1,0:T(8,128)(2,1)} %get-tuple-element.26), channel_id=1, source_target_pairs={{0,96},{32,0},{64,32},{96,64},{1,97},{33,1},{65,33},{97,65},{2,98}... | collective-permute-start | bytes 589832 | tf_op jit(solution)/shard_map/ppermute | solution.py:41
  25.1 17.6 %collective-permute-done.6 = bf16[64,1536]{1,0:T(8,128)(2,1)S(1)} collective-permute-done((bf16[64,1536]{1,0:T(8,128)(2,1)}, bf16[64,1536]{1,0:T(8,128)(2,1)S(1)}, u32[]{:S(2)}, u32[]{:S(2)}) %collective-permute-start.6) | collective-permute-done | bytes 196640 | tf_op jit(solution)/shard_map/ppermute | solution.py:41
  42.7 2.9 %collective-permute-start.5 = (bf16[4,64,1536]{2,1,0:T(8,128)(2,1)S(1)}, bf16[4,64,1536]{2,1,0:T(8,128)(2,1)S(1)}, u32[]{:S(2)}, u32[]{:S(2)}) collective-permute-start(bf16[4,64,1536]{2,1,0:T(8,128)(2,1)S(1)} %pad_maximum_fusion.refs_0_), channel_id=1, source_target_pairs={{0,96},{32,0},{64,32},{96,64},{1,97},{33,1},{65,33},{97,65},{2,98}... | collective-permute-start | bytes 2359304 | tf_op jit(solution)/shard_map/ppermute | solution.py:41
  45.7 3.6 %collective-permute-done.7 = bf16[64,1536]{1,0:T(8,128)(2,1)S(1)} collective-permute-done((bf16[64,1536]{1,0:T(8,128)(2,1)}, bf16[64,1536]{1,0:T(8,128)(2,1)S(1)}, u32[]{:S(2)}, u32[]{:S(2)}) %collective-permute-start.7) | collective-permute-done | bytes 196640 | tf_op jit(solution)/shard_map/ppermute | solution.py:41
  49.3 1.9 pad_maximum_fusion.1.refs_4_
  51.2 2.7 %collective-permute-start.10 = (bf16[4,64,1536]{2,1,0:T(8,128)(2,1)}, bf16[4,64,1536]{2,1,0:T(8,128)(2,1)}, u32[]{:S(2)}, u32[]{:S(2)}) collective-permute-start(bf16[4,64,1536]{2,1,0:T(8,128)(2,1)} %pad_maximum_fusion.1.refs_4_), channel_id=1, source_target_pairs={{0,16},{8,24},{16,0},{24,8},{1,17},{9,25},{17,1},{25,9},{2,18},{10... | collective-permute-start | bytes 2359304 | tf_op jit(solution)/shard_map/ppermute | solution.py:41
  53.9 1.3 collective-permute-start.11
  55.2 0.7 collective-permute-start.9
  55.9 0.7 copy.12.rows
  56.6 10.9 %early.1 = (bf16[4,64,1536]{2,1,0:T(8,128)(2,1)}, bf16[4,64,1536]{2,1,0:T(8,128)(2,1)}, bf16[4,64,1536]{2,1,0:T(8,128)(2,1)}, bf16[4,64,1536]{2,1,0:T(8,128)(2,1...) custom-call(s32[12,8]{1,0:T(8,128)} %copy.12.rows, bf16[512,4096]{1,0:T(8,128)(2,1)} %tok_in.1, ...), custom_call_target="tpu_custom_call" | custom-call | tf_op jit(solution)/shard_map/early/pallas_call | solution.py:210
  67.5 4.6 %collective-permute-done.5.refs_3_ = bf16[4,64,1536]{2,1,0:T(8,128)(2,1)S(1)} collective-permute-done((bf16[4,64,1536]{2,1,0:T(8,128)(2,1)S(1)}, bf16[4,64,1536]{2,1,0:T(8,128)(2,1)S(1)}, u32[]{:S(2)}, u32[]{:S(2)}) %collective-permute-start.5) | collective-permute-done | bytes 786464 | tf_op jit(solution)/shard_map/ppermute | solution.py:41
  72.2 1.0 copy-done.3
  73.1 15.3 %middle.1 = (bf16[4,64,1536]{2,1,0:T(8,128)(2,1)}, bf16[4,64,1536]{2,1,0:T(8,128)(2,1)}, bf16[4,64,1536]{2,1,0:T(8,128)(2,1)}, bf16[4,64,1536]{2,1,0:T(8,128)(2,...) custom-call(s32[12,8]{1,0:T(8,128)} %copy.12.rows, bf16[512,4096]{1,0:T(8,128)(2,1)} %get-tuple-element.21.sq_in, ...), custom_call_target="tpu_custom_call" | custom-call | tf_op jit(solution)/shard_map/middle/pallas_call | solution.py:300
  88.5 24.8 %late.1 = (bf16[512,1536]{1,0:T(8,128)(2,1)}, bf16[4,512,512]{2,1,0:T(8,128)(2,1)}, bf16[4,512,512]{2,1,0:T(8,128)(2,1)}) custom-call(s32[12,8]{1,0:T(8,128)} %copy.12.rows, bf16[512,4096]{1,0:T(8,128)(2,1)} %tok_in.1, bf16[512,1536]{1,0:T(8,128)(2,1)} %cot_in.3, bf16[512,1536]{1,0:T(8,128)(2,1)} %get-tuple-element.24.gv_in, ...), custom_call_target="tpu_custom_call" | custom-call | tf_op jit(solution)/shard_map/late/pallas_call | solution.py:396
  113.4 1.8 collective-permute-start.16
  115.2 2.8 %collective-permute-start.17 = (bf16[4,64,1536]{2,1,0:T(8,128)(2,1)}, bf16[4,64,1536]{2,1,0:T(8,128)(2,1)S(1)}, u32[]{:S(2)}, u32[]{:S(2)}) collective-permute-start(bf16[4,64,1536]{2,1,0:T(8,128)(2,1)} %get-tuple-element.32), channel_id=1, source_target_pairs={{0,16},{8,24},{16,0},{24,8},{1,17},{9,25},{17,1},{25,9},{2,18},{10... | collective-permute-start | bytes 2359304 | tf_op jit(solution)/shard_map/ppermute | solution.py:41
  117.9 0.6 collective-permute-start.18
  118.5 7.8 %collective-permute-start.22 = (bf16[4,64,1536]{2,1,0:T(8,128)(2,1)}, bf16[4,64,1536]{2,1,0:T(8,128)(2,1)S(1)}, u32[]{:S(2)}, u32[]{:S(2)}) collective-permute-start(bf16[4,64,1536]{2,1,0:T(8,128)(2,1)} %get-tuple-element.35), channel_id=1, source_target_pairs={{0,32},{32,64},{64,96},{96,0},{1,33},{33,65},{65,97},{97,1},{2,34}... | collective-permute-start | bytes 2359304 | tf_op jit(solution)/shard_map/ppermute | solution.py:41
  126.4 8.5 %collective-permute-done.16 = bf16[4,64,1536]{2,1,0:T(8,128)(2,1)S(1)} collective-permute-done((bf16[4,64,1536]{2,1,0:T(8,128)(2,1)}, bf16[4,64,1536]{2,1,0:T(8,128)(2,1)S(1)}, u32[]{:S(2)}, u32[]{:S(2)}) %collective-permute-start.16) | collective-permute-done | bytes 786464 | tf_op jit(solution)/shard_map/ppermute | solution.py:41
  134.8 10.8 %collective-permute-start.23 = (bf16[4,64,1536]{2,1,0:T(8,128)(2,1)}, bf16[4,64,1536]{2,1,0:T(8,128)(2,1)S(1)}, u32[]{:S(2)}, u32[]{:S(2)}) collective-permute-start(bf16[4,64,1536]{2,1,0:T(8,128)(2,1)} %get-tuple-element.36), channel_id=1, source_target_pairs={{0,64},{32,96},{64,0},{96,32},{1,65},{33,97},{65,1},{97,33},{2,66}... | collective-permute-start | bytes 2359304 | tf_op jit(solution)/shard_map/ppermute | solution.py:41
  145.6 7.2 %collective-permute-done.17 = bf16[4,64,1536]{2,1,0:T(8,128)(2,1)S(1)} collective-permute-done((bf16[4,64,1536]{2,1,0:T(8,128)(2,1)}, bf16[4,64,1536]{2,1,0:T(8,128)(2,1)S(1)}, u32[]{:S(2)}, u32[]{:S(2)}) %collective-permute-start.17) | collective-permute-done | bytes 786464 | tf_op jit(solution)/shard_map/ppermute | solution.py:41
  152.9 11.4 %collective-permute-start.24 = (bf16[4,64,1536]{2,1,0:T(8,128)(2,1)}, bf16[4,64,1536]{2,1,0:T(8,128)(2,1)S(1)}, u32[]{:S(2)}, u32[]{:S(2)}) collective-permute-start(bf16[4,64,1536]{2,1,0:T(8,128)(2,1)} %get-tuple-element.37), channel_id=1, source_target_pairs={{0,96},{32,0},{64,32},{96,64},{1,97},{33,1},{65,33},{97,65},{2,98}... | collective-permute-start | bytes 2359304 | tf_op jit(solution)/shard_map/ppermute | solution.py:41
  164.2 1.1 fusion.9
  165.3 1.5 collective-permute-start.20
  166.8 1.2 fusion.3
  168.0 1.5 collective-permute-start.13
  169.6 2.9 %collective-permute-start.14 = (bf16[512,512]{1,0:T(8,128)(2,1)S(1)}, bf16[512,512]{1,0:T(8,128)(2,1)}, u32[]{:S(2)}, u32[]{:S(2)}) collective-permute-start(bf16[512,512]{1,0:T(8,128)(2,1)S(1)} %get-tuple-element.40), channel_id=1, source_target_pairs={{0,4},{2,6},{4,0},{6,2},{1,5},{3,7},{5,1},{7,3},{8,12},{10,14},{12... | collective-permute-start | bytes 1572872 | tf_op jit(solution)/shard_map/ppermute | solution.py:41
  172.5 13.1 %collective-permute-done.24 = bf16[4,64,1536]{2,1,0:T(8,128)(2,1)S(1)} collective-permute-done((bf16[4,64,1536]{2,1,0:T(8,128)(2,1)}, bf16[4,64,1536]{2,1,0:T(8,128)(2,1)S(1)}, u32[]{:S(2)}, u32[]{:S(2)}) %collective-permute-start.24) | collective-permute-done | bytes 786464 | tf_op jit(solution)/shard_map/ppermute | solution.py:41
  185.6 3.0 %collective-permute-start.15 = (bf16[512,512]{1,0:T(8,128)(2,1)S(1)}, bf16[512,512]{1,0:T(8,128)(2,1)}, u32[]{:S(2)}, u32[]{:S(2)}) collective-permute-start(bf16[512,512]{1,0:T(8,128)(2,1)S(1)} %get-tuple-element.39), channel_id=1, source_target_pairs={{0,6},{2,0},{4,2},{6,4},{1,7},{3,1},{5,3},{7,5},{8,14},{10,8},{12,... | collective-permute-start | bytes 1572872 | tf_op jit(solution)/shard_map/ppermute | solution.py:41
  188.6 1.1 fusion.13
  189.7 3.6 %collective-permute-start.21 = (bf16[64,1536]{1,0:T(8,128)(2,1)S(1)}, bf16[64,1536]{1,0:T(8,128)(2,1)}, u32[]{:S(2)}, u32[]{:S(2)}) collective-permute-start(bf16[64,1536]{1,0:T(8,128)(2,1)S(1)} %get-tuple-element.45), channel_id=1, source_target_pairs={{0,96},{32,0},{64,32},{96,64},{1,97},{33,1},{65,33},{97,65},{2,98}... | collective-permute-start | bytes 589832 | tf_op jit(solution)/shard_map/ppermute | solution.py:41
  193.3 3.2 %collective-permute-done.21.refs_3_ = bf16[64,1536]{1,0:T(8,128)(2,1)} collective-permute-done((bf16[64,1536]{1,0:T(8,128)(2,1)S(1)}, bf16[64,1536]{1,0:T(8,128)(2,1)}, u32[]{:S(2)}, u32[]{:S(2)}) %collective-permute-start.21) | collective-permute-done | bytes 196640 | tf_op jit(solution)/shard_map/ppermute | solution.py:41
  196.5 1.1 collective-permute-start.26
  197.6 4.2 %collective-permute-done.25.refs_2_ = bf16[64,1536]{1,0:T(8,128)(2,1)} collective-permute-done((bf16[64,1536]{1,0:T(8,128)(2,1)S(1)}, bf16[64,1536]{1,0:T(8,128)(2,1)}, u32[]{:S(2)}, u32[]{:S(2)}) %collective-permute-start.25) | collective-permute-done | bytes 196640 | tf_op jit(solution)/shard_map/ppermute | solution.py:41
  201.8 2.1 shard_map.93
  203.9 3.8 %collective-permute-done.27.refs_4_ = bf16[64,1536]{1,0:T(8,128)(2,1)} collective-permute-done((bf16[64,1536]{1,0:T(8,128)(2,1)}, bf16[64,1536]{1,0:T(8,128)(2,1)}, u32[]{:S(2)}, u32[]{:S(2)}) %collective-permute-start.27) | collective-permute-done | bytes 196640 | tf_op jit(solution)/shard_map/ppermute | solution.py:41
  207.8 2.2 %shard_map.94 = f32[12,64,128]{2,1,0:T(8,128)} custom-call(f32[12,64,128]{2,1,0:T(8,128)} %refs_0_.1, bf16[64,1536]{1,0:T(8,128)(2,1)} %get-tuple-element.44.refs_1_, bf16[64,1536]{1,0:T(8,128)(2,1)} %collective-permute-done.25.refs_2_, bf16[64,1536]{1,0:T(8,128)(2,1)} %collective-permute-done.26.refs_3_, bf16[64,1536]{1,0:T(8,128)(2,1)} %collective-permute-done.27.refs_4_), custom_call_target="tpu_custom_call" | custom-call | tf_op jit(solution)/shard_map/pallas_call | solution.py:128
  210.0 2.7 %fusion.1 = f32[512,512]{1,0:T(8,128)} fusion(bf16[512,512]{1,0:T(8,128)(2,1)} %collective-permute-done.15, bf16[512,512]{1,0:T(8,128)(2,1)} %collective-permute-done.14, bf16[512,512]{1,0:T(8,128)(2,1)S(1)} %collective-permute-done.13, bf16[4,512,512]{2,1,0:T(8,128)(2,1)} %copy-done.5, bf16[4,512,512]{2,1,0:T(8,128)(2,1)S(1)} %copy-done.4), kind=kLoop, calls=%fused_computation.2 | loop fusion | flops 2883584 | bytes 3670016 | tf_op jit(solution)/shard_map/add | solution.py:441
  (45 shorter events, 0.2 us)
Async XLA Ops:
  0.6 55.3 %copy-start.10 = (s32[12,8]{0,1:T(8,128)S(1)}, s32[12,8]{0,1:T(8,128)}, u32[]{:S(2)}) copy-start(s32[12,8]{0,1:T(8,128)} %param.9) | copy-start | bytes 1156
  2.5 8.0 %collective-permute-start = (bf16[64,1536]{1,0:T(8,128)(2,1)}, bf16[64,1536]{1,0:T(8,128)(2,1)S(1)}, u32[]{:S(2)}, u32[]{:S(2)}) collective-permute-start(bf16[64,1536]{1,0:T(8,128)(2,1)} %get-tuple-element.23), channel_id=1, source_target_pairs={{0,8},{8,16},{16,24},{24,0},{1,9},{9,17},{17,25},{25,1},{2,10},{10... | collective-permute-start | bytes 589832 | tf_op jit(solution)/shard_map/ppermute | solution.py:41
  4.1 11.8 %collective-permute-start.1 = (bf16[64,1536]{1,0:T(8,128)(2,1)}, bf16[64,1536]{1,0:T(8,128)(2,1)S(1)}, u32[]{:S(2)}, u32[]{:S(2)}) collective-permute-start(bf16[64,1536]{1,0:T(8,128)(2,1)} %get-tuple-element.23), channel_id=1, source_target_pairs={{0,16},{8,24},{16,0},{24,8},{1,17},{9,25},{17,1},{25,9},{2,18},{10... | collective-permute-start | bytes 589832 | tf_op jit(solution)/shard_map/ppermute | solution.py:41
  6.8 9.0 %collective-permute-start.2 = (bf16[64,1536]{1,0:T(8,128)(2,1)}, bf16[64,1536]{1,0:T(8,128)(2,1)S(1)}, u32[]{:S(2)}, u32[]{:S(2)}) collective-permute-start(bf16[64,1536]{1,0:T(8,128)(2,1)} %get-tuple-element.23), channel_id=1, source_target_pairs={{0,24},{8,0},{16,8},{24,16},{1,25},{9,1},{17,9},{25,17},{2,26},{10... | collective-permute-start | bytes 589832 | tf_op jit(solution)/shard_map/ppermute | solution.py:41
  16.9 50.6 %copy-start = (bf16[4,64,1536]{2,1,0:T(8,128)(2,1)}, bf16[4,64,1536]{2,1,0:T(8,128)(2,1)S(1)}, u32[]{:S(2)}) copy-start(bf16[4,64,1536]{2,1,0:T(8,128)(2,1)S(1)} %pad_maximum_fusion.refs_0_) | copy-start | bytes 2359300
  16.9 38.3 %collective-permute-start.3 = (bf16[4,64,1536]{2,1,0:T(8,128)(2,1)S(1)}, bf16[4,64,1536]{2,1,0:T(8,128)(2,1)S(1)}, u32[]{:S(2)}, u32[]{:S(2)}) collective-permute-start(bf16[4,64,1536]{2,1,0:T(8,128)(2,1)S(1)} %pad_maximum_fusion.refs_0_), channel_id=1, source_target_pairs={{0,32},{32,64},{64,96},{96,0},{1,33},{33,65},{65,97},{97,1},{2,34}... | collective-permute-start | bytes 2359304 | tf_op jit(solution)/shard_map/ppermute | solution.py:41
  18.9 23.8 %collective-permute-start.6 = (bf16[64,1536]{1,0:T(8,128)(2,1)}, bf16[64,1536]{1,0:T(8,128)(2,1)S(1)}, u32[]{:S(2)}, u32[]{:S(2)}) collective-permute-start(bf16[64,1536]{1,0:T(8,128)(2,1)} %get-tuple-element.26), channel_id=1, source_target_pairs={{0,32},{32,64},{64,96},{96,0},{1,33},{33,65},{65,97},{97,1},{2,34}... | collective-permute-start | bytes 589832 | tf_op jit(solution)/shard_map/ppermute | solution.py:41
  20.8 28.5 %collective-permute-start.7 = (bf16[64,1536]{1,0:T(8,128)(2,1)}, bf16[64,1536]{1,0:T(8,128)(2,1)S(1)}, u32[]{:S(2)}, u32[]{:S(2)}) collective-permute-start(bf16[64,1536]{1,0:T(8,128)(2,1)} %get-tuple-element.26), channel_id=1, source_target_pairs={{0,64},{32,96},{64,0},{96,32},{1,65},{33,97},{65,1},{97,33},{2,66}... | collective-permute-start | bytes 589832 | tf_op jit(solution)/shard_map/ppermute | solution.py:41
  22.6 26.7 %collective-permute-start.8 = (bf16[64,1536]{1,0:T(8,128)(2,1)}, bf16[64,1536]{1,0:T(8,128)(2,1)S(1)}, u32[]{:S(2)}, u32[]{:S(2)}) collective-permute-start(bf16[64,1536]{1,0:T(8,128)(2,1)} %get-tuple-element.26), channel_id=1, source_target_pairs={{0,96},{32,0},{64,32},{96,64},{1,97},{33,1},{65,33},{97,65},{2,98}... | collective-permute-start | bytes 589832 | tf_op jit(solution)/shard_map/ppermute | solution.py:41
  25.1 42.4 %collective-permute-start.4 = (bf16[4,64,1536]{2,1,0:T(8,128)(2,1)S(1)}, bf16[4,64,1536]{2,1,0:T(8,128)(2,1)S(1)}, u32[]{:S(2)}, u32[]{:S(2)}) collective-permute-start(bf16[4,64,1536]{2,1,0:T(8,128)(2,1)S(1)} %pad_maximum_fusion.refs_0_), channel_id=1, source_target_pairs={{0,64},{32,96},{64,0},{96,32},{1,65},{33,97},{65,1},{97,33},{2,66}... | collective-permute-start | bytes 2359304 | tf_op jit(solution)/shard_map/ppermute | solution.py:41
  42.7 29.4 %collective-permute-start.5 = (bf16[4,64,1536]{2,1,0:T(8,128)(2,1)S(1)}, bf16[4,64,1536]{2,1,0:T(8,128)(2,1)S(1)}, u32[]{:S(2)}, u32[]{:S(2)}) collective-permute-start(bf16[4,64,1536]{2,1,0:T(8,128)(2,1)S(1)} %pad_maximum_fusion.refs_0_), channel_id=1, source_target_pairs={{0,96},{32,0},{64,32},{96,64},{1,97},{33,1},{65,33},{97,65},{2,98}... | collective-permute-start | bytes 2359304 | tf_op jit(solution)/shard_map/ppermute | solution.py:41
  51.2 37.2 %collective-permute-start.10 = (bf16[4,64,1536]{2,1,0:T(8,128)(2,1)}, bf16[4,64,1536]{2,1,0:T(8,128)(2,1)}, u32[]{:S(2)}, u32[]{:S(2)}) collective-permute-start(bf16[4,64,1536]{2,1,0:T(8,128)(2,1)} %pad_maximum_fusion.1.refs_4_), channel_id=1, source_target_pairs={{0,16},{8,24},{16,0},{24,8},{1,17},{9,25},{17,1},{25,9},{2,18},{10... | collective-permute-start | bytes 2359304 | tf_op jit(solution)/shard_map/ppermute | solution.py:41
  53.9 34.6 %collective-permute-start.11 = (bf16[4,64,1536]{2,1,0:T(8,128)(2,1)}, bf16[4,64,1536]{2,1,0:T(8,128)(2,1)}, u32[]{:S(2)}, u32[]{:S(2)}) collective-permute-start(bf16[4,64,1536]{2,1,0:T(8,128)(2,1)} %pad_maximum_fusion.1.refs_4_), channel_id=1, source_target_pairs={{0,24},{8,0},{16,8},{24,16},{1,25},{9,1},{17,9},{25,17},{2,26},{10... | collective-permute-start | bytes 2359304 | tf_op jit(solution)/shard_map/ppermute | solution.py:41
  55.2 12.2 %copy-start.1 = (bf16[4,64,1536]{2,1,0:T(8,128)(2,1)}, bf16[4,64,1536]{2,1,0:T(8,128)(2,1)S(1)}, u32[]{:S(2)}) copy-start(bf16[4,64,1536]{2,1,0:T(8,128)(2,1)S(1)} %collective-permute-done.3.refs_1_) | copy-start | bytes 2359300
  55.2 33.2 %collective-permute-start.9 = (bf16[4,64,1536]{2,1,0:T(8,128)(2,1)}, bf16[4,64,1536]{2,1,0:T(8,128)(2,1)}, u32[]{:S(2)}, u32[]{:S(2)}) collective-permute-start(bf16[4,64,1536]{2,1,0:T(8,128)(2,1)} %pad_maximum_fusion.1.refs_4_), channel_id=1, source_target_pairs={{0,8},{8,16},{16,24},{24,0},{1,9},{9,17},{17,25},{25,1},{2,10},{10... | collective-permute-start | bytes 2359304 | tf_op jit(solution)/shard_map/ppermute | solution.py:41
  67.5 4.7 %copy-start.2 = (bf16[4,64,1536]{2,1,0:T(8,128)(2,1)}, bf16[4,64,1536]{2,1,0:T(8,128)(2,1)S(1)}, u32[]{:S(2)}) copy-start(bf16[4,64,1536]{2,1,0:T(8,128)(2,1)S(1)} %collective-permute-done.4.refs_2_) | copy-start | bytes 2359300
  72.2 1.0 copy-start.3
  88.5 29.5 %copy-start.11 = (bf16[4,64,1536]{2,1,0:T(8,128)(2,1)S(1)}, bf16[4,64,1536]{2,1,0:T(8,128)(2,1)}, u32[]{:S(2)}) copy-start(bf16[4,64,1536]{2,1,0:T(8,128)(2,1)} %get-tuple-element.33) | copy-start | bytes 2359300
  88.5 75.7 %copy-start.7 = (bf16[4,64,1536]{2,1,0:T(8,128)(2,1)S(1)}, bf16[4,64,1536]{2,1,0:T(8,128)(2,1)}, u32[]{:S(2)}) copy-start(bf16[4,64,1536]{2,1,0:T(8,128)(2,1)} %get-tuple-element.30) | copy-start | bytes 2359300
  113.3 53.5 %copy-start.4 = (bf16[4,512,512]{2,1,0:T(8,128)(2,1)S(1)}, bf16[4,512,512]{2,1,0:T(8,128)(2,1)}, u32[]{:S(2)}) copy-start(bf16[4,512,512]{2,1,0:T(8,128)(2,1)} %get-tuple-element.28) | copy-start | bytes 6291460
  113.3 52.0 %collective-permute-start.12 = (bf16[4,512,512]{2,1,0:T(8,128)(2,1)}, bf16[4,512,512]{2,1,0:T(8,128)(2,1)S(1)}, u32[]{:S(2)}, u32[]{:S(2)}) collective-permute-start(bf16[4,512,512]{2,1,0:T(8,128)(2,1)} %get-tuple-element.29), channel_id=1, source_target_pairs={{0,1},{1,0},{2,3},{3,2},{4,5},{5,4},{6,7},{7,6},{8,9},{9,8},{10,11... | collective-permute-start | bytes 6291464 | tf_op jit(solution)/shard_map/ppermute | solution.py:41
  113.4 21.4 %collective-permute-start.16 = (bf16[4,64,1536]{2,1,0:T(8,128)(2,1)}, bf16[4,64,1536]{2,1,0:T(8,128)(2,1)S(1)}, u32[]{:S(2)}, u32[]{:S(2)}) collective-permute-start(bf16[4,64,1536]{2,1,0:T(8,128)(2,1)} %get-tuple-element.31), channel_id=1, source_target_pairs={{0,8},{8,16},{16,24},{24,0},{1,9},{9,17},{17,25},{25,1},{2,10},{10... | collective-permute-start | bytes 2359304 | tf_op jit(solution)/shard_map/ppermute | solution.py:41
  115.2 37.7 %collective-permute-start.17 = (bf16[4,64,1536]{2,1,0:T(8,128)(2,1)}, bf16[4,64,1536]{2,1,0:T(8,128)(2,1)S(1)}, u32[]{:S(2)}, u32[]{:S(2)}) collective-permute-start(bf16[4,64,1536]{2,1,0:T(8,128)(2,1)} %get-tuple-element.32), channel_id=1, source_target_pairs={{0,16},{8,24},{16,0},{24,8},{1,17},{9,25},{17,1},{25,9},{2,18},{10... | collective-permute-start | bytes 2359304 | tf_op jit(solution)/shard_map/ppermute | solution.py:41
  117.9 46.3 %collective-permute-start.18 = (bf16[4,64,1536]{2,1,0:T(8,128)(2,1)S(1)}, bf16[4,64,1536]{2,1,0:T(8,128)(2,1)S(1)}, u32[]{:S(2)}, u32[]{:S(2)}) collective-permute-start(bf16[4,64,1536]{2,1,0:T(8,128)(2,1)S(1)} %copy-done.11), channel_id=1, source_target_pairs={{0,24},{8,0},{16,8},{24,16},{1,25},{9,1},{17,9},{25,17},{2,26},{10... | collective-permute-start | bytes 2359304 | tf_op jit(solution)/shard_map/ppermute | solution.py:41
  118.5 49.5 %collective-permute-start.22 = (bf16[4,64,1536]{2,1,0:T(8,128)(2,1)}, bf16[4,64,1536]{2,1,0:T(8,128)(2,1)S(1)}, u32[]{:S(2)}, u32[]{:S(2)}) collective-permute-start(bf16[4,64,1536]{2,1,0:T(8,128)(2,1)} %get-tuple-element.35), channel_id=1, source_target_pairs={{0,32},{32,64},{64,96},{96,0},{1,33},{33,65},{65,97},{97,1},{2,34}... | collective-permute-start | bytes 2359304 | tf_op jit(solution)/shard_map/ppermute | solution.py:41
  134.8 34.7 %collective-permute-start.23 = (bf16[4,64,1536]{2,1,0:T(8,128)(2,1)}, bf16[4,64,1536]{2,1,0:T(8,128)(2,1)S(1)}, u32[]{:S(2)}, u32[]{:S(2)}) collective-permute-start(bf16[4,64,1536]{2,1,0:T(8,128)(2,1)} %get-tuple-element.36), channel_id=1, source_target_pairs={{0,64},{32,96},{64,0},{96,32},{1,65},{33,97},{65,1},{97,33},{2,66}... | collective-permute-start | bytes 2359304 | tf_op jit(solution)/shard_map/ppermute | solution.py:41
  152.9 32.7 %collective-permute-start.24 = (bf16[4,64,1536]{2,1,0:T(8,128)(2,1)}, bf16[4,64,1536]{2,1,0:T(8,128)(2,1)S(1)}, u32[]{:S(2)}, u32[]{:S(2)}) collective-permute-start(bf16[4,64,1536]{2,1,0:T(8,128)(2,1)} %get-tuple-element.37), channel_id=1, source_target_pairs={{0,96},{32,0},{64,32},{96,64},{1,97},{33,1},{65,33},{97,65},{2,98}... | collective-permute-start | bytes 2359304 | tf_op jit(solution)/shard_map/ppermute | solution.py:41
  165.3 24.4 %collective-permute-start.19 = (bf16[64,1536]{1,0:T(8,128)(2,1)S(1)}, bf16[64,1536]{1,0:T(8,128)(2,1)S(1)}, u32[]{:S(2)}, u32[]{:S(2)}) collective-permute-start(bf16[64,1536]{1,0:T(8,128)(2,1)S(1)} %get-tuple-element.47), channel_id=1, source_target_pairs={{0,32},{32,64},{64,96},{96,0},{1,33},{33,65},{65,97},{97,1},{2,34}... | collective-permute-start | bytes 589832 | tf_op jit(solution)/shard_map/ppermute | solution.py:41
  165.3 1.5 copy-start.5
  165.3 28.0 %collective-permute-start.20 = (bf16[64,1536]{1,0:T(8,128)(2,1)S(1)}, bf16[64,1536]{1,0:T(8,128)(2,1)S(1)}, u32[]{:S(2)}, u32[]{:S(2)}) collective-permute-start(bf16[64,1536]{1,0:T(8,128)(2,1)S(1)} %get-tuple-element.46), channel_id=1, source_target_pairs={{0,64},{32,96},{64,0},{96,32},{1,65},{33,97},{65,1},{97,33},{2,66}... | collective-permute-start | bytes 589832 | tf_op jit(solution)/shard_map/ppermute | solution.py:41
  166.8 21.8 %copy-start.6 = (bf16[4,64,1536]{2,1,0:T(8,128)(2,1)S(1)}, bf16[4,64,1536]{2,1,0:T(8,128)(2,1)}, u32[]{:S(2)}) copy-start(bf16[4,64,1536]{2,1,0:T(8,128)(2,1)} %get-tuple-element.34) | copy-start | bytes 2359300
  168.0 42.0 %collective-permute-start.13 = (bf16[512,512]{1,0:T(8,128)(2,1)}, bf16[512,512]{1,0:T(8,128)(2,1)S(1)}, u32[]{:S(2)}, u32[]{:S(2)}) collective-permute-start(bf16[512,512]{1,0:T(8,128)(2,1)} %get-tuple-element.38), channel_id=1, source_target_pairs={{0,2},{2,4},{4,6},{6,0},{1,3},{3,5},{5,7},{7,1},{8,10},{10,12},{12... | collective-permute-start | bytes 1572872 | tf_op jit(solution)/shard_map/ppermute | solution.py:41
  169.6 40.4 %collective-permute-start.14 = (bf16[512,512]{1,0:T(8,128)(2,1)S(1)}, bf16[512,512]{1,0:T(8,128)(2,1)}, u32[]{:S(2)}, u32[]{:S(2)}) collective-permute-start(bf16[512,512]{1,0:T(8,128)(2,1)S(1)} %get-tuple-element.40), channel_id=1, source_target_pairs={{0,4},{2,6},{4,0},{6,2},{1,5},{3,7},{5,1},{7,3},{8,12},{10,14},{12... | collective-permute-start | bytes 1572872 | tf_op jit(solution)/shard_map/ppermute | solution.py:41
  185.6 24.4 %collective-permute-start.15 = (bf16[512,512]{1,0:T(8,128)(2,1)S(1)}, bf16[512,512]{1,0:T(8,128)(2,1)}, u32[]{:S(2)}, u32[]{:S(2)}) collective-permute-start(bf16[512,512]{1,0:T(8,128)(2,1)S(1)} %get-tuple-element.39), channel_id=1, source_target_pairs={{0,6},{2,0},{4,2},{6,4},{1,7},{3,1},{5,3},{7,5},{8,14},{10,8},{12,... | collective-permute-start | bytes 1572872 | tf_op jit(solution)/shard_map/ppermute | solution.py:41
  189.7 12.1 %copy-start.8 = (bf16[64,1536]{1,0:T(8,128)(2,1)}, bf16[64,1536]{1,0:T(8,128)(2,1)S(1)}, u32[]{:S(2)}) copy-start(bf16[64,1536]{1,0:T(8,128)(2,1)S(1)} %collective-permute-done.19.refs_1_) | copy-start | bytes 589828
  189.7 6.7 %collective-permute-start.21 = (bf16[64,1536]{1,0:T(8,128)(2,1)S(1)}, bf16[64,1536]{1,0:T(8,128)(2,1)}, u32[]{:S(2)}, u32[]{:S(2)}) collective-permute-start(bf16[64,1536]{1,0:T(8,128)(2,1)S(1)} %get-tuple-element.45), channel_id=1, source_target_pairs={{0,96},{32,0},{64,32},{96,64},{1,97},{33,1},{65,33},{97,65},{2,98}... | collective-permute-start | bytes 589832 | tf_op jit(solution)/shard_map/ppermute | solution.py:41
  193.3 8.5 %copy-start.9 = (bf16[64,1536]{1,0:T(8,128)(2,1)}, bf16[64,1536]{1,0:T(8,128)(2,1)S(1)}, u32[]{:S(2)}) copy-start(bf16[64,1536]{1,0:T(8,128)(2,1)S(1)} %collective-permute-done.20.refs_2_) | copy-start | bytes 589828
  193.3 8.5 %collective-permute-start.25 = (bf16[64,1536]{1,0:T(8,128)(2,1)S(1)}, bf16[64,1536]{1,0:T(8,128)(2,1)}, u32[]{:S(2)}, u32[]{:S(2)}) collective-permute-start(bf16[64,1536]{1,0:T(8,128)(2,1)S(1)} %get-tuple-element.43), channel_id=1, source_target_pairs={{0,8},{8,16},{16,24},{24,0},{1,9},{9,17},{17,25},{25,1},{2,10},{10... | collective-permute-start | bytes 589832 | tf_op jit(solution)/shard_map/ppermute | solution.py:41
  196.5 7.5 %collective-permute-start.26 = (bf16[64,1536]{1,0:T(8,128)(2,1)}, bf16[64,1536]{1,0:T(8,128)(2,1)}, u32[]{:S(2)}, u32[]{:S(2)}) collective-permute-start(bf16[64,1536]{1,0:T(8,128)(2,1)} %get-tuple-element.42), channel_id=1, source_target_pairs={{0,16},{8,24},{16,0},{24,8},{1,17},{9,25},{17,1},{25,9},{2,18},{10... | collective-permute-start | bytes 589832 | tf_op jit(solution)/shard_map/ppermute | solution.py:41
  201.8 6.0 %collective-permute-start.27 = (bf16[64,1536]{1,0:T(8,128)(2,1)}, bf16[64,1536]{1,0:T(8,128)(2,1)}, u32[]{:S(2)}, u32[]{:S(2)}) collective-permute-start(bf16[64,1536]{1,0:T(8,128)(2,1)} %get-tuple-element.41), channel_id=1, source_target_pairs={{0,24},{8,0},{16,8},{24,16},{1,25},{9,1},{17,9},{25,17},{2,26},{10... | collective-permute-start | bytes 589832 | tf_op jit(solution)/shard_map/ppermute | solution.py:41

commit v2 on v1

--- a/solution.py
+++ b/solution.py
@@ -21,10 +21,10 @@
 HB = pl.BlockSpec(memory_space=pl.ANY)
 NT = (((1,), (1,)), ((), ()))
 
-GATHER_SIGMA = (("x", "z", 0, 64),)
+GATHER_SIGMA = (("x", "z", 0, 32), ("z", "x", 32, 64))
 GATHER_THETA = (("z", "x", 0, 64),)
-SCATTER_THETA = (("x", "z", 0, 64),)
-SCATTER_VAR = (("z", "x", 0, 64),)
+SCATTER_THETA = (("z", "x", 0, 64),)
+SCATTER_VAR = (("x", "z", 0, 64),)
 PLACE = {"z": 0, "x": 1, "y": 2, "core": 3}
 
 
@@ -37,8 +37,7 @@
 
 
 def sent(value, axis, step):
-    n = lax.axis_size(axis)
-    return lax.ppermute(value, axis, [(i, (i + step) % n) for i in range(n)])
+    return lax.ppermute(value, axis, [(i, i ^ step) for i in range(lax.axis_size(axis))])
 
 
 def steps_of(value, axis):
@@ -130,7 +129,7 @@
     )(*args)
 
 
-GROUPS = 2
+EARLY_GROUPS, MIDDLE_GROUPS, LATE_GROUPS = 4, 2, 4
 
 
 def issue(copies):
@@ -143,13 +142,13 @@
     return pl.ds(pl.multiple_of(group * w, w), w)
 
 
-def gather_starts(place, paths, groups, whole, sems, per):
-    for g in range(GROUPS):
+def gather_starts(place, paths, groups, whole, sems, per, count):
+    for g in range(count):
         cols = slice(g * per * LANE, (g + 1) * per * LANE)
         for (one, two, lo, hi), refs in zip(paths, groups):
             for k in range(RING):
                 for j in range(RING):
-                    spot = {one: (place[PLACE[one]] - j) & 3, two: (place[PLACE[two]] - k) & 3}
+                    spot = {one: place[PLACE[one]] ^ j, two: place[PLACE[two]] ^ k}
                     pltpu.make_async_copy(
                         refs[k].at[j, :, cols], whole.at[spot["z"], spot["x"], lo:hi, cols], sems.at[g]
                     ).start()
@@ -165,7 +164,7 @@
     for (one, two, lo, hi), refs in zip(paths, groups):
         for k in range(RING):
             for j in range(RING):
-                spot = {one: (place[PLACE[one]] + k) & 3, two: (place[PLACE[two]] + j) & 3}
+                spot = {one: place[PLACE[one]] ^ k, two: place[PLACE[two]] ^ j}
                 pltpu.make_async_copy(
                     held.at[spot["z"], spot["x"], lo:hi, cols], refs[k].at[j, :, cols], sem
                 ).start()
@@ -176,7 +175,7 @@
     place = [lax.axis_index(a) for a in ROW + COL]
     blocks = tok.shape[1] // LANE
     ks = rows.shape[1]
-    per = cot.shape[1] // LANE // GROUPS
+    per = cot.shape[1] // LANE // EARLY_GROUPS
     for k in range(blocks):
         at = slice(k * LANE, (k + 1) * LANE)
         wide = tok[:, at].astype(f32)
@@ -197,7 +196,7 @@
         scatter_start(place, SCATTER_THETA, held, chunked(outs, RING), sems.at[2], column_span(g, per))
         return 0
 
-    lax.fori_loop(0, GROUPS, group, 0)
+    lax.fori_loop(0, EARLY_GROUPS, group, 0)
     for c in saves:
         c.wait()
     pltpu.make_async_copy(held, held, sems.at[2]).wait()
@@ -231,11 +230,11 @@
     gv_out, rn_out, sq, sqt, noise, cot, whole, held, gv, rn, s_sig, s_in, s_one, s_out = refs[-14:]
     place = [lax.axis_index(a) for a in ROW + COL]
     ks = rows.shape[1]
-    per = noise.shape[1] // LANE // GROUPS
+    per = noise.shape[1] // LANE // MIDDLE_GROUPS
     first = pltpu.make_async_copy(sq_in, sq, s_one.at[0])
     second = pltpu.make_async_copy(sqt_in, sqt, s_one.at[1])
     first.start()
-    gather_starts(place, GATHER_SIGMA, chunked(sigma_refs, RING), whole, s_sig, per)
+    gather_starts(place, GATHER_SIGMA, chunked(sigma_refs, RING), whole, s_sig, per, MIDDLE_GROUPS)
 
     def loads(g):
         at = column_span(g, per)
@@ -253,7 +252,7 @@
 
     issue(loads(0))
     second.start()
-    for g in range(1, GROUPS):
+    for g in range(1, MIDDLE_GROUPS):
         issue(loads(g))
     first.wait()
 
@@ -269,7 +268,7 @@
             inv = lax.rsqrt(var)
             draw = noise[:, at].astype(f32)
             rn[:, at] = var * inv * draw
-            gv[:, at] = (cot[:, at].astype(f32) * draw * (0.5 * inv)).astype(bf16)
+            gv[:, at] = (cot[:, at].astype(f32) * draw * inv).astype(bf16)
 
         @pl.when(g == 0)
         def _():
@@ -285,8 +284,8 @@
         scatter_start(place, SCATTER_VAR, held, chunked(outs, RING), s_one.at[2], column_span(g, per))
         return 0
 
-    lax.fori_loop(0, GROUPS, group, 0)
-    for g in range(GROUPS):
+    lax.fori_loop(0, MIDDLE_GROUPS, group, 0)
+    for g in range(MIDDLE_GROUPS):
         for c in saves(g):
             c.wait()
     pltpu.make_async_copy(held, held, s_one.at[2]).wait()
@@ -311,10 +310,10 @@
             pltpu.VMEM((RING, RING, own, ff), bf16),
             pltpu.VMEM((t, ff), bf16),
             pltpu.VMEM((t, ff), f32),
-            pltpu.SemaphoreType.DMA((GROUPS,)),
-            pltpu.SemaphoreType.DMA((2, GROUPS)),
+            pltpu.SemaphoreType.DMA((MIDDLE_GROUPS,)),
+            pltpu.SemaphoreType.DMA((2, MIDDLE_GROUPS)),
             pltpu.SemaphoreType.DMA((3,)),
-            pltpu.SemaphoreType.DMA((2, GROUPS)),
+            pltpu.SemaphoreType.DMA((2, MIDDLE_GROUPS)),
         ],
         compiler_params=PARAMS,
         name="middle",
@@ -328,7 +327,7 @@
     (out_out, away_out, home_out, tok, cot, gv, rn, out, both, sigma, theta, acc, s_w, s_in, s_one, s_out) = refs[n_s + n_t :]
     place = [lax.axis_index(a) for a in ROW + COL]
     ks = rows.shape[1]
-    per = cot.shape[1] // LANE // GROUPS
+    per = cot.shape[1] // LANE // LATE_GROUPS
     first = pltpu.make_async_copy(tok_in, tok, s_one.at[0])
     first.start()
 
@@ -342,9 +341,9 @@
         return pltpu.make_async_copy(out.at[:, at], out_out.at[:, at], s_out.at[g])
 
     issue(loads(0))
-    gather_starts(place, GATHER_THETA, chunked(theta_refs, RING), theta, s_w.at[0], per)
-    gather_starts(place, GATHER_SIGMA, chunked(sigma_refs, RING), sigma, s_w.at[1], per)
-    for g in range(1, GROUPS):
+    gather_starts(place, GATHER_THETA, chunked(theta_refs, RING), theta, s_w.at[0], per, LATE_GROUPS)
+    gather_starts(place, GATHER_SIGMA, chunked(sigma_refs, RING), sigma, s_w.at[1], per, LATE_GROUPS)
+    for g in range(1, LATE_GROUPS):
         issue(loads(g))
     acc[...] = jnp.zeros_like(acc)
     first.wait()
@@ -369,21 +368,21 @@
                 for h in range(2):
                     pick = at_block(rows[n, 2 * q + h])
                     p = slice(h * LANE, (h + 1) * LANE)
-                    acc[:, pick] += one[:, p] + 2.0 * tok[:, pick].astype(f32) * two[:, p]
+                    acc[:, pick] += one[:, p] + tok[:, pick].astype(f32) * two[:, p]
         save(g).start()
         return 0
 
-    lax.fori_loop(0, GROUPS, group, 0)
+    lax.fori_loop(0, LATE_GROUPS, group, 0)
     w = away_out.shape[2]
     core = place[PLACE["core"]]
     ends = []
     for side, (ref, half) in enumerate(((away_out, 1 - core), (home_out, core))):
         for k in range(RING):
-            y = (place[PLACE["y"]] + k) & 3
+            y = place[PLACE["y"]] ^ k
             both[side, k] = acc[:, pl.ds(pl.multiple_of((y * 2 + half) * w, w), w)].astype(bf16)
             ends.append(pltpu.make_async_copy(both.at[side, k], ref.at[k], s_one.at[1 + side * RING + k]))
             ends[-1].start()
-    for c in [save(g) for g in range(GROUPS)] + ends:
+    for c in [save(g) for g in range(LATE_GROUPS)] + ends:
         c.wait()
 
 
@@ -408,10 +407,10 @@
             pltpu.VMEM((RING, RING, own, ff), bf16),
             pltpu.VMEM((RING, RING, own, ff), bf16),
             pltpu.VMEM((t, d), f32),
-            pltpu.SemaphoreType.DMA((2, GROUPS)),
-            pltpu.SemaphoreType.DMA((3, GROUPS)),
+            pltpu.SemaphoreType.DMA((2, LATE_GROUPS)),
+            pltpu.SemaphoreType.DMA((3, LATE_GROUPS)),
             pltpu.SemaphoreType.DMA((1 + 2 * RING,)),
-            pltpu.SemaphoreType.DMA((GROUPS,)),
+            pltpu.SemaphoreType.DMA((LATE_GROUPS,)),
         ],
         compiler_params=PARAMS,
         name="late",
@@ -432,7 +431,7 @@
     got_theta = scatter(parts_theta, SCATTER_THETA)
     grad_theta = final(got_theta, SCATTER_THETA, theta.shape, inv_root, None)
     got_var = scatter(parts_var, SCATTER_VAR)
-    grad_logvar = final(got_var, SCATTER_VAR, theta.shape, width * inv_root, log_sigma2)
+    grad_logvar = final(got_var, SCATTER_VAR, theta.shape, 0.5 * width * inv_root, log_sigma2)
     came = sent(away, "core", 1)
     pairs = [(home[k].astype(f32) + came[k].astype(f32)).astype(bf16) for k in range(RING)]
     arrived = steps_sent(pairs, "y")

time: 213 us -> 205 us (0.962)
  the two profiles are of different devices: /device:TPU:0 before, /device:TPU:1 now
where the time goes in v2:
time: 205 us; the launch traced here: 204 us
  waiting for transfers between devices  86.8 us (42%)
  Pallas kernels  57.5 us (28%)
  starting transfers between devices  49.3 us (24%)
  other arithmetic  9.01 us (4%)
    ppermute x34, waiting for transfers between devices, sent(): lax.ppermute(value, axis, [(i, i ^ step) for i in range(lax.axis_size(axi...  86.8 us
    ppermute x34, starting transfers between devices, sent(): lax.ppermute(value, axis, [(i, i ^ step) for i in range(lax.axis_size(axi...  49.3 us
    pallas_call x1, Pallas kernels, late(): pl.pallas_call(late_kernel, out_shape=shapes, in_specs=[SM] + [HB] * (4 +...  25 us
    pallas_call x1, Pallas kernels, middle(): pl.pallas_call(middle_kernel, out_shape=shapes, in_specs=[SM, HB, HB, HB,...  15.4 us
    pallas_call x1, Pallas kernels, early(): pl.pallas_call(early_kernel, out_shape=shapes, in_specs=[SM, VB, VB], out...  11 us
    pallas_call x2, Pallas kernels, final(): pl.pallas_call(final_kernel(paths, scale, ls is not None), out_shape=sds(...  4.26 us
  transfers between devices with their start and end apart: 34, of which 11 were waited for; matrix products, arithmetic and copies ran while one was open for 3% of the time, Pallas kernels for 15%

profile of v2, /device:TPU:1, one launch (start us, length us, event | category | flops | bytes accessed | tf_op | source)
XLA Modules:
  0.0 204.4 jit_solution(12984849568120196574)
XLA Ops:
  0.6 1.9 prep.1
  2.5 2.5 %collective-permute-start.6 = (bf16[32,1536]{1,0:T(8,128)(2,1)}, bf16[32,1536]{1,0:T(8,128)(2,1)S(1)}, u32[]{:S(2)}, u32[]{:S(2)}) collective-permute-start(bf16[32,1536]{1,0:T(8,128)(2,1)} %get-tuple-element.25), channel_id=1, source_target_pairs={{0,32},{32,0},{64,96},{96,64},{1,33},{33,1},{65,97},{97,65},{2,34}... | collective-permute-start | bytes 294920 | tf_op jit(solution)/shard_map/ppermute | solution.py:40
  5.0 3.3 %collective-permute-start.7 = (bf16[32,1536]{1,0:T(8,128)(2,1)}, bf16[32,1536]{1,0:T(8,128)(2,1)S(1)}, u32[]{:S(2)}, u32[]{:S(2)}) collective-permute-start(bf16[32,1536]{1,0:T(8,128)(2,1)} %get-tuple-element.25), channel_id=1, source_target_pairs={{0,64},{32,96},{64,0},{96,32},{1,65},{33,97},{65,1},{97,33},{2,66}... | collective-permute-start | bytes 294920 | tf_op jit(solution)/shard_map/ppermute | solution.py:40
  8.3 1.2 collective-permute-start
  9.5 2.5 %collective-permute-start.1 = (bf16[32,1536]{1,0:T(8,128)(2,1)}, bf16[32,1536]{1,0:T(8,128)(2,1)S(1)}, u32[]{:S(2)}, u32[]{:S(2)}) collective-permute-start(bf16[32,1536]{1,0:T(8,128)(2,1)} %get-tuple-element.24), channel_id=1, source_target_pairs={{0,16},{8,24},{16,0},{24,8},{1,17},{9,25},{17,1},{25,9},{2,18},{10... | collective-permute-start | bytes 294920 | tf_op jit(solution)/shard_map/ppermute | solution.py:40
  12.5 1.0 collective-permute-start.13
  13.5 1.8 collective-permute-done.8
  15.5 0.9 pad_maximum_fusion.2.refs_4_
  16.5 2.8 %collective-permute-start.10 = (bf16[4,32,1536]{2,1,0:T(8,128)(2,1)S(1)}, bf16[4,32,1536]{2,1,0:T(8,128)(2,1)S(1)}, u32[]{:S(2)}, u32[]{:S(2)}) collective-permute-start(bf16[4,32,1536]{2,1,0:T(8,128)(2,1)S(1)} %pad_maximum_fusion.2.refs_4_), channel_id=1, source_target_pairs={{0,16},{8,24},{16,0},{24,8},{1,17},{9,25},{17,1},{25,9},{2,18},{10... | collective-permute-start | bytes 1179656 | tf_op jit(solution)/shard_map/ppermute | solution.py:40
  19.4 0.9 collective-permute-start.11
  20.2 0.9 pad_maximum_fusion.1.refs_0_
  21.2 1.4 collective-permute-start.3
  22.6 2.9 %collective-permute-done.14 = bf16[64,1536]{1,0:T(8,128)(2,1)S(1)} collective-permute-done((bf16[64,1536]{1,0:T(8,128)(2,1)}, bf16[64,1536]{1,0:T(8,128)(2,1)S(1)}, u32[]{:S(2)}, u32[]{:S(2)}) %collective-permute-start.14) | collective-permute-done | bytes 196640 | tf_op jit(solution)/shard_map/ppermute | solution.py:40
  25.5 1.0 pad_maximum_fusion.refs_8_
  26.6 1.7 collective-permute-start.15
  28.3 2.0 collective-permute-start.16
  30.3 7.3 %collective-permute-done.11.refs_7_ = bf16[4,32,1536]{2,1,0:T(8,128)(2,1)S(1)} collective-permute-done((bf16[4,32,1536]{2,1,0:T(8,128)(2,1)S(1)}, bf16[4,32,1536]{2,1,0:T(8,128)(2,1)S(1)}, u32[]{:S(2)}, u32[]{:S(2)}) %collective-permute-start.11) | collective-permute-done | bytes 393248 | tf_op jit(solution)/shard_map/ppermute | solution.py:40
  37.6 2.5 %collective-permute-start.17 = (bf16[4,64,1536]{2,1,0:T(8,128)(2,1)S(1)}, bf16[4,64,1536]{2,1,0:T(8,128)(2,1)}, u32[]{:S(2)}, u32[]{:S(2)}) collective-permute-start(bf16[4,64,1536]{2,1,0:T(8,128)(2,1)S(1)} %pad_maximum_fusion.refs_8_), channel_id=1, source_target_pairs={{0,24},{8,16},{16,8},{24,0},{1,25},{9,17},{17,9},{25,1},{2,26},{10... | collective-permute-start | bytes 2359304 | tf_op jit(solution)/shard_map/ppermute | solution.py:40
  40.1 2.5 %collective-permute-start.5 = (bf16[4,32,1536]{2,1,0:T(8,128)(2,1)S(1)}, bf16[4,32,1536]{2,1,0:T(8,128)(2,1)S(1)}, u32[]{:S(2)}, u32[]{:S(2)}) collective-permute-start(bf16[4,32,1536]{2,1,0:T(8,128)(2,1)S(1)} %pad_maximum_fusion.1.refs_0_), channel_id=1, source_target_pairs={{0,96},{32,64},{64,32},{96,0},{1,97},{33,65},{65,33},{97,1},{2,98}... | collective-permute-start | bytes 1179656 | tf_op jit(solution)/shard_map/ppermute | solution.py:40
  43.3 11.0 %early.1 = (bf16[4,64,1536]{2,1,0:T(8,128)(2,1)}, bf16[4,64,1536]{2,1,0:T(8,128)(2,1)}, bf16[4,64,1536]{2,1,0:T(8,128)(2,1)}, bf16[4,64,1536]{2,1,0:T(8,128)(2,1...) custom-call(s32[12,8]{1,0:T(8,128)} %copy.12.rows, bf16[512,4096]{1,0:T(8,128)(2,1)} %tok_in.1, ...), custom_call_target="tpu_custom_call" | custom-call | tf_op jit(solution)/shard_map/early/pallas_call | solution.py:209
  54.5 15.0 %collective-permute-done.9.refs_5_ = bf16[4,32,1536]{2,1,0:T(8,128)(2,1)} collective-permute-done((bf16[4,32,1536]{2,1,0:T(8,128)(2,1)S(1)}, bf16[4,32,1536]{2,1,0:T(8,128)(2,1)}, u32[]{:S(2)}, u32[]{:S(2)}) %collective-permute-start.9) | collective-permute-done | bytes 393248 | tf_op jit(solution)/shard_map/ppermute | solution.py:40
  69.5 15.4 %middle.1 = (bf16[4,64,1536]{2,1,0:T(8,128)(2,1)}, bf16[4,64,1536]{2,1,0:T(8,128)(2,1)}, bf16[4,64,1536]{2,1,0:T(8,128)(2,1)}, bf16[4,64,1536]{2,1,0:T(8,128)(2,...) custom-call(s32[12,8]{1,0:T(8,128)} %copy.12.rows, bf16[512,4096]{1,0:T(8,128)(2,1)} %get-tuple-element.22.sq_in, ...), custom_call_target="tpu_custom_call" | custom-call | tf_op jit(solution)/shard_map/middle/pallas_call | solution.py:299
  84.9 25.0 %late.1 = (bf16[512,1536]{1,0:T(8,128)(2,1)}, bf16[4,512,512]{2,1,0:T(8,128)(2,1)}, bf16[4,512,512]{2,1,0:T(8,128)(2,1)}) custom-call(s32[12,8]{1,0:T(8,128)} %copy.12.rows, bf16[512,4096]{1,0:T(8,128)(2,1)} %tok_in.1, bf16[512,1536]{1,0:T(8,128)(2,1)} %cot_in.3, bf16[512,1536]{1,0:T(8,128)(2,1)} %get-tuple-element.26.gv_in, ...), custom_call_target="tpu_custom_call" | custom-call | tf_op jit(solution)/shard_map/late/pallas_call | solution.py:395
  109.9 2.8 %collective-permute-start.18 = (bf16[4,512,512]{2,1,0:T(8,128)(2,1)}, bf16[4,512,512]{2,1,0:T(8,128)(2,1)S(1)}, u32[]{:S(2)}, u32[]{:S(2)}) collective-permute-start(bf16[4,512,512]{2,1,0:T(8,128)(2,1)} %get-tuple-element.31), channel_id=1, source_target_pairs={{0,1},{1,0},{2,3},{3,2},{4,5},{5,4},{6,7},{7,6},{8,9},{9,8},{10,11... | collective-permute-start | bytes 6291464 | tf_op jit(solution)/shard_map/ppermute | solution.py:40
  112.8 2.0 collective-permute-start.22
  114.8 1.5 collective-permute-start.23
  116.3 0.9 collective-permute-start.24
  117.2 0.9 collective-permute-start.28
  118.1 14.7 %collective-permute-done.22 = bf16[4,64,1536]{2,1,0:T(8,128)(2,1)S(1)} collective-permute-done((bf16[4,64,1536]{2,1,0:T(8,128)(2,1)}, bf16[4,64,1536]{2,1,0:T(8,128)(2,1)S(1)}, u32[]{:S(2)}, u32[]{:S(2)}) %collective-permute-start.22) | collective-permute-done | bytes 786464 | tf_op jit(solution)/shard_map/ppermute | solution.py:40
  132.8 2.2 %collective-permute-start.29 = (bf16[4,64,1536]{2,1,0:T(8,128)(2,1)}, bf16[4,64,1536]{2,1,0:T(8,128)(2,1)S(1)}, u32[]{:S(2)}, u32[]{:S(2)}) collective-permute-start(bf16[4,64,1536]{2,1,0:T(8,128)(2,1)} %get-tuple-element.38), channel_id=1, source_target_pairs={{0,16},{8,24},{16,0},{24,8},{1,17},{9,25},{17,1},{25,9},{2,18},{10... | collective-permute-start | bytes 2359304 | tf_op jit(solution)/shard_map/ppermute | solution.py:40
  135.0 16.0 %collective-permute-done.23 = bf16[4,64,1536]{2,1,0:T(8,128)(2,1)S(1)} collective-permute-done((bf16[4,64,1536]{2,1,0:T(8,128)(2,1)}, bf16[4,64,1536]{2,1,0:T(8,128)(2,1)S(1)}, u32[]{:S(2)}, u32[]{:S(2)}) %collective-permute-start.23) | collective-permute-done | bytes 786464 | tf_op jit(solution)/shard_map/ppermute | solution.py:40
  150.9 1.9 collective-permute-start.30
  152.8 1.1 fusion.9
  153.9 1.1 collective-permute-start.25
  155.0 1.9 collective-permute-start.26
  157.0 1.3 fusion.3
  158.2 1.2 collective-permute-start.19
  159.5 2.7 %collective-permute-start.20 = (bf16[512,512]{1,0:T(8,128)(2,1)S(1)}, bf16[512,512]{1,0:T(8,128)(2,1)}, u32[]{:S(2)}, u32[]{:S(2)}) collective-permute-start(bf16[512,512]{1,0:T(8,128)(2,1)S(1)} %get-tuple-element.42), channel_id=1, source_target_pairs={{0,4},{2,6},{4,0},{6,2},{1,5},{3,7},{5,1},{7,3},{8,12},{10,14},{12... | collective-permute-start | bytes 1572872 | tf_op jit(solution)/shard_map/ppermute | solution.py:40
  162.2 14.3 %collective-permute-done.30 = bf16[4,64,1536]{2,1,0:T(8,128)(2,1)S(1)} collective-permute-done((bf16[4,64,1536]{2,1,0:T(8,128)(2,1)}, bf16[4,64,1536]{2,1,0:T(8,128)(2,1)S(1)}, u32[]{:S(2)}, u32[]{:S(2)}) %collective-permute-start.30) | collective-permute-done | bytes 786464 | tf_op jit(solution)/shard_map/ppermute | solution.py:40
  176.5 2.9 %collective-permute-start.21 = (bf16[512,512]{1,0:T(8,128)(2,1)S(1)}, bf16[512,512]{1,0:T(8,128)(2,1)}, u32[]{:S(2)}, u32[]{:S(2)}) collective-permute-start(bf16[512,512]{1,0:T(8,128)(2,1)S(1)} %get-tuple-element.41), channel_id=1, source_target_pairs={{0,6},{2,4},{4,2},{6,0},{1,7},{3,5},{5,3},{7,1},{8,14},{10,12},{12... | collective-permute-start | bytes 1572872 | tf_op jit(solution)/shard_map/ppermute | solution.py:40
  179.4 1.1 fusion.13
  181.4 5.8 %collective-permute-done.27.refs_3_ = bf16[64,1536]{1,0:T(8,128)(2,1)} collective-permute-done((bf16[64,1536]{1,0:T(8,128)(2,1)S(1)}, bf16[64,1536]{1,0:T(8,128)(2,1)}, u32[]{:S(2)}, u32[]{:S(2)}) %collective-permute-start.27) | collective-permute-done | bytes 196640 | tf_op jit(solution)/shard_map/ppermute | solution.py:40
  187.3 1.4 collective-permute-start.33
  188.7 2.1 %shard_map.93 = f32[12,64,128]{2,1,0:T(8,128)} custom-call(bf16[64,1536]{1,0:T(8,128)(2,1)} %get-tuple-element.50.refs_0_, bf16[64,1536]{1,0:T(8,128)(2,1)} %copy-done.12, bf16[64,1536]{1,0:T(8,128)(2,1)} %copy-done.13, bf16[64,1536]{1,0:T(8,128)(2,1)} %collective-permute-done.27.refs_3_), custom_call_target="tpu_custom_call" | custom-call | tf_op jit(solution)/shard_map/pallas_call | solution.py:127
  190.8 2.8 %collective-permute-done.32.refs_3_ = bf16[64,1536]{1,0:T(8,128)(2,1)} collective-permute-done((bf16[64,1536]{1,0:T(8,128)(2,1)}, bf16[64,1536]{1,0:T(8,128)(2,1)}, u32[]{:S(2)}, u32[]{:S(2)}) %collective-permute-start.32) | collective-permute-done | bytes 196640 | tf_op jit(solution)/shard_map/ppermute | solution.py:40
  193.6 6.0 %collective-permute-done.33.refs_4_ = bf16[64,1536]{1,0:T(8,128)(2,1)} collective-permute-done((bf16[64,1536]{1,0:T(8,128)(2,1)}, bf16[64,1536]{1,0:T(8,128)(2,1)}, u32[]{:S(2)}, u32[]{:S(2)}) %collective-permute-start.33) | collective-permute-done | bytes 196640 | tf_op jit(solution)/shard_map/ppermute | solution.py:40
  199.6 2.2 %shard_map.94 = f32[12,64,128]{2,1,0:T(8,128)} custom-call(f32[12,64,128]{2,1,0:T(8,128)} %refs_0_.1, bf16[64,1536]{1,0:T(8,128)(2,1)} %get-tuple-element.46.refs_1_, bf16[64,1536]{1,0:T(8,128)(2,1)} %collective-permute-done.31.refs_2_, bf16[64,1536]{1,0:T(8,128)(2,1)} %collective-permute-done.32.refs_3_, bf16[64,1536]{1,0:T(8,128)(2,1)} %collective-permute-done.33.refs_4_), custom_call_target="tpu_custom_call" | custom-call | tf_op jit(solution)/shard_map/pallas_call | solution.py:127
  201.8 2.7 %fusion.1 = f32[512,512]{1,0:T(8,128)} fusion(bf16[512,512]{1,0:T(8,128)(2,1)} %collective-permute-done.21, bf16[512,512]{1,0:T(8,128)(2,1)} %collective-permute-done.20, bf16[512,512]{1,0:T(8,128)(2,1)S(1)} %collective-permute-done.19, bf16[4,512,512]{2,1,0:T(8,128)(2,1)} %copy-done.4, bf16[4,512,512]{2,1,0:T(8,128)(2,1)S(1)} %copy-done.3), kind=kLoop, calls=%fused_computation.2 | loop fusion | flops 2883584 | bytes 3670016 | tf_op jit(solution)/shard_map/add | solution.py:440
  (66 shorter events, 2.8 us)
Async XLA Ops:
  0.6 42.0 %copy-start.14 = (s32[12,8]{0,1:T(8,128)S(1)}, s32[12,8]{0,1:T(8,128)}, u32[]{:S(2)}) copy-start(s32[12,8]{0,1:T(8,128)} %param.9) | copy-start | bytes 1156
  2.5 9.4 %collective-permute-start.6 = (bf16[32,1536]{1,0:T(8,128)(2,1)}, bf16[32,1536]{1,0:T(8,128)(2,1)S(1)}, u32[]{:S(2)}, u32[]{:S(2)}) collective-permute-start(bf16[32,1536]{1,0:T(8,128)(2,1)} %get-tuple-element.25), channel_id=1, source_target_pairs={{0,32},{32,0},{64,96},{96,64},{1,33},{33,1},{65,97},{97,65},{2,34}... | collective-permute-start | bytes 294920 | tf_op jit(solution)/shard_map/ppermute | solution.py:40
  5.0 7.5 %collective-permute-start.7 = (bf16[32,1536]{1,0:T(8,128)(2,1)}, bf16[32,1536]{1,0:T(8,128)(2,1)S(1)}, u32[]{:S(2)}, u32[]{:S(2)}) collective-permute-start(bf16[32,1536]{1,0:T(8,128)(2,1)} %get-tuple-element.25), channel_id=1, source_target_pairs={{0,64},{32,96},{64,0},{96,32},{1,65},{33,97},{65,1},{97,33},{2,66}... | collective-permute-start | bytes 294920 | tf_op jit(solution)/shard_map/ppermute | solution.py:40
  8.3 7.0 %collective-permute-start.8 = (bf16[32,1536]{1,0:T(8,128)(2,1)}, bf16[32,1536]{1,0:T(8,128)(2,1)S(1)}, u32[]{:S(2)}, u32[]{:S(2)}) collective-permute-start(bf16[32,1536]{1,0:T(8,128)(2,1)} %get-tuple-element.25), channel_id=1, source_target_pairs={{0,96},{32,64},{64,32},{96,0},{1,97},{33,65},{65,33},{97,1},{2,98}... | collective-permute-start | bytes 294920 | tf_op jit(solution)/shard_map/ppermute | solution.py:40
  8.3 8.2 %collective-permute-start = (bf16[32,1536]{1,0:T(8,128)(2,1)}, bf16[32,1536]{1,0:T(8,128)(2,1)S(1)}, u32[]{:S(2)}, u32[]{:S(2)}) collective-permute-start(bf16[32,1536]{1,0:T(8,128)(2,1)} %get-tuple-element.24), channel_id=1, source_target_pairs={{0,8},{8,0},{16,24},{24,16},{1,9},{9,1},{17,25},{25,17},{2,10},{10... | collective-permute-start | bytes 294920 | tf_op jit(solution)/shard_map/ppermute | solution.py:40
  9.5 7.1 %collective-permute-start.1 = (bf16[32,1536]{1,0:T(8,128)(2,1)}, bf16[32,1536]{1,0:T(8,128)(2,1)S(1)}, u32[]{:S(2)}, u32[]{:S(2)}) collective-permute-start(bf16[32,1536]{1,0:T(8,128)(2,1)} %get-tuple-element.24), channel_id=1, source_target_pairs={{0,16},{8,24},{16,0},{24,8},{1,17},{9,25},{17,1},{25,9},{2,18},{10... | collective-permute-start | bytes 294920 | tf_op jit(solution)/shard_map/ppermute | solution.py:40
  11.9 7.4 %collective-permute-start.2 = (bf16[32,1536]{1,0:T(8,128)(2,1)}, bf16[32,1536]{1,0:T(8,128)(2,1)S(1)}, u32[]{:S(2)}, u32[]{:S(2)}) collective-permute-start(bf16[32,1536]{1,0:T(8,128)(2,1)} %get-tuple-element.24), channel_id=1, source_target_pairs={{0,24},{8,16},{16,8},{24,0},{1,25},{9,17},{17,9},{25,1},{2,26},{10... | collective-permute-start | bytes 294920 | tf_op jit(solution)/shard_map/ppermute | solution.py:40
  12.5 8.7 %collective-permute-start.13 = (bf16[64,1536]{1,0:T(8,128)(2,1)}, bf16[64,1536]{1,0:T(8,128)(2,1)S(1)}, u32[]{:S(2)}, u32[]{:S(2)}) collective-permute-start(bf16[64,1536]{1,0:T(8,128)(2,1)} %get-tuple-element.28), channel_id=1, source_target_pairs={{0,64},{32,96},{64,0},{96,32},{1,65},{33,97},{65,1},{97,33},{2,66}... | collective-permute-start | bytes 589832 | tf_op jit(solution)/shard_map/ppermute | solution.py:40
  15.3 10.2 %collective-permute-start.14 = (bf16[64,1536]{1,0:T(8,128)(2,1)}, bf16[64,1536]{1,0:T(8,128)(2,1)S(1)}, u32[]{:S(2)}, u32[]{:S(2)}) collective-permute-start(bf16[64,1536]{1,0:T(8,128)(2,1)} %get-tuple-element.28), channel_id=1, source_target_pairs={{0,96},{32,64},{64,32},{96,0},{1,97},{33,65},{65,33},{97,1},{2,98}... | collective-permute-start | bytes 589832 | tf_op jit(solution)/shard_map/ppermute | solution.py:40
  16.4 38.0 %copy-start = (bf16[4,32,1536]{2,1,0:T(8,128)(2,1)}, bf16[4,32,1536]{2,1,0:T(8,128)(2,1)S(1)}, u32[]{:S(2)}) copy-start(bf16[4,32,1536]{2,1,0:T(8,128)(2,1)S(1)} %pad_maximum_fusion.2.refs_4_) | copy-start | bytes 1179652
  16.4 9.1 %collective-permute-start.12 = (bf16[64,1536]{1,0:T(8,128)(2,1)}, bf16[64,1536]{1,0:T(8,128)(2,1)S(1)}, u32[]{:S(2)}, u32[]{:S(2)}) collective-permute-start(bf16[64,1536]{1,0:T(8,128)(2,1)} %get-tuple-element.28), channel_id=1, source_target_pairs={{0,32},{32,0},{64,96},{96,64},{1,33},{33,1},{65,97},{97,65},{2,34}... | collective-permute-start | bytes 589832 | tf_op jit(solution)/shard_map/ppermute | solution.py:40
  16.5 11.8 %collective-permute-start.10 = (bf16[4,32,1536]{2,1,0:T(8,128)(2,1)S(1)}, bf16[4,32,1536]{2,1,0:T(8,128)(2,1)S(1)}, u32[]{:S(2)}, u32[]{:S(2)}) collective-permute-start(bf16[4,32,1536]{2,1,0:T(8,128)(2,1)S(1)} %pad_maximum_fusion.2.refs_4_), channel_id=1, source_target_pairs={{0,16},{8,24},{16,0},{24,8},{1,17},{9,25},{17,1},{25,9},{2,18},{10... | collective-permute-start | bytes 1179656 | tf_op jit(solution)/shard_map/ppermute | solution.py:40
  19.4 18.2 %collective-permute-start.11 = (bf16[4,32,1536]{2,1,0:T(8,128)(2,1)S(1)}, bf16[4,32,1536]{2,1,0:T(8,128)(2,1)S(1)}, u32[]{:S(2)}, u32[]{:S(2)}) collective-permute-start(bf16[4,32,1536]{2,1,0:T(8,128)(2,1)S(1)} %pad_maximum_fusion.2.refs_4_), channel_id=1, source_target_pairs={{0,24},{8,16},{16,8},{24,0},{1,25},{9,17},{17,9},{25,1},{2,26},{10... | collective-permute-start | bytes 1179656 | tf_op jit(solution)/shard_map/ppermute | solution.py:40
  21.2 33.2 %copy-start.1 = (bf16[4,32,1536]{2,1,0:T(8,128)(2,1)}, bf16[4,32,1536]{2,1,0:T(8,128)(2,1)S(1)}, u32[]{:S(2)}) copy-start(bf16[4,32,1536]{2,1,0:T(8,128)(2,1)S(1)} %pad_maximum_fusion.1.refs_0_) | copy-start | bytes 1179652
  21.2 18.9 %collective-permute-start.3 = (bf16[4,32,1536]{2,1,0:T(8,128)(2,1)S(1)}, bf16[4,32,1536]{2,1,0:T(8,128)(2,1)S(1)}, u32[]{:S(2)}, u32[]{:S(2)}) collective-permute-start(bf16[4,32,1536]{2,1,0:T(8,128)(2,1)S(1)} %pad_maximum_fusion.1.refs_0_), channel_id=1, source_target_pairs={{0,32},{32,0},{64,96},{96,64},{1,33},{33,1},{65,97},{97,65},{2,34}... | collective-permute-start | bytes 1179656 | tf_op jit(solution)/shard_map/ppermute | solution.py:40
  25.5 17.1 %collective-permute-start.4 = (bf16[4,32,1536]{2,1,0:T(8,128)(2,1)S(1)}, bf16[4,32,1536]{2,1,0:T(8,128)(2,1)S(1)}, u32[]{:S(2)}, u32[]{:S(2)}) collective-permute-start(bf16[4,32,1536]{2,1,0:T(8,128)(2,1)S(1)} %pad_maximum_fusion.1.refs_0_), channel_id=1, source_target_pairs={{0,64},{32,96},{64,0},{96,32},{1,65},{33,97},{65,1},{97,33},{2,66}... | collective-permute-start | bytes 1179656 | tf_op jit(solution)/shard_map/ppermute | solution.py:40
  26.6 27.8 %copy-start.2 = (bf16[4,64,1536]{2,1,0:T(8,128)(2,1)}, bf16[4,64,1536]{2,1,0:T(8,128)(2,1)S(1)}, u32[]{:S(2)}) copy-start(bf16[4,64,1536]{2,1,0:T(8,128)(2,1)S(1)} %pad_maximum_fusion.refs_8_) | copy-start | bytes 2359300
  26.6 58.3 %collective-permute-start.15 = (bf16[4,64,1536]{2,1,0:T(8,128)(2,1)S(1)}, bf16[4,64,1536]{2,1,0:T(8,128)(2,1)}, u32[]{:S(2)}, u32[]{:S(2)}) collective-permute-start(bf16[4,64,1536]{2,1,0:T(8,128)(2,1)S(1)} %pad_maximum_fusion.refs_8_), channel_id=1, source_target_pairs={{0,8},{8,0},{16,24},{24,16},{1,9},{9,1},{17,25},{25,17},{2,10},{10... | collective-permute-start | bytes 2359304 | tf_op jit(solution)/shard_map/ppermute | solution.py:40
  28.3 26.1 %copy-start.5 = (bf16[4,32,1536]{2,1,0:T(8,128)(2,1)}, bf16[4,32,1536]{2,1,0:T(8,128)(2,1)S(1)}, u32[]{:S(2)}) copy-start(bf16[4,32,1536]{2,1,0:T(8,128)(2,1)S(1)} %collective-permute-done.10.refs_6_) | copy-start | bytes 1179652
  28.3 56.5 %collective-permute-start.16 = (bf16[4,64,1536]{2,1,0:T(8,128)(2,1)S(1)}, bf16[4,64,1536]{2,1,0:T(8,128)(2,1)}, u32[]{:S(2)}, u32[]{:S(2)}) collective-permute-start(bf16[4,64,1536]{2,1,0:T(8,128)(2,1)S(1)} %pad_maximum_fusion.refs_8_), channel_id=1, source_target_pairs={{0,16},{8,24},{16,0},{24,8},{1,17},{9,25},{17,1},{25,9},{2,18},{10... | collective-permute-start | bytes 2359304 | tf_op jit(solution)/shard_map/ppermute | solution.py:40
  37.6 16.8 %copy-start.6 = (bf16[4,32,1536]{2,1,0:T(8,128)(2,1)}, bf16[4,32,1536]{2,1,0:T(8,128)(2,1)S(1)}, u32[]{:S(2)}) copy-start(bf16[4,32,1536]{2,1,0:T(8,128)(2,1)S(1)} %collective-permute-done.11.refs_7_) | copy-start | bytes 1179652
  37.6 47.3 %collective-permute-start.17 = (bf16[4,64,1536]{2,1,0:T(8,128)(2,1)S(1)}, bf16[4,64,1536]{2,1,0:T(8,128)(2,1)}, u32[]{:S(2)}, u32[]{:S(2)}) collective-permute-start(bf16[4,64,1536]{2,1,0:T(8,128)(2,1)S(1)} %pad_maximum_fusion.refs_8_), channel_id=1, source_target_pairs={{0,24},{8,16},{16,8},{24,0},{1,25},{9,17},{17,9},{25,1},{2,26},{10... | collective-permute-start | bytes 2359304 | tf_op jit(solution)/shard_map/ppermute | solution.py:40
  40.1 14.3 %copy-start.7 = (bf16[4,32,1536]{2,1,0:T(8,128)(2,1)}, bf16[4,32,1536]{2,1,0:T(8,128)(2,1)S(1)}, u32[]{:S(2)}) copy-start(bf16[4,32,1536]{2,1,0:T(8,128)(2,1)S(1)} %collective-permute-done.3.refs_1_) | copy-start | bytes 1179652
  40.1 14.4 %collective-permute-start.5 = (bf16[4,32,1536]{2,1,0:T(8,128)(2,1)S(1)}, bf16[4,32,1536]{2,1,0:T(8,128)(2,1)S(1)}, u32[]{:S(2)}, u32[]{:S(2)}) collective-permute-start(bf16[4,32,1536]{2,1,0:T(8,128)(2,1)S(1)} %pad_maximum_fusion.1.refs_0_), channel_id=1, source_target_pairs={{0,96},{32,64},{64,32},{96,0},{1,97},{33,65},{65,33},{97,1},{2,98}... | collective-permute-start | bytes 1179656 | tf_op jit(solution)/shard_map/ppermute | solution.py:40
  42.6 11.8 %copy-start.8 = (bf16[4,32,1536]{2,1,0:T(8,128)(2,1)}, bf16[4,32,1536]{2,1,0:T(8,128)(2,1)S(1)}, u32[]{:S(2)}) copy-start(bf16[4,32,1536]{2,1,0:T(8,128)(2,1)S(1)} %collective-permute-done.4.refs_2_) | copy-start | bytes 1179652
  42.6 26.9 %collective-permute-start.9 = (bf16[4,32,1536]{2,1,0:T(8,128)(2,1)S(1)}, bf16[4,32,1536]{2,1,0:T(8,128)(2,1)}, u32[]{:S(2)}, u32[]{:S(2)}) collective-permute-start(bf16[4,32,1536]{2,1,0:T(8,128)(2,1)S(1)} %pad_maximum_fusion.2.refs_4_), channel_id=1, source_target_pairs={{0,8},{8,0},{16,24},{24,16},{1,9},{9,1},{17,25},{25,17},{2,10},{10... | collective-permute-start | bytes 1179656 | tf_op jit(solution)/shard_map/ppermute | solution.py:40
  54.5 15.0 %copy-start.9 = (bf16[4,32,1536]{2,1,0:T(8,128)(2,1)}, bf16[4,32,1536]{2,1,0:T(8,128)(2,1)S(1)}, u32[]{:S(2)}) copy-start(bf16[4,32,1536]{2,1,0:T(8,128)(2,1)S(1)} %collective-permute-done.5.refs_3_) | copy-start | bytes 1179652
  84.9 31.4 %copy-start.15 = (bf16[4,64,1536]{2,1,0:T(8,128)(2,1)S(1)}, bf16[4,64,1536]{2,1,0:T(8,128)(2,1)}, u32[]{:S(2)}) copy-start(bf16[4,64,1536]{2,1,0:T(8,128)(2,1)} %get-tuple-element.35) | copy-start | bytes 2359300
  84.9 68.0 %copy-start.11 = (bf16[4,64,1536]{2,1,0:T(8,128)(2,1)S(1)}, bf16[4,64,1536]{2,1,0:T(8,128)(2,1)}, u32[]{:S(2)}) copy-start(bf16[4,64,1536]{2,1,0:T(8,128)(2,1)} %get-tuple-element.32) | copy-start | bytes 2359300
  109.9 47.0 %copy-start.3 = (bf16[4,512,512]{2,1,0:T(8,128)(2,1)S(1)}, bf16[4,512,512]{2,1,0:T(8,128)(2,1)}, u32[]{:S(2)}) copy-start(bf16[4,512,512]{2,1,0:T(8,128)(2,1)} %get-tuple-element.30) | copy-start | bytes 6291460
  109.9 45.1 %collective-permute-start.18 = (bf16[4,512,512]{2,1,0:T(8,128)(2,1)}, bf16[4,512,512]{2,1,0:T(8,128)(2,1)S(1)}, u32[]{:S(2)}, u32[]{:S(2)}) collective-permute-start(bf16[4,512,512]{2,1,0:T(8,128)(2,1)} %get-tuple-element.31), channel_id=1, source_target_pairs={{0,1},{1,0},{2,3},{3,2},{4,5},{5,4},{6,7},{7,6},{8,9},{9,8},{10,11... | collective-permute-start | bytes 6291464 | tf_op jit(solution)/shard_map/ppermute | solution.py:40
  112.8 20.0 %collective-permute-start.22 = (bf16[4,64,1536]{2,1,0:T(8,128)(2,1)}, bf16[4,64,1536]{2,1,0:T(8,128)(2,1)S(1)}, u32[]{:S(2)}, u32[]{:S(2)}) collective-permute-start(bf16[4,64,1536]{2,1,0:T(8,128)(2,1)} %get-tuple-element.33), channel_id=1, source_target_pairs={{0,32},{32,0},{64,96},{96,64},{1,33},{33,1},{65,97},{97,65},{2,34}... | collective-permute-start | bytes 2359304 | tf_op jit(solution)/shard_map/ppermute | solution.py:40
  114.8 36.2 %collective-permute-start.23 = (bf16[4,64,1536]{2,1,0:T(8,128)(2,1)}, bf16[4,64,1536]{2,1,0:T(8,128)(2,1)S(1)}, u32[]{:S(2)}, u32[]{:S(2)}) collective-permute-start(bf16[4,64,1536]{2,1,0:T(8,128)(2,1)} %get-tuple-element.34), channel_id=1, source_target_pairs={{0,64},{32,96},{64,0},{96,32},{1,65},{33,97},{65,1},{97,33},{2,66}... | collective-permute-start | bytes 2359304 | tf_op jit(solution)/shard_map/ppermute | solution.py:40
  116.3 36.5 %collective-permute-start.24 = (bf16[4,64,1536]{2,1,0:T(8,128)(2,1)S(1)}, bf16[4,64,1536]{2,1,0:T(8,128)(2,1)S(1)}, u32[]{:S(2)}, u32[]{:S(2)}) collective-permute-start(bf16[4,64,1536]{2,1,0:T(8,128)(2,1)S(1)} %copy-done.15), channel_id=1, source_target_pairs={{0,96},{32,64},{64,32},{96,0},{1,97},{33,65},{65,33},{97,1},{2,98}... | collective-permute-start | bytes 2359304 | tf_op jit(solution)/shard_map/ppermute | solution.py:40
  117.2 41.0 %collective-permute-start.28 = (bf16[4,64,1536]{2,1,0:T(8,128)(2,1)}, bf16[4,64,1536]{2,1,0:T(8,128)(2,1)S(1)}, u32[]{:S(2)}, u32[]{:S(2)}) collective-permute-start(bf16[4,64,1536]{2,1,0:T(8,128)(2,1)} %get-tuple-element.37), channel_id=1, source_target_pairs={{0,8},{8,0},{16,24},{24,16},{1,9},{9,1},{17,25},{25,17},{2,10},{10... | collective-permute-start | bytes 2359304 | tf_op jit(solution)/shard_map/ppermute | solution.py:40
  132.8 26.7 %collective-permute-start.29 = (bf16[4,64,1536]{2,1,0:T(8,128)(2,1)}, bf16[4,64,1536]{2,1,0:T(8,128)(2,1)S(1)}, u32[]{:S(2)}, u32[]{:S(2)}) collective-permute-start(bf16[4,64,1536]{2,1,0:T(8,128)(2,1)} %get-tuple-element.38), channel_id=1, source_target_pairs={{0,16},{8,24},{16,0},{24,8},{1,17},{9,25},{17,1},{25,9},{2,18},{10... | collective-permute-start | bytes 2359304 | tf_op jit(solution)/shard_map/ppermute | solution.py:40
  150.9 25.6 %collective-permute-start.30 = (bf16[4,64,1536]{2,1,0:T(8,128)(2,1)}, bf16[4,64,1536]{2,1,0:T(8,128)(2,1)S(1)}, u32[]{:S(2)}, u32[]{:S(2)}) collective-permute-start(bf16[4,64,1536]{2,1,0:T(8,128)(2,1)} %get-tuple-element.39), channel_id=1, source_target_pairs={{0,24},{8,16},{16,8},{24,0},{1,25},{9,17},{17,9},{25,1},{2,26},{10... | collective-permute-start | bytes 2359304 | tf_op jit(solution)/shard_map/ppermute | solution.py:40
  153.9 26.6 %collective-permute-start.25 = (bf16[64,1536]{1,0:T(8,128)(2,1)S(1)}, bf16[64,1536]{1,0:T(8,128)(2,1)S(1)}, u32[]{:S(2)}, u32[]{:S(2)}) collective-permute-start(bf16[64,1536]{1,0:T(8,128)(2,1)S(1)} %get-tuple-element.49), channel_id=1, source_target_pairs={{0,8},{8,0},{16,24},{24,16},{1,9},{9,1},{17,25},{25,17},{2,10},{10... | collective-permute-start | bytes 589832 | tf_op jit(solution)/shard_map/ppermute | solution.py:40
  155.0 25.7 %collective-permute-start.26 = (bf16[64,1536]{1,0:T(8,128)(2,1)S(1)}, bf16[64,1536]{1,0:T(8,128)(2,1)S(1)}, u32[]{:S(2)}, u32[]{:S(2)}) collective-permute-start(bf16[64,1536]{1,0:T(8,128)(2,1)S(1)} %get-tuple-element.48), channel_id=1, source_target_pairs={{0,16},{8,24},{16,0},{24,8},{1,17},{9,25},{17,1},{25,9},{2,18},{10... | collective-permute-start | bytes 589832 | tf_op jit(solution)/shard_map/ppermute | solution.py:40
  156.9 22.4 %copy-start.10 = (bf16[4,64,1536]{2,1,0:T(8,128)(2,1)S(1)}, bf16[4,64,1536]{2,1,0:T(8,128)(2,1)}, u32[]{:S(2)}) copy-start(bf16[4,64,1536]{2,1,0:T(8,128)(2,1)} %get-tuple-element.36) | copy-start | bytes 2359300
  158.2 43.5 %collective-permute-start.19 = (bf16[512,512]{1,0:T(8,128)(2,1)}, bf16[512,512]{1,0:T(8,128)(2,1)S(1)}, u32[]{:S(2)}, u32[]{:S(2)}) collective-permute-start(bf16[512,512]{1,0:T(8,128)(2,1)} %get-tuple-element.40), channel_id=1, source_target_pairs={{0,2},{2,0},{4,6},{6,4},{1,3},{3,1},{5,7},{7,5},{8,10},{10,8},{12,... | collective-permute-start | bytes 1572872 | tf_op jit(solution)/shard_map/ppermute | solution.py:40
  159.5 42.3 %collective-permute-start.20 = (bf16[512,512]{1,0:T(8,128)(2,1)S(1)}, bf16[512,512]{1,0:T(8,128)(2,1)}, u32[]{:S(2)}, u32[]{:S(2)}) collective-permute-start(bf16[512,512]{1,0:T(8,128)(2,1)S(1)} %get-tuple-element.42), channel_id=1, source_target_pairs={{0,4},{2,6},{4,0},{6,2},{1,5},{3,7},{5,1},{7,3},{8,12},{10,14},{12... | collective-permute-start | bytes 1572872 | tf_op jit(solution)/shard_map/ppermute | solution.py:40
  176.5 25.3 %collective-permute-start.21 = (bf16[512,512]{1,0:T(8,128)(2,1)S(1)}, bf16[512,512]{1,0:T(8,128)(2,1)}, u32[]{:S(2)}, u32[]{:S(2)}) collective-permute-start(bf16[512,512]{1,0:T(8,128)(2,1)S(1)} %get-tuple-element.41), channel_id=1, source_target_pairs={{0,6},{2,4},{4,2},{6,0},{1,7},{3,5},{5,3},{7,1},{8,14},{10,12},{12... | collective-permute-start | bytes 1572872 | tf_op jit(solution)/shard_map/ppermute | solution.py:40
  180.5 8.3 %copy-start.12 = (bf16[64,1536]{1,0:T(8,128)(2,1)}, bf16[64,1536]{1,0:T(8,128)(2,1)S(1)}, u32[]{:S(2)}) copy-start(bf16[64,1536]{1,0:T(8,128)(2,1)S(1)} %collective-permute-done.25.refs_1_) | copy-start | bytes 589828
  180.5 6.7 %collective-permute-start.27 = (bf16[64,1536]{1,0:T(8,128)(2,1)S(1)}, bf16[64,1536]{1,0:T(8,128)(2,1)}, u32[]{:S(2)}, u32[]{:S(2)}) collective-permute-start(bf16[64,1536]{1,0:T(8,128)(2,1)S(1)} %get-tuple-element.47), channel_id=1, source_target_pairs={{0,24},{8,16},{16,8},{24,0},{1,25},{9,17},{17,9},{25,1},{2,26},{10... | collective-permute-start | bytes 589832 | tf_op jit(solution)/shard_map/ppermute | solution.py:40
  180.7 6.6 %collective-permute-start.31 = (bf16[64,1536]{1,0:T(8,128)(2,1)S(1)}, bf16[64,1536]{1,0:T(8,128)(2,1)}, u32[]{:S(2)}, u32[]{:S(2)}) collective-permute-start(bf16[64,1536]{1,0:T(8,128)(2,1)S(1)} %get-tuple-element.45), channel_id=1, source_target_pairs={{0,32},{32,0},{64,96},{96,64},{1,33},{33,1},{65,97},{97,65},{2,34}... | collective-permute-start | bytes 589832 | tf_op jit(solution)/shard_map/ppermute | solution.py:40
  187.1 6.4 %collective-permute-start.32 = (bf16[64,1536]{1,0:T(8,128)(2,1)}, bf16[64,1536]{1,0:T(8,128)(2,1)}, u32[]{:S(2)}, u32[]{:S(2)}) collective-permute-start(bf16[64,1536]{1,0:T(8,128)(2,1)} %get-tuple-element.44), channel_id=1, source_target_pairs={{0,64},{32,96},{64,0},{96,32},{1,65},{33,97},{65,1},{97,33},{2,66}... | collective-permute-start | bytes 589832 | tf_op jit(solution)/shard_map/ppermute | solution.py:40
  187.3 12.2 %collective-permute-start.33 = (bf16[64,1536]{1,0:T(8,128)(2,1)}, bf16[64,1536]{1,0:T(8,128)(2,1)}, u32[]{:S(2)}, u32[]{:S(2)}) collective-permute-start(bf16[64,1536]{1,0:T(8,128)(2,1)} %get-tuple-element.43), channel_id=1, source_target_pairs={{0,96},{32,64},{64,32},{96,0},{1,97},{33,65},{65,33},{97,1},{2,98}... | collective-permute-start | bytes 589832 | tf_op jit(solution)/shard_map/ppermute | solution.py:40
  (2 other events, 11.2 us)

commit v3 on v2

--- a/solution.py
+++ b/solution.py
@@ -21,10 +21,10 @@
 HB = pl.BlockSpec(memory_space=pl.ANY)
 NT = (((1,), (1,)), ((), ()))
 
-GATHER_SIGMA = (("x", "z", 0, 32), ("z", "x", 32, 64))
+GATHER_SIGMA = (("x", "z", 0, 64),)
 GATHER_THETA = (("z", "x", 0, 64),)
-SCATTER_THETA = (("z", "x", 0, 64),)
-SCATTER_VAR = (("x", "z", 0, 64),)
+SCATTER_THETA = (("x", "z", 0, 64),)
+SCATTER_VAR = (("z", "x", 0, 64),)
 PLACE = {"z": 0, "x": 1, "y": 2, "core": 3}
 
 
@@ -37,7 +37,8 @@
 
 
 def sent(value, axis, step):
-    return lax.ppermute(value, axis, [(i, i ^ step) for i in range(lax.axis_size(axis))])
+    n = lax.axis_size(axis)
+    return lax.ppermute(value, axis, [(i, (i + step) % n) for i in range(n)])
 
 
 def steps_of(value, axis):
@@ -72,6 +73,22 @@
 def gather(pieces, paths):
     blocks = [jnp.stack([p] + steps_of(p, path[0])) for p, path in zip(pieces, paths)]
     return [[b] + steps_of(b, path[1]) for b, path in zip(blocks, paths)]
+
+
+def gather_relayed(piece, path):
+    one, two = path[:2]
+    block = jnp.stack([piece] + steps_of(piece, one))
+    up, down = sent(block, two, 1), sent(block, two, RING - 1)
+    far_up, far_down = sent(up[:2], two, 1), sent(down[2:], two, RING - 1)
+    return [[block, up, far_up, far_down, down]]
+
+
+def piece_at(refs, k, j):
+    if len(refs) == RING:
+        return refs[k].at[j]
+    if k == 2:
+        return refs[2 + j // 2].at[j % 2]
+    return refs[k if k < 2 else 4].at[j]
 
 
 def chunked(refs, size):
@@ -130,6 +147,7 @@
 
 
 EARLY_GROUPS, MIDDLE_GROUPS, LATE_GROUPS = 4, 2, 4
+SIGMA_PARTS = 5
 
 
 def issue(copies):
@@ -148,9 +166,9 @@
         for (one, two, lo, hi), refs in zip(paths, groups):
             for k in range(RING):
                 for j in range(RING):
-                    spot = {one: place[PLACE[one]] ^ j, two: place[PLACE[two]] ^ k}
+                    spot = {one: (place[PLACE[one]] - j) & 3, two: (place[PLACE[two]] - k) & 3}
                     pltpu.make_async_copy(
-                        refs[k].at[j, :, cols], whole.at[spot["z"], spot["x"], lo:hi, cols], sems.at[g]
+                        piece_at(refs, k, j).at[:, cols], whole.at[spot["z"], spot["x"], lo:hi, cols], sems.at[g]
                     ).start()
 
 
@@ -164,7 +182,7 @@
     for (one, two, lo, hi), refs in zip(paths, groups):
         for k in range(RING):
             for j in range(RING):
-                spot = {one: place[PLACE[one]] ^ k, two: place[PLACE[two]] ^ j}
+                spot = {one: (place[PLACE[one]] + k) & 3, two: (place[PLACE[two]] + j) & 3}
                 pltpu.make_async_copy(
                     held.at[spot["z"], spot["x"], lo:hi, cols], refs[k].at[j, :, cols], sem
                 ).start()
@@ -225,7 +243,7 @@
 
 
 def middle_kernel(rows, sq_in, sqt_in, noise_in, cot_in, *refs):
-    n_in = RING * len(GATHER_SIGMA)
+    n_in = SIGMA_PARTS
     sigma_refs, outs = refs[:n_in], refs[n_in:-14]
     gv_out, rn_out, sq, sqt, noise, cot, whole, held, gv, rn, s_sig, s_in, s_one, s_out = refs[-14:]
     place = [lax.axis_index(a) for a in ROW + COL]
@@ -234,7 +252,7 @@
     first = pltpu.make_async_copy(sq_in, sq, s_one.at[0])
     second = pltpu.make_async_copy(sqt_in, sqt, s_one.at[1])
     first.start()
-    gather_starts(place, GATHER_SIGMA, chunked(sigma_refs, RING), whole, s_sig, per, MIDDLE_GROUPS)
+    gather_starts(place, GATHER_SIGMA, [sigma_refs], whole, s_sig, per, MIDDLE_GROUPS)
 
     def loads(g):
         at = column_span(g, per)
@@ -322,7 +340,7 @@
 
 
 def late_kernel(rows, tok_in, cot_in, gv_in, rn_in, *refs):
-    n_s, n_t = RING * len(GATHER_SIGMA), RING * len(GATHER_THETA)
+    n_s, n_t = SIGMA_PARTS, RING * len(GATHER_THETA)
     sigma_refs, theta_refs = refs[:n_s], refs[n_s : n_s + n_t]
     (out_out, away_out, home_out, tok, cot, gv, rn, out, both, sigma, theta, acc, s_w, s_in, s_one, s_out) = refs[n_s + n_t :]
     place = [lax.axis_index(a) for a in ROW + COL]
@@ -342,7 +360,7 @@
 
     issue(loads(0))
     gather_starts(place, GATHER_THETA, chunked(theta_refs, RING), theta, s_w.at[0], per, LATE_GROUPS)
-    gather_starts(place, GATHER_SIGMA, chunked(sigma_refs, RING), sigma, s_w.at[1], per, LATE_GROUPS)
+    gather_starts(place, GATHER_SIGMA, [sigma_refs], sigma, s_w.at[1], per, LATE_GROUPS)
     for g in range(1, LATE_GROUPS):
         issue(loads(g))
     acc[...] = jnp.zeros_like(acc)
@@ -378,7 +396,7 @@
     ends = []
     for side, (ref, half) in enumerate(((away_out, 1 - core), (home_out, core))):
         for k in range(RING):
-            y = place[PLACE["y"]] ^ k
+            y = (place[PLACE["y"]] + k) & 3
             both[side, k] = acc[:, pl.ds(pl.multiple_of((y * 2 + half) * w, w), w)].astype(bf16)
             ends.append(pltpu.make_async_copy(both.at[side, k], ref.at[k], s_one.at[1 + side * RING + k]))
             ends[-1].start()
@@ -420,7 +438,7 @@
 def step(tokens, theta, log_sigma2, block_rows, noise, cotangent):
     own = theta.shape[1]
     sg, th = prep(log_sigma2, theta)
-    sigma_in = gather(sg, GATHER_SIGMA)
+    sigma_in = gather_relayed(sg[0], GATHER_SIGMA[0])
     theta_in = gather(th, GATHER_THETA)
     parts_theta, sq, sqt = early(block_rows, tokens, cotangent, own)
     parts_var, gv, rn = middle(block_rows, sq, sqt, noise, cotangent, sigma_in, own)
@@ -434,6 +452,7 @@
     grad_logvar = final(got_var, SCATTER_VAR, theta.shape, 0.5 * width * inv_root, log_sigma2)
     came = sent(away, "core", 1)
     pairs = [(home[k].astype(f32) + came[k].astype(f32)).astype(bf16) for k in range(RING)]
+    pairs = lax.optimization_barrier(pairs)
     arrived = steps_sent(pairs, "y")
     grad_tokens = arrived[0].astype(f32)
     for a in arrived[1:]:

time: 205 us -> 180 us (0.88)
  waiting for transfers between devices: 86.8 us -> 68 us
  starting transfers between devices: 49.3 us -> 42 us
  other arithmetic: 9.01 us -> 6.22 us
  local copies, waits for them, and re-layouts: 0.79 us -> 3.11 us
    ppermute x34 -> x29, waiting for transfers between devices: 86.8 us -> 68 us  [sent(): return lax.ppermute(value, axis, [(i, (i + step) % n) for i in range(n)])]
    ppermute x34 -> x29, starting transfers between devices: 49.3 us -> 42 us  [sent(): return lax.ppermute(value, axis, [(i, (i + step) % n) for i in range(n)])]
  transfers between devices with their start and end apart: 34 -> 29, of which waited for: 11 -> 10; matrix products, arithmetic and copies ran while one was open for 3% -> 4% of each run, Pallas kernels for 15% -> 17%
where the time goes in v3:
time: 180 us; the launch traced here: 178 us
  waiting for transfers between devices  68 us (38%)
  Pallas kernels  57.6 us (32%)
  starting transfers between devices  42 us (23%)
  other arithmetic  6.22 us (3%)
  local copies, waits for them, and re-layouts  3.11 us (2%)
    ppermute x29, waiting for transfers between devices, sent(): return lax.ppermute(value, axis, [(i, (i + step) % n) for i in range(n)])  68 us
    ppermute x29, starting transfers between devices, sent(): return lax.ppermute(value, axis, [(i, (i + step) % n) for i in range(n)])  42 us
    pallas_call x1, Pallas kernels, late(): pl.pallas_call(late_kernel, out_shape=shapes, in_specs=[SM] + [HB] * (4 +...  25.1 us
    pallas_call x1, Pallas kernels, middle(): pl.pallas_call(middle_kernel, out_shape=shapes, in_specs=[SM, HB, HB, HB,...  15.3 us
    pallas_call x1, Pallas kernels, early(): pl.pallas_call(early_kernel, out_shape=shapes, in_specs=[SM, VB, VB], out...  11 us
    pallas_call x2, Pallas kernels, final(): pl.pallas_call(final_kernel(paths, scale, ls is not None), out_shape=sds(...  4.26 us
  transfers between devices with their start and end apart: 29, of which 10 were waited for; matrix products, arithmetic and copies ran while one was open for 4% of the time, Pallas kernels for 17%

profile of v3, /device:TPU:1, one launch (start us, length us, event | category | flops | bytes accessed | tf_op | source)
XLA Modules:
  0.0 177.8 jit_solution(8130991646859603221)
XLA Ops:
  0.6 1.9 %prep.1 = (bf16[64,1536]{1,0:T(8,128)(2,1)}, bf16[64,1536]{1,0:T(8,128)(2,1)}) custom-call(f32[12,64,128]{2,1,0:T(8,128)} %refs_0_.1, bf16[12,64,128]{2,1,0:T(8,128)(2,1)} %theta_ref.1), custom_call_target="tpu_custom_call" | custom-call | tf_op jit(solution)/shard_map/prep/pallas_call | solution.py:67
  2.5 2.0 %collective-permute-start = (bf16[64,1536]{1,0:T(8,128)(2,1)}, bf16[64,1536]{1,0:T(8,128)(2,1)S(1)}, u32[]{:S(2)}, u32[]{:S(2)}) collective-permute-start(bf16[64,1536]{1,0:T(8,128)(2,1)} %get-tuple-element.27), channel_id=1, source_target_pairs={{0,8},{8,16},{16,24},{24,0},{1,9},{9,17},{17,25},{25,1},{2,10},{10... | collective-permute-start | bytes 589832 | tf_op jit(solution)/shard_map/ppermute | solution.py:41
  4.5 2.5 %collective-permute-start.1 = (bf16[64,1536]{1,0:T(8,128)(2,1)}, bf16[64,1536]{1,0:T(8,128)(2,1)S(1)}, u32[]{:S(2)}, u32[]{:S(2)}) collective-permute-start(bf16[64,1536]{1,0:T(8,128)(2,1)} %get-tuple-element.27), channel_id=1, source_target_pairs={{0,16},{8,24},{16,0},{24,8},{1,17},{9,25},{17,1},{25,9},{2,18},{10... | collective-permute-start | bytes 589832 | tf_op jit(solution)/shard_map/ppermute | solution.py:41
  7.0 1.2 collective-permute-start.2
  8.1 1.6 collective-permute-start.7
  9.8 3.3 %collective-permute-start.8 = (bf16[64,1536]{1,0:T(8,128)(2,1)}, bf16[64,1536]{1,0:T(8,128)(2,1)S(1)}, u32[]{:S(2)}, u32[]{:S(2)}) collective-permute-start(bf16[64,1536]{1,0:T(8,128)(2,1)} %get-tuple-element.30), channel_id=1, source_target_pairs={{0,64},{32,96},{64,0},{96,32},{1,65},{33,97},{65,1},{97,33},{2,66}... | collective-permute-start | bytes 589832 | tf_op jit(solution)/shard_map/ppermute | solution.py:41
  13.1 1.2 collective-permute-start.9
  14.3 1.4 collective-permute-done.1
  15.7 1.0 pad_maximum_fusion.refs_0_
  16.8 1.7 collective-permute-start.3
  18.5 2.2 %collective-permute-start.5 = (bf16[4,64,1536]{2,1,0:T(8,128)(2,1)S(1)}, bf16[4,64,1536]{2,1,0:T(8,128)(2,1)S(1)}, u32[]{:S(2)}, u32[]{:S(2)}) collective-permute-start(bf16[4,64,1536]{2,1,0:T(8,128)(2,1)S(1)} %pad_maximum_fusion.refs_0_), channel_id=1, source_target_pairs={{0,96},{32,0},{64,32},{96,64},{1,97},{33,1},{65,33},{97,65},{2,98}... | collective-permute-start | bytes 2359304 | tf_op jit(solution)/shard_map/ppermute | solution.py:41
  21.0 1.0 pad_maximum_fusion.1.refs_5_
  22.0 1.2 collective-permute-start.10
  23.2 2.5 %collective-permute-start.11 = (bf16[4,64,1536]{2,1,0:T(8,128)(2,1)S(1)}, bf16[4,64,1536]{2,1,0:T(8,128)(2,1)}, u32[]{:S(2)}, u32[]{:S(2)}) collective-permute-start(bf16[4,64,1536]{2,1,0:T(8,128)(2,1)S(1)} %pad_maximum_fusion.1.refs_5_), channel_id=1, source_target_pairs={{0,16},{8,24},{16,0},{24,8},{1,17},{9,25},{17,1},{25,9},{2,18},{10... | collective-permute-start | bytes 2359304 | tf_op jit(solution)/shard_map/ppermute | solution.py:41
  26.0 13.3 %collective-permute-done.3.refs_1_ = bf16[4,64,1536]{2,1,0:T(8,128)(2,1)S(1)} collective-permute-done((bf16[4,64,1536]{2,1,0:T(8,128)(2,1)S(1)}, bf16[4,64,1536]{2,1,0:T(8,128)(2,1)S(1)}, u32[]{:S(2)}, u32[]{:S(2)}) %collective-permute-start.3) | collective-permute-done | bytes 786464 | tf_op jit(solution)/shard_map/ppermute | solution.py:41
  39.3 0.8 slice.168
  40.1 0.8 slice.169
  41.0 2.7 %collective-permute-start.6 = (bf16[2,64,1536]{2,1,0:T(8,128)(2,1)}, bf16[2,64,1536]{2,1,0:T(8,128)(2,1)}, u32[]{:S(2)}, u32[]{:S(2)}) collective-permute-start(bf16[2,64,1536]{2,1,0:T(8,128)(2,1)} %slice.169), channel_id=1, source_target_pairs={{0,96},{32,0},{64,32},{96,64},{1,97},{33,1},{65,33},{97,65},{2,98}... | collective-permute-start | bytes 1179656 | tf_op jit(solution)/shard_map/ppermute | solution.py:41
  43.6 0.7 copy.12.rows
  44.3 11.0 %early.1 = (bf16[4,64,1536]{2,1,0:T(8,128)(2,1)}, bf16[4,64,1536]{2,1,0:T(8,128)(2,1)}, bf16[4,64,1536]{2,1,0:T(8,128)(2,1)}, bf16[4,64,1536]{2,1,0:T(8,128)(2,1...) custom-call(s32[12,8]{1,0:T(8,128)} %copy.12.rows, bf16[512,4096]{1,0:T(8,128)(2,1)} %tok_in.1, ...), custom_call_target="tpu_custom_call" | custom-call | tf_op jit(solution)/shard_map/early/pallas_call | solution.py:227
  55.4 0.7 copy-done.5
  56.1 15.3 %middle.1 = (bf16[4,64,1536]{2,1,0:T(8,128)(2,1)}, bf16[4,64,1536]{2,1,0:T(8,128)(2,1)}, bf16[4,64,1536]{2,1,0:T(8,128)(2,1)}, bf16[4,64,1536]{2,1,0:T(8,128)(2,...) custom-call(s32[12,8]{1,0:T(8,128)} %copy.12.rows, bf16[512,4096]{1,0:T(8,128)(2,1)} %get-tuple-element.25.sq_in, ...), custom_call_target="tpu_custom_call" | custom-call | tf_op jit(solution)/shard_map/middle/pallas_call | solution.py:317
  71.5 25.1 %late.1 = (bf16[512,1536]{1,0:T(8,128)(2,1)}, bf16[4,512,512]{2,1,0:T(8,128)(2,1)}, bf16[4,512,512]{2,1,0:T(8,128)(2,1)}) custom-call(s32[12,8]{1,0:T(8,128)} %copy.12.rows, bf16[512,4096]{1,0:T(8,128)(2,1)} %tok_in.1, bf16[512,1536]{1,0:T(8,128)(2,1)} %cot_in.3, bf16[512,1536]{1,0:T(8,128)(2,1)} %get-tuple-element.28.gv_in, ...), custom_call_target="tpu_custom_call" | custom-call | tf_op jit(solution)/shard_map/late/pallas_call | solution.py:413
  96.7 1.5 collective-permute-start.13
  98.2 0.3 collective-permute-start.17
  98.5 2.5 %collective-permute-start.18 = (bf16[4,64,1536]{2,1,0:T(8,128)(2,1)S(1)}, bf16[4,64,1536]{2,1,0:T(8,128)(2,1)S(1)}, u32[]{:S(2)}, u32[]{:S(2)}) collective-permute-start(bf16[4,64,1536]{2,1,0:T(8,128)(2,1)S(1)} %copy-done.13), channel_id=1, source_target_pairs={{0,16},{8,24},{16,0},{24,8},{1,17},{9,25},{17,1},{25,9},{2,18},{10... | collective-permute-start | bytes 2359304 | tf_op jit(solution)/shard_map/ppermute | solution.py:41
  101.0 0.3 collective-permute-start.19
  101.3 17.3 %collective-permute-done.17 = bf16[4,64,1536]{2,1,0:T(8,128)(2,1)S(1)} collective-permute-done((bf16[4,64,1536]{2,1,0:T(8,128)(2,1)}, bf16[4,64,1536]{2,1,0:T(8,128)(2,1)S(1)}, u32[]{:S(2)}, u32[]{:S(2)}) %collective-permute-start.17) | collective-permute-done | bytes 786464 | tf_op jit(solution)/shard_map/ppermute | solution.py:41
  118.6 17.0 %collective-permute-done.18 = bf16[4,64,1536]{2,1,0:T(8,128)(2,1)S(1)} collective-permute-done((bf16[4,64,1536]{2,1,0:T(8,128)(2,1)S(1)}, bf16[4,64,1536]{2,1,0:T(8,128)(2,1)S(1)}, u32[]{:S(2)}, u32[]{:S(2)}) %collective-permute-start.18) | collective-permute-done | bytes 786464 | tf_op jit(solution)/shard_map/ppermute | solution.py:41
  135.9 1.1 fusion.7
  137.0 1.2 collective-permute-start.20
  138.3 0.7 fusion.3
  139.0 1.3 collective-permute-start.14
  140.3 2.7 %collective-permute-start.15 = (bf16[512,512]{1,0:T(8,128)(2,1)S(1)}, bf16[512,512]{1,0:T(8,128)(2,1)S(1)}, u32[]{:S(2)}, u32[]{:S(2)}) collective-permute-start(bf16[512,512]{1,0:T(8,128)(2,1)S(1)} %get-tuple-element.36), channel_id=1, source_target_pairs={{0,4},{2,6},{4,0},{6,2},{1,5},{3,7},{5,1},{7,3},{8,12},{10,14},{12... | collective-permute-start | bytes 1572872 | tf_op jit(solution)/shard_map/ppermute | solution.py:41
  143.0 11.0 %collective-permute-done.25 = bf16[4,64,1536]{2,1,0:T(8,128)(2,1)S(1)} collective-permute-done((bf16[4,64,1536]{2,1,0:T(8,128)(2,1)}, bf16[4,64,1536]{2,1,0:T(8,128)(2,1)S(1)}, u32[]{:S(2)}, u32[]{:S(2)}) %collective-permute-start.25) | collective-permute-done | bytes 786464 | tf_op jit(solution)/shard_map/ppermute | solution.py:41
  154.0 2.7 %collective-permute-start.16 = (bf16[512,512]{1,0:T(8,128)(2,1)S(1)}, bf16[512,512]{1,0:T(8,128)(2,1)S(1)}, u32[]{:S(2)}, u32[]{:S(2)}) collective-permute-start(bf16[512,512]{1,0:T(8,128)(2,1)S(1)} %get-tuple-element.37), channel_id=1, source_target_pairs={{0,6},{2,0},{4,2},{6,4},{1,7},{3,1},{5,3},{7,5},{8,14},{10,8},{12,... | collective-permute-start | bytes 1572872 | tf_op jit(solution)/shard_map/ppermute | solution.py:41
  156.8 1.2 fusion.11
  157.9 1.5 collective-permute-start.22
  159.4 2.1 %collective-permute-start.26 = (bf16[64,1536]{1,0:T(8,128)(2,1)S(1)}, bf16[64,1536]{1,0:T(8,128)(2,1)}, u32[]{:S(2)}, u32[]{:S(2)}) collective-permute-start(bf16[64,1536]{1,0:T(8,128)(2,1)S(1)} %get-tuple-element.52), channel_id=1, source_target_pairs={{0,8},{8,16},{16,24},{24,0},{1,9},{9,17},{17,25},{25,1},{2,10},{10... | collective-permute-start | bytes 589832 | tf_op jit(solution)/shard_map/ppermute | solution.py:41
  161.5 1.5 collective-permute-done.22.refs_3_
  163.0 1.0 collective-permute-start.27
  164.0 2.2 %collective-permute-done.26.refs_2_ = bf16[64,1536]{1,0:T(8,128)(2,1)} collective-permute-done((bf16[64,1536]{1,0:T(8,128)(2,1)S(1)}, bf16[64,1536]{1,0:T(8,128)(2,1)}, u32[]{:S(2)}, u32[]{:S(2)}) %collective-permute-start.26) | collective-permute-done | bytes 196640 | tf_op jit(solution)/shard_map/ppermute | solution.py:41
  166.2 2.1 %collective-permute-start.28 = (bf16[64,1536]{1,0:T(8,128)(2,1)}, bf16[64,1536]{1,0:T(8,128)(2,1)}, u32[]{:S(2)}, u32[]{:S(2)}) collective-permute-start(bf16[64,1536]{1,0:T(8,128)(2,1)} %get-tuple-element.50), channel_id=1, source_target_pairs={{0,24},{8,0},{16,8},{24,16},{1,25},{9,1},{17,9},{25,17},{2,26},{10... | collective-permute-start | bytes 589832 | tf_op jit(solution)/shard_map/ppermute | solution.py:41
  168.3 2.1 %shard_map.93 = f32[12,64,128]{2,1,0:T(8,128)} custom-call(bf16[64,1536]{1,0:T(8,128)(2,1)} %get-tuple-element.57.refs_0_, bf16[64,1536]{1,0:T(8,128)(2,1)} %copy-done.8, bf16[64,1536]{1,0:T(8,128)(2,1)} %copy-done.9, bf16[64,1536]{1,0:T(8,128)(2,1)} %collective-permute-done.22.refs_3_), custom_call_target="tpu_custom_call" | custom-call | tf_op jit(solution)/shard_map/pallas_call | solution.py:144
  170.4 1.1 collective-permute-done.27.refs_3_
  171.4 2.9 %collective-permute-done.28.refs_4_ = bf16[64,1536]{1,0:T(8,128)(2,1)} collective-permute-done((bf16[64,1536]{1,0:T(8,128)(2,1)}, bf16[64,1536]{1,0:T(8,128)(2,1)}, u32[]{:S(2)}, u32[]{:S(2)}) %collective-permute-start.28) | collective-permute-done | bytes 196640 | tf_op jit(solution)/shard_map/ppermute | solution.py:41
  174.3 2.2 %shard_map.94 = f32[12,64,128]{2,1,0:T(8,128)} custom-call(f32[12,64,128]{2,1,0:T(8,128)} %refs_0_.1, bf16[64,1536]{1,0:T(8,128)(2,1)} %get-tuple-element.53.refs_1_, bf16[64,1536]{1,0:T(8,128)(2,1)} %collective-permute-done.26.refs_2_, bf16[64,1536]{1,0:T(8,128)(2,1)} %collective-permute-done.27.refs_3_, bf16[64,1536]{1,0:T(8,128)(2,1)} %collective-permute-done.28.refs_4_), custom_call_target="tpu_custom_call" | custom-call | tf_op jit(solution)/shard_map/pallas_call | solution.py:144
  176.5 1.2 convert_add_fusion
  (53 shorter events, 1.0 us)
Async XLA Ops:
  2.5 10.6 %collective-permute-start = (bf16[64,1536]{1,0:T(8,128)(2,1)}, bf16[64,1536]{1,0:T(8,128)(2,1)S(1)}, u32[]{:S(2)}, u32[]{:S(2)}) collective-permute-start(bf16[64,1536]{1,0:T(8,128)(2,1)} %get-tuple-element.27), channel_id=1, source_target_pairs={{0,8},{8,16},{16,24},{24,0},{1,9},{9,17},{17,25},{25,1},{2,10},{10... | collective-permute-start | bytes 589832 | tf_op jit(solution)/shard_map/ppermute | solution.py:41
  4.5 11.2 %collective-permute-start.1 = (bf16[64,1536]{1,0:T(8,128)(2,1)}, bf16[64,1536]{1,0:T(8,128)(2,1)S(1)}, u32[]{:S(2)}, u32[]{:S(2)}) collective-permute-start(bf16[64,1536]{1,0:T(8,128)(2,1)} %get-tuple-element.27), channel_id=1, source_target_pairs={{0,16},{8,24},{16,0},{24,8},{1,17},{9,25},{17,1},{25,9},{2,18},{10... | collective-permute-start | bytes 589832 | tf_op jit(solution)/shard_map/ppermute | solution.py:41
  7.0 8.7 %collective-permute-start.2 = (bf16[64,1536]{1,0:T(8,128)(2,1)}, bf16[64,1536]{1,0:T(8,128)(2,1)S(1)}, u32[]{:S(2)}, u32[]{:S(2)}) collective-permute-start(bf16[64,1536]{1,0:T(8,128)(2,1)} %get-tuple-element.27), channel_id=1, source_target_pairs={{0,24},{8,0},{16,8},{24,16},{1,25},{9,1},{17,9},{25,17},{2,26},{10... | collective-permute-start | bytes 589832 | tf_op jit(solution)/shard_map/ppermute | solution.py:41
  8.1 12.6 %collective-permute-start.7 = (bf16[64,1536]{1,0:T(8,128)(2,1)}, bf16[64,1536]{1,0:T(8,128)(2,1)S(1)}, u32[]{:S(2)}, u32[]{:S(2)}) collective-permute-start(bf16[64,1536]{1,0:T(8,128)(2,1)} %get-tuple-element.30), channel_id=1, source_target_pairs={{0,32},{32,64},{64,96},{96,0},{1,33},{33,65},{65,97},{97,1},{2,34}... | collective-permute-start | bytes 589832 | tf_op jit(solution)/shard_map/ppermute | solution.py:41
  9.8 11.2 %collective-permute-start.8 = (bf16[64,1536]{1,0:T(8,128)(2,1)}, bf16[64,1536]{1,0:T(8,128)(2,1)S(1)}, u32[]{:S(2)}, u32[]{:S(2)}) collective-permute-start(bf16[64,1536]{1,0:T(8,128)(2,1)} %get-tuple-element.30), channel_id=1, source_target_pairs={{0,64},{32,96},{64,0},{96,32},{1,65},{33,97},{65,1},{97,33},{2,66}... | collective-permute-start | bytes 589832 | tf_op jit(solution)/shard_map/ppermute | solution.py:41
  13.1 7.9 %collective-permute-start.9 = (bf16[64,1536]{1,0:T(8,128)(2,1)}, bf16[64,1536]{1,0:T(8,128)(2,1)S(1)}, u32[]{:S(2)}, u32[]{:S(2)}) collective-permute-start(bf16[64,1536]{1,0:T(8,128)(2,1)} %get-tuple-element.30), channel_id=1, source_target_pairs={{0,96},{32,0},{64,32},{96,64},{1,97},{33,1},{65,33},{97,65},{2,98}... | collective-permute-start | bytes 589832 | tf_op jit(solution)/shard_map/ppermute | solution.py:41
  15.7 27.9 %copy-start.10 = (s32[12,8]{0,1:T(8,128)S(1)}, s32[12,8]{0,1:T(8,128)}, u32[]{:S(2)}) copy-start(s32[12,8]{0,1:T(8,128)} %param.9) | copy-start | bytes 1156
  16.8 38.6 %copy-start = (bf16[4,64,1536]{2,1,0:T(8,128)(2,1)}, bf16[4,64,1536]{2,1,0:T(8,128)(2,1)S(1)}, u32[]{:S(2)}) copy-start(bf16[4,64,1536]{2,1,0:T(8,128)(2,1)S(1)} %pad_maximum_fusion.refs_0_) | copy-start | bytes 2359300
  16.8 22.5 %collective-permute-start.3 = (bf16[4,64,1536]{2,1,0:T(8,128)(2,1)S(1)}, bf16[4,64,1536]{2,1,0:T(8,128)(2,1)S(1)}, u32[]{:S(2)}, u32[]{:S(2)}) collective-permute-start(bf16[4,64,1536]{2,1,0:T(8,128)(2,1)S(1)} %pad_maximum_fusion.refs_0_), channel_id=1, source_target_pairs={{0,32},{32,64},{64,96},{96,0},{1,33},{33,65},{65,97},{97,1},{2,34}... | collective-permute-start | bytes 2359304 | tf_op jit(solution)/shard_map/ppermute | solution.py:41
  18.5 21.6 %collective-permute-start.5 = (bf16[4,64,1536]{2,1,0:T(8,128)(2,1)S(1)}, bf16[4,64,1536]{2,1,0:T(8,128)(2,1)S(1)}, u32[]{:S(2)}, u32[]{:S(2)}) collective-permute-start(bf16[4,64,1536]{2,1,0:T(8,128)(2,1)S(1)} %pad_maximum_fusion.refs_0_), channel_id=1, source_target_pairs={{0,96},{32,0},{64,32},{96,64},{1,97},{33,1},{65,33},{97,65},{2,98}... | collective-permute-start | bytes 2359304 | tf_op jit(solution)/shard_map/ppermute | solution.py:41
  22.0 33.3 %copy-start.3 = (bf16[4,64,1536]{2,1,0:T(8,128)(2,1)}, bf16[4,64,1536]{2,1,0:T(8,128)(2,1)S(1)}, u32[]{:S(2)}) copy-start(bf16[4,64,1536]{2,1,0:T(8,128)(2,1)S(1)} %pad_maximum_fusion.1.refs_5_) | copy-start | bytes 2359300
  22.0 49.4 %collective-permute-start.10 = (bf16[4,64,1536]{2,1,0:T(8,128)(2,1)S(1)}, bf16[4,64,1536]{2,1,0:T(8,128)(2,1)}, u32[]{:S(2)}, u32[]{:S(2)}) collective-permute-start(bf16[4,64,1536]{2,1,0:T(8,128)(2,1)S(1)} %pad_maximum_fusion.1.refs_5_), channel_id=1, source_target_pairs={{0,8},{8,16},{16,24},{24,0},{1,9},{9,17},{17,25},{25,1},{2,10},{10... | collective-permute-start | bytes 2359304 | tf_op jit(solution)/shard_map/ppermute | solution.py:41
  23.2 48.2 %collective-permute-start.11 = (bf16[4,64,1536]{2,1,0:T(8,128)(2,1)S(1)}, bf16[4,64,1536]{2,1,0:T(8,128)(2,1)}, u32[]{:S(2)}, u32[]{:S(2)}) collective-permute-start(bf16[4,64,1536]{2,1,0:T(8,128)(2,1)S(1)} %pad_maximum_fusion.1.refs_5_), channel_id=1, source_target_pairs={{0,16},{8,24},{16,0},{24,8},{1,17},{9,25},{17,1},{25,9},{2,18},{10... | collective-permute-start | bytes 2359304 | tf_op jit(solution)/shard_map/ppermute | solution.py:41
  25.7 45.7 %collective-permute-start.12 = (bf16[4,64,1536]{2,1,0:T(8,128)(2,1)S(1)}, bf16[4,64,1536]{2,1,0:T(8,128)(2,1)}, u32[]{:S(2)}, u32[]{:S(2)}) collective-permute-start(bf16[4,64,1536]{2,1,0:T(8,128)(2,1)S(1)} %pad_maximum_fusion.1.refs_5_), channel_id=1, source_target_pairs={{0,24},{8,0},{16,8},{24,16},{1,25},{9,1},{17,9},{25,17},{2,26},{10... | collective-permute-start | bytes 2359304 | tf_op jit(solution)/shard_map/ppermute | solution.py:41
  39.3 16.1 %copy-start.1 = (bf16[4,64,1536]{2,1,0:T(8,128)(2,1)}, bf16[4,64,1536]{2,1,0:T(8,128)(2,1)S(1)}, u32[]{:S(2)}) copy-start(bf16[4,64,1536]{2,1,0:T(8,128)(2,1)S(1)} %collective-permute-done.3.refs_1_) | copy-start | bytes 2359300
  40.1 15.2 %collective-permute-start.4 = (bf16[2,64,1536]{2,1,0:T(8,128)(2,1)}, bf16[2,64,1536]{2,1,0:T(8,128)(2,1)S(1)}, u32[]{:S(2)}, u32[]{:S(2)}) collective-permute-start(bf16[2,64,1536]{2,1,0:T(8,128)(2,1)} %slice.168), channel_id=1, source_target_pairs={{0,32},{32,64},{64,96},{96,0},{1,33},{33,65},{65,97},{97,1},{2,34}... | collective-permute-start | bytes 1179656 | tf_op jit(solution)/shard_map/ppermute | solution.py:41
  40.1 15.2 %copy-start.2 = (bf16[4,64,1536]{2,1,0:T(8,128)(2,1)}, bf16[4,64,1536]{2,1,0:T(8,128)(2,1)S(1)}, u32[]{:S(2)}) copy-start(bf16[4,64,1536]{2,1,0:T(8,128)(2,1)S(1)} %collective-permute-done.5.refs_4_) | copy-start | bytes 2359300
  41.0 14.4 %collective-permute-start.6 = (bf16[2,64,1536]{2,1,0:T(8,128)(2,1)}, bf16[2,64,1536]{2,1,0:T(8,128)(2,1)}, u32[]{:S(2)}, u32[]{:S(2)}) collective-permute-start(bf16[2,64,1536]{2,1,0:T(8,128)(2,1)} %slice.169), channel_id=1, source_target_pairs={{0,96},{32,0},{64,32},{96,64},{1,97},{33,1},{65,33},{97,65},{2,98}... | collective-permute-start | bytes 1179656 | tf_op jit(solution)/shard_map/ppermute | solution.py:41
  55.4 0.7 copy-start.5
  71.5 27.1 %copy-start.13 = (bf16[4,64,1536]{2,1,0:T(8,128)(2,1)S(1)}, bf16[4,64,1536]{2,1,0:T(8,128)(2,1)}, u32[]{:S(2)}) copy-start(bf16[4,64,1536]{2,1,0:T(8,128)(2,1)} %get-tuple-element.40) | copy-start | bytes 2359300
  71.5 29.6 %copy-start.12 = (bf16[4,64,1536]{2,1,0:T(8,128)(2,1)S(1)}, bf16[4,64,1536]{2,1,0:T(8,128)(2,1)}, u32[]{:S(2)}) copy-start(bf16[4,64,1536]{2,1,0:T(8,128)(2,1)} %get-tuple-element.41) | copy-start | bytes 2359300
  71.5 47.2 %copy-start.11 = (bf16[4,64,1536]{2,1,0:T(8,128)(2,1)S(1)}, bf16[4,64,1536]{2,1,0:T(8,128)(2,1)}, u32[]{:S(2)}) copy-start(bf16[4,64,1536]{2,1,0:T(8,128)(2,1)} %get-tuple-element.44) | copy-start | bytes 2359300
  71.5 64.4 %copy-start.7 = (bf16[4,64,1536]{2,1,0:T(8,128)(2,1)S(1)}, bf16[4,64,1536]{2,1,0:T(8,128)(2,1)}, u32[]{:S(2)}) copy-start(bf16[4,64,1536]{2,1,0:T(8,128)(2,1)} %get-tuple-element.38) | copy-start | bytes 2359300
  96.7 41.6 %copy-start.4 = (bf16[4,512,512]{2,1,0:T(8,128)(2,1)S(1)}, bf16[4,512,512]{2,1,0:T(8,128)(2,1)}, u32[]{:S(2)}) copy-start(bf16[4,512,512]{2,1,0:T(8,128)(2,1)} %get-tuple-element.32) | copy-start | bytes 6291460
  96.7 41.5 %collective-permute-start.13 = (bf16[4,512,512]{2,1,0:T(8,128)(2,1)}, bf16[4,512,512]{2,1,0:T(8,128)(2,1)S(1)}, u32[]{:S(2)}, u32[]{:S(2)}) collective-permute-start(bf16[4,512,512]{2,1,0:T(8,128)(2,1)} %get-tuple-element.33), channel_id=1, source_target_pairs={{0,1},{1,0},{2,3},{3,2},{4,5},{5,4},{6,7},{7,6},{8,9},{9,8},{10,11... | collective-permute-start | bytes 6291464 | tf_op jit(solution)/shard_map/ppermute | solution.py:41
  98.2 20.4 %collective-permute-start.17 = (bf16[4,64,1536]{2,1,0:T(8,128)(2,1)}, bf16[4,64,1536]{2,1,0:T(8,128)(2,1)S(1)}, u32[]{:S(2)}, u32[]{:S(2)}) collective-permute-start(bf16[4,64,1536]{2,1,0:T(8,128)(2,1)} %get-tuple-element.39), channel_id=1, source_target_pairs={{0,8},{8,16},{16,24},{24,0},{1,9},{9,17},{17,25},{25,1},{2,10},{10... | collective-permute-start | bytes 2359304 | tf_op jit(solution)/shard_map/ppermute | solution.py:41
  98.5 37.1 %collective-permute-start.18 = (bf16[4,64,1536]{2,1,0:T(8,128)(2,1)S(1)}, bf16[4,64,1536]{2,1,0:T(8,128)(2,1)S(1)}, u32[]{:S(2)}, u32[]{:S(2)}) collective-permute-start(bf16[4,64,1536]{2,1,0:T(8,128)(2,1)S(1)} %copy-done.13), channel_id=1, source_target_pairs={{0,16},{8,24},{16,0},{24,8},{1,17},{9,25},{17,1},{25,9},{2,18},{10... | collective-permute-start | bytes 2359304 | tf_op jit(solution)/shard_map/ppermute | solution.py:41
  101.0 34.9 %collective-permute-start.19 = (bf16[4,64,1536]{2,1,0:T(8,128)(2,1)S(1)}, bf16[4,64,1536]{2,1,0:T(8,128)(2,1)S(1)}, u32[]{:S(2)}, u32[]{:S(2)}) collective-permute-start(bf16[4,64,1536]{2,1,0:T(8,128)(2,1)S(1)} %copy-done.12), channel_id=1, source_target_pairs={{0,24},{8,0},{16,8},{24,16},{1,25},{9,1},{17,9},{25,17},{2,26},{10... | collective-permute-start | bytes 2359304 | tf_op jit(solution)/shard_map/ppermute | solution.py:41
  101.3 37.7 %collective-permute-start.23 = (bf16[4,64,1536]{2,1,0:T(8,128)(2,1)}, bf16[4,64,1536]{2,1,0:T(8,128)(2,1)S(1)}, u32[]{:S(2)}, u32[]{:S(2)}) collective-permute-start(bf16[4,64,1536]{2,1,0:T(8,128)(2,1)} %get-tuple-element.43), channel_id=1, source_target_pairs={{0,32},{32,64},{64,96},{96,0},{1,33},{33,65},{65,97},{97,1},{2,34}... | collective-permute-start | bytes 2359304 | tf_op jit(solution)/shard_map/ppermute | solution.py:41
  118.6 21.7 %collective-permute-start.24 = (bf16[4,64,1536]{2,1,0:T(8,128)(2,1)S(1)}, bf16[4,64,1536]{2,1,0:T(8,128)(2,1)S(1)}, u32[]{:S(2)}, u32[]{:S(2)}) collective-permute-start(bf16[4,64,1536]{2,1,0:T(8,128)(2,1)S(1)} %copy-done.11), channel_id=1, source_target_pairs={{0,64},{32,96},{64,0},{96,32},{1,65},{33,97},{65,1},{97,33},{2,66}... | collective-permute-start | bytes 2359304 | tf_op jit(solution)/shard_map/ppermute | solution.py:41
  135.6 18.4 %collective-permute-start.25 = (bf16[4,64,1536]{2,1,0:T(8,128)(2,1)}, bf16[4,64,1536]{2,1,0:T(8,128)(2,1)S(1)}, u32[]{:S(2)}, u32[]{:S(2)}) collective-permute-start(bf16[4,64,1536]{2,1,0:T(8,128)(2,1)} %get-tuple-element.45), channel_id=1, source_target_pairs={{0,96},{32,0},{64,32},{96,64},{1,97},{33,1},{65,33},{97,65},{2,98}... | collective-permute-start | bytes 2359304 | tf_op jit(solution)/shard_map/ppermute | solution.py:41
  137.0 21.0 %collective-permute-start.20 = (bf16[64,1536]{1,0:T(8,128)(2,1)S(1)}, bf16[64,1536]{1,0:T(8,128)(2,1)S(1)}, u32[]{:S(2)}, u32[]{:S(2)}) collective-permute-start(bf16[64,1536]{1,0:T(8,128)(2,1)S(1)} %get-tuple-element.56), channel_id=1, source_target_pairs={{0,32},{32,64},{64,96},{96,0},{1,33},{33,65},{65,97},{97,1},{2,34}... | collective-permute-start | bytes 589832 | tf_op jit(solution)/shard_map/ppermute | solution.py:41
  138.2 21.2 %collective-permute-start.21 = (bf16[64,1536]{1,0:T(8,128)(2,1)S(1)}, bf16[64,1536]{1,0:T(8,128)(2,1)S(1)}, u32[]{:S(2)}, u32[]{:S(2)}) collective-permute-start(bf16[64,1536]{1,0:T(8,128)(2,1)S(1)} %get-tuple-element.55), channel_id=1, source_target_pairs={{0,64},{32,96},{64,0},{96,32},{1,65},{33,97},{65,1},{97,33},{2,66}... | collective-permute-start | bytes 589832 | tf_op jit(solution)/shard_map/ppermute | solution.py:41
  138.3 18.5 %copy-start.6 = (bf16[4,64,1536]{2,1,0:T(8,128)(2,1)S(1)}, bf16[4,64,1536]{2,1,0:T(8,128)(2,1)}, u32[]{:S(2)}) copy-start(bf16[4,64,1536]{2,1,0:T(8,128)(2,1)} %get-tuple-element.42) | copy-start | bytes 2359300
  139.0 37.5 %collective-permute-start.14 = (bf16[512,512]{1,0:T(8,128)(2,1)S(1)}, bf16[512,512]{1,0:T(8,128)(2,1)S(1)}, u32[]{:S(2)}, u32[]{:S(2)}) collective-permute-start(bf16[512,512]{1,0:T(8,128)(2,1)S(1)} %get-tuple-element.35), channel_id=1, source_target_pairs={{0,2},{2,4},{4,6},{6,0},{1,3},{3,5},{5,7},{7,1},{8,10},{10,12},{12... | collective-permute-start | bytes 1572872 | tf_op jit(solution)/shard_map/ppermute | solution.py:41
  140.3 36.2 %collective-permute-start.15 = (bf16[512,512]{1,0:T(8,128)(2,1)S(1)}, bf16[512,512]{1,0:T(8,128)(2,1)S(1)}, u32[]{:S(2)}, u32[]{:S(2)}) collective-permute-start(bf16[512,512]{1,0:T(8,128)(2,1)S(1)} %get-tuple-element.36), channel_id=1, source_target_pairs={{0,4},{2,6},{4,0},{6,2},{1,5},{3,7},{5,1},{7,3},{8,12},{10,14},{12... | collective-permute-start | bytes 1572872 | tf_op jit(solution)/shard_map/ppermute | solution.py:41
  154.0 22.5 %collective-permute-start.16 = (bf16[512,512]{1,0:T(8,128)(2,1)S(1)}, bf16[512,512]{1,0:T(8,128)(2,1)S(1)}, u32[]{:S(2)}, u32[]{:S(2)}) collective-permute-start(bf16[512,512]{1,0:T(8,128)(2,1)S(1)} %get-tuple-element.37), channel_id=1, source_target_pairs={{0,6},{2,0},{4,2},{6,4},{1,7},{3,1},{5,3},{7,5},{8,14},{10,8},{12,... | collective-permute-start | bytes 1572872 | tf_op jit(solution)/shard_map/ppermute | solution.py:41
  157.9 10.3 %copy-start.8 = (bf16[64,1536]{1,0:T(8,128)(2,1)}, bf16[64,1536]{1,0:T(8,128)(2,1)S(1)}, u32[]{:S(2)}) copy-start(bf16[64,1536]{1,0:T(8,128)(2,1)S(1)} %collective-permute-done.20.refs_1_) | copy-start | bytes 589828
  157.9 5.1 %collective-permute-start.22 = (bf16[64,1536]{1,0:T(8,128)(2,1)S(1)}, bf16[64,1536]{1,0:T(8,128)(2,1)}, u32[]{:S(2)}, u32[]{:S(2)}) collective-permute-start(bf16[64,1536]{1,0:T(8,128)(2,1)S(1)} %get-tuple-element.54), channel_id=1, source_target_pairs={{0,96},{32,0},{64,32},{96,64},{1,97},{33,1},{65,33},{97,65},{2,98}... | collective-permute-start | bytes 589832 | tf_op jit(solution)/shard_map/ppermute | solution.py:41
  159.4 8.9 %copy-start.9 = (bf16[64,1536]{1,0:T(8,128)(2,1)}, bf16[64,1536]{1,0:T(8,128)(2,1)S(1)}, u32[]{:S(2)}) copy-start(bf16[64,1536]{1,0:T(8,128)(2,1)S(1)} %collective-permute-done.21.refs_2_) | copy-start | bytes 589828
  159.4 6.8 %collective-permute-start.26 = (bf16[64,1536]{1,0:T(8,128)(2,1)S(1)}, bf16[64,1536]{1,0:T(8,128)(2,1)}, u32[]{:S(2)}, u32[]{:S(2)}) collective-permute-start(bf16[64,1536]{1,0:T(8,128)(2,1)S(1)} %get-tuple-element.52), channel_id=1, source_target_pairs={{0,8},{8,16},{16,24},{24,0},{1,9},{9,17},{17,25},{25,1},{2,10},{10... | collective-permute-start | bytes 589832 | tf_op jit(solution)/shard_map/ppermute | solution.py:41
  163.0 8.4 %collective-permute-start.27 = (bf16[64,1536]{1,0:T(8,128)(2,1)}, bf16[64,1536]{1,0:T(8,128)(2,1)}, u32[]{:S(2)}, u32[]{:S(2)}) collective-permute-start(bf16[64,1536]{1,0:T(8,128)(2,1)} %get-tuple-element.51), channel_id=1, source_target_pairs={{0,16},{8,24},{16,0},{24,8},{1,17},{9,25},{17,1},{25,9},{2,18},{10... | collective-permute-start | bytes 589832 | tf_op jit(solution)/shard_map/ppermute | solution.py:41
  166.2 8.1 %collective-permute-start.28 = (bf16[64,1536]{1,0:T(8,128)(2,1)}, bf16[64,1536]{1,0:T(8,128)(2,1)}, u32[]{:S(2)}, u32[]{:S(2)}) collective-permute-start(bf16[64,1536]{1,0:T(8,128)(2,1)} %get-tuple-element.50), channel_id=1, source_target_pairs={{0,24},{8,0},{16,8},{24,16},{1,25},{9,1},{17,9},{25,17},{2,26},{10... | collective-permute-start | bytes 589832 | tf_op jit(solution)/shard_map/ppermute | solution.py:41

commit v4 on v3

--- a/solution.py
+++ b/solution.py
@@ -21,10 +21,10 @@
 HB = pl.BlockSpec(memory_space=pl.ANY)
 NT = (((1,), (1,)), ((), ()))
 
-GATHER_SIGMA = (("x", "z", 0, 64),)
-GATHER_THETA = (("z", "x", 0, 64),)
-SCATTER_THETA = (("x", "z", 0, 64),)
-SCATTER_VAR = (("z", "x", 0, 64),)
+GATHER_SIGMA = (("x", "z"),)
+GATHER_THETA = (("z", "x"),)
+SCATTER_THETA = (("x", "z"),)
+SCATTER_VAR = (("z", "x"),)
 PLACE = {"z": 0, "x": 1, "y": 2, "core": 3}
 
 
@@ -47,27 +47,6 @@
 
 def steps_sent(values, axis):
     return [values[0]] + [sent(values[k], axis, k) for k in range(1, RING)]
-
-
-def prep_kernel(paths_s, paths_t):
-    def kernel(ls_ref, theta_ref, *outs):
-        for n in range(theta_ref.shape[0]):
-            at = slice(n * LANE, (n + 1) * LANE)
-            for (_, _, lo, hi), o in zip(paths_s, outs):
-                o[:, at] = jnp.exp(ls_ref[n, lo:hi]).astype(bf16)
-            for (_, _, lo, hi), o in zip(paths_t, outs[len(paths_s) :]):
-                o[:, at] = theta_ref[n, lo:hi]
-
-    return kernel
-
-
-def prep(ls, theta):
-    c, _, b = theta.shape
-    shapes = [sds((hi - lo, c * b), bf16) for _, _, lo, hi in GATHER_SIGMA + GATHER_THETA]
-    outs = pl.pallas_call(
-        prep_kernel(GATHER_SIGMA, GATHER_THETA), out_shape=shapes, compiler_params=PARAMS, name="prep"
-    )(ls, theta)
-    return outs[: len(GATHER_SIGMA)], outs[len(GATHER_SIGMA) :]
 
 
 def gather(pieces, paths):
@@ -96,12 +75,11 @@
 
 
 def block_column(whole, n):
-    blk = whole[:, :, :, at_block(n)]
-    return blk.reshape(-1, LANE)
-
-
-def scatter_shapes(paths, ff):
-    return [sds((RING, hi - lo, ff), bf16) for _, _, lo, hi in paths for _ in range(RING)]
+    return whole[n].reshape(-1, LANE)
+
+
+def scatter_shapes(paths, columns, own):
+    return [sds((RING, columns, own, LANE), bf16) for _ in paths for _ in range(RING)]
 
 
 def summed(arrived, spot):
@@ -122,28 +100,11 @@
     return arrived
 
 
-def final_kernel(paths, scale, with_sigma):
-    def kernel(*refs):
-        ls = refs[0] if with_sigma else None
-        ins, out = refs[int(with_sigma) : -1], refs[-1]
-        for n in range(out.shape[0]):
-            at = slice(n * LANE, (n + 1) * LANE)
-            for (_, _, lo, hi), group in zip(paths, chunked(ins, RING)):
-                total = group[0][:, at].astype(f32)
-                for r in group[1:]:
-                    total = total + r[:, at].astype(f32)
-                if with_sigma:
-                    total = total * jnp.exp(ls[n, lo:hi])
-                out[n, lo:hi] = total * scale
-
-    return kernel
-
-
-def final(arrived, paths, shape, scale, ls):
-    args = ([] if ls is None else [ls]) + list(arrived)
-    return pl.pallas_call(
-        final_kernel(paths, scale, ls is not None), out_shape=sds(shape, f32), compiler_params=PARAMS
-    )(*args)
+def total_of(arrived):
+    total = arrived[0].astype(f32)
+    for a in arrived[1:]:
+        total = total + a.astype(f32)
+    return total
 
 
 EARLY_GROUPS, MIDDLE_GROUPS, LATE_GROUPS = 4, 2, 4
@@ -162,29 +123,28 @@
 
 def gather_starts(place, paths, groups, whole, sems, per, count):
     for g in range(count):
-        cols = slice(g * per * LANE, (g + 1) * per * LANE)
-        for (one, two, lo, hi), refs in zip(paths, groups):
+        cols = slice(g * per, (g + 1) * per)
+        for (one, two), refs in zip(paths, groups):
             for k in range(RING):
                 for j in range(RING):
                     spot = {one: (place[PLACE[one]] - j) & 3, two: (place[PLACE[two]] - k) & 3}
                     pltpu.make_async_copy(
-                        piece_at(refs, k, j).at[:, cols], whole.at[spot["z"], spot["x"], lo:hi, cols], sems.at[g]
+                        piece_at(refs, k, j).at[cols], whole.at[cols, spot["z"], spot["x"]], sems.at[g]
                     ).start()
 
 
 def gather_wait(whole, sems, g, per):
-    cols = column_span(g, per)
-    part = whole.at[:, :, :, cols]
+    part = whole.at[pl.ds(g * per, per)]
     pltpu.make_async_copy(part, part, sems.at[g]).wait()
 
 
 def scatter_start(place, paths, held, groups, sem, cols):
-    for (one, two, lo, hi), refs in zip(paths, groups):
+    for (one, two), refs in zip(paths, groups):
         for k in range(RING):
             for j in range(RING):
                 spot = {one: (place[PLACE[one]] + k) & 3, two: (place[PLACE[two]] + j) & 3}
                 pltpu.make_async_copy(
-                    held.at[spot["z"], spot["x"], lo:hi, cols], refs[k].at[j, :, cols], sem
+                    held.at[cols, spot["z"], spot["x"]], refs[k].at[j, cols], sem
                 ).start()
 
 
@@ -192,7 +152,7 @@
     outs, (sq_out, sqt_out, tokt, held, sq, sqt, sems) = refs[:-7], refs[-7:]
     place = [lax.axis_index(a) for a in ROW + COL]
     blocks = tok.shape[1] // LANE
-    ks = rows.shape[1]
+    ks = rows.shape[0]
     per = cot.shape[1] // LANE // EARLY_GROUPS
     for k in range(blocks):
         at = slice(k * LANE, (k + 1) * LANE)
@@ -208,10 +168,10 @@
     def group(g, _):
         for u in range(per):
             n = g * per + u
-            lhs = jnp.concatenate([tokt[rows[n, s]] for s in range(ks)], axis=0)
+            lhs = jnp.concatenate([tokt[rows[s, n]] for s in range(ks)], axis=0)
             part = jnp.dot(lhs, cot[:, at_block(n)], preferred_element_type=f32)
-            held[:, :, :, at_block(n)] = part.astype(bf16).reshape(RING, RING, -1, LANE)
-        scatter_start(place, SCATTER_THETA, held, chunked(outs, RING), sems.at[2], column_span(g, per))
+            held[n] = part.astype(bf16).reshape(RING, RING, -1, LANE)
+        scatter_start(place, SCATTER_THETA, held, chunked(outs, RING), sems.at[2], pl.ds(g * per, per))
         return 0
 
     lax.fori_loop(0, EARLY_GROUPS, group, 0)
@@ -223,7 +183,7 @@
 def early(rows, tok, cot, own):
     t, d = tok.shape
     ff = cot.shape[1]
-    shapes = scatter_shapes(SCATTER_THETA, ff) + [sds((t, d), bf16), sds((d // LANE, LANE, t), bf16)]
+    shapes = scatter_shapes(SCATTER_THETA, ff // LANE, own) + [sds((t, d), bf16), sds((d // LANE, LANE, t), bf16)]
     outs = pl.pallas_call(
         early_kernel,
         out_shape=shapes,
@@ -231,7 +191,7 @@
         out_specs=[HB] * len(shapes),
         scratch_shapes=[
             pltpu.VMEM((d // LANE, LANE, t), bf16),
-            pltpu.VMEM((RING, RING, own, ff), bf16),
+            pltpu.VMEM((ff // LANE, RING, RING, own, LANE), bf16),
             pltpu.VMEM((t, d), bf16),
             pltpu.VMEM((d // LANE, LANE, t), bf16),
             pltpu.SemaphoreType.DMA((3,)),
@@ -247,7 +207,7 @@
     sigma_refs, outs = refs[:n_in], refs[n_in:-14]
     gv_out, rn_out, sq, sqt, noise, cot, whole, held, gv, rn, s_sig, s_in, s_one, s_out = refs[-14:]
     place = [lax.axis_index(a) for a in ROW + COL]
-    ks = rows.shape[1]
+    ks = rows.shape[0]
     per = noise.shape[1] // LANE // MIDDLE_GROUPS
     first = pltpu.make_async_copy(sq_in, sq, s_one.at[0])
     second = pltpu.make_async_copy(sqt_in, sqt, s_one.at[1])
@@ -281,7 +241,7 @@
         for u in range(per):
             n = g * per + u
             at = at_block(n)
-            lhs = jnp.concatenate([sq[:, at_block(rows[n, s])] for s in range(ks)], axis=1)
+            lhs = jnp.concatenate([sq[:, at_block(rows[s, n])] for s in range(ks)], axis=1)
             var = jnp.dot(lhs, block_column(whole, n), preferred_element_type=f32) + EPS
             inv = lax.rsqrt(var)
             draw = noise[:, at].astype(f32)
@@ -295,11 +255,11 @@
         for u in range(per):
             n = g * per + u
             at = at_block(n)
-            lhs = jnp.concatenate([sqt[rows[n, s]] for s in range(ks)], axis=0)
+            lhs = jnp.concatenate([sqt[rows[s, n]] for s in range(ks)], axis=0)
             part = jnp.dot(lhs, gv[:, at], preferred_element_type=f32)
-            held[:, :, :, at] = part.astype(bf16).reshape(RING, RING, -1, LANE)
+            held[n] = part.astype(bf16).reshape(RING, RING, -1, LANE)
         issue(saves(g))
-        scatter_start(place, SCATTER_VAR, held, chunked(outs, RING), s_one.at[2], column_span(g, per))
+        scatter_start(place, SCATTER_VAR, held, chunked(outs, RING), s_one.at[2], pl.ds(g * per, per))
         return 0
 
     lax.fori_loop(0, MIDDLE_GROUPS, group, 0)
@@ -312,7 +272,7 @@
 def middle(rows, sq, sqt, noise, cot, sigma, own):
     t, d = sq.shape
     ff = cot.shape[1]
-    shapes = scatter_shapes(SCATTER_VAR, ff) + [sds((t, ff), bf16), sds((t, ff), f32)]
+    shapes = scatter_shapes(SCATTER_VAR, ff // LANE, own) + [sds((t, ff), bf16), sds((t, ff), f32)]
     refs = [r for group in sigma for r in group]
     outs = pl.pallas_call(
         middle_kernel,
@@ -324,8 +284,8 @@
             pltpu.VMEM((d // LANE, LANE, t), bf16),
             pltpu.VMEM((t, ff), bf16),
             pltpu.VMEM((t, ff), bf16),
-            pltpu.VMEM((RING, RING, own, ff), bf16),
-            pltpu.VMEM((RING, RING, own, ff), bf16),
+            pltpu.VMEM((ff // LANE, RING, RING, own, LANE), bf16),
+            pltpu.VMEM((ff // LANE, RING, RING, own, LANE), bf16),
             pltpu.VMEM((t, ff), bf16),
             pltpu.VMEM((t, ff), f32),
             pltpu.SemaphoreType.DMA((MIDDLE_GROUPS,)),
@@ -344,7 +304,7 @@
     sigma_refs, theta_refs = refs[:n_s], refs[n_s : n_s + n_t]
     (out_out, away_out, home_out, tok, cot, gv, rn, out, both, sigma, theta, acc, s_w, s_in, s_one, s_out) = refs[n_s + n_t :]
     place = [lax.axis_index(a) for a in ROW + COL]
-    ks = rows.shape[1]
+    ks = rows.shape[0]
     per = cot.shape[1] // LANE // LATE_GROUPS
     first = pltpu.make_async_copy(tok_in, tok, s_one.at[0])
     first.start()
@@ -376,17 +336,20 @@
             at = at_block(n)
             th = block_column(theta, n)
             sg = block_column(sigma, n)
-            lhs = jnp.concatenate([tok[:, at_block(rows[n, s])] for s in range(ks)], axis=1)
+            lhs = jnp.concatenate([tok[:, at_block(rows[s, n])] for s in range(ks)], axis=1)
             mean = jnp.dot(lhs, th, preferred_element_type=f32)
             out[:, at] = (mean + rn[:, at]).astype(bf16)
+            part_rows = tok.shape[0] // 4
             for q in range(ks // 2):
                 span = slice(q * 2 * LANE, (q + 1) * 2 * LANE)
-                one = lax.dot_general(cot[:, at], th[span], NT, preferred_element_type=f32)
-                two = lax.dot_general(gv[:, at], sg[span], NT, preferred_element_type=f32)
-                for h in range(2):
-                    pick = at_block(rows[n, 2 * q + h])
-                    p = slice(h * LANE, (h + 1) * LANE)
-                    acc[:, pick] += one[:, p] + tok[:, pick].astype(f32) * two[:, p]
+                for m in range(4):
+                    r = slice(m * part_rows, (m + 1) * part_rows)
+                    one = lax.dot_general(cot[r, at], th[span], NT, preferred_element_type=f32)
+                    two = lax.dot_general(gv[r, at], sg[span], NT, preferred_element_type=f32)
+                    for h in range(2):
+                        pick = at_block(rows[2 * q + h, n])
+                        p = slice(h * LANE, (h + 1) * LANE)
+                        acc[r, pick] += one[:, p] + tok[r, pick].astype(f32) * two[:, p]
         save(g).start()
         return 0
 
@@ -422,8 +385,8 @@
             pltpu.VMEM((t, ff), f32),
             pltpu.VMEM((t, ff), bf16),
             pltpu.VMEM((2, RING, t, w), bf16),
-            pltpu.VMEM((RING, RING, own, ff), bf16),
-            pltpu.VMEM((RING, RING, own, ff), bf16),
+            pltpu.VMEM((ff // LANE, RING, RING, own, LANE), bf16),
+            pltpu.VMEM((ff // LANE, RING, RING, own, LANE), bf16),
             pltpu.VMEM((t, d), f32),
             pltpu.SemaphoreType.DMA((2, LATE_GROUPS)),
             pltpu.SemaphoreType.DMA((3, LATE_GROUPS)),
@@ -437,26 +400,25 @@
 
 def step(tokens, theta, log_sigma2, block_rows, noise, cotangent):
     own = theta.shape[1]
-    sg, th = prep(log_sigma2, theta)
+    width = block_rows.shape[1] * LANE
+    rows = block_rows.T
+    sg, th = [jnp.exp(log_sigma2).astype(bf16)], [theta]
     sigma_in = gather_relayed(sg[0], GATHER_SIGMA[0])
     theta_in = gather(th, GATHER_THETA)
-    parts_theta, sq, sqt = early(block_rows, tokens, cotangent, own)
-    parts_var, gv, rn = middle(block_rows, sq, sqt, noise, cotangent, sigma_in, own)
-    output, away, home = late(block_rows, tokens, cotangent, gv, rn, sigma_in, theta_in, own)
+    parts_theta, sq, sqt = early(rows, tokens, cotangent, own)
+    parts_var, gv, rn = middle(rows, sq, sqt, noise, cotangent, sigma_in, own)
+    output, away, home = late(rows, tokens, cotangent, gv, rn, sigma_in, theta_in, own)
     tokens_all = tokens.shape[0] * lax.axis_size(ROW)
-    width = block_rows.shape[1] * LANE
     inv_root = 1.0 / math.sqrt(tokens_all)
     got_theta = scatter(parts_theta, SCATTER_THETA)
-    grad_theta = final(got_theta, SCATTER_THETA, theta.shape, inv_root, None)
+    grad_theta = total_of(got_theta) * inv_root
     got_var = scatter(parts_var, SCATTER_VAR)
-    grad_logvar = final(got_var, SCATTER_VAR, theta.shape, 0.5 * width * inv_root, log_sigma2)
+    grad_logvar = jnp.exp(log_sigma2) * total_of(got_var) * (0.5 * width * inv_root)
     came = sent(away, "core", 1)
     pairs = [(home[k].astype(f32) + came[k].astype(f32)).astype(bf16) for k in range(RING)]
     pairs = lax.optimization_barrier(pairs)
     arrived = steps_sent(pairs, "y")
-    grad_tokens = arrived[0].astype(f32)
-    for a in arrived[1:]:
-        grad_tokens = grad_tokens + a.astype(f32)
+    grad_tokens = total_of(arrived)
     return (output, grad_tokens, grad_theta, grad_logvar)
 
 

time: 180 us -> 201 us (1.12)
  waiting for transfers between devices: 68 us -> 101 us
  Pallas kernels: 57.6 us -> 49 us
  starting transfers between devices: 42 us -> 39.7 us
    ppermute x29, waiting for transfers between devices: 68 us -> 101 us  [sent(): return lax.ppermute(value, axis, [(i, (i + step) % n) for i in range(n)])]
    pallas_call x3 -> x0, Pallas kernels: 6.12 us -> none  [the longest x2 4.26 us: final(): pl.pallas_call(final_kernel(paths, scale, ls is not None), out_shape=sds(...]
    ppermute x29, starting transfers between devices: 42 us -> 39.7 us  [sent(): return lax.ppermute(value, axis, [(i, (i + step) % n) for i in range(n)])]
  transfers between devices with their start and end apart: 29 -> 29, of which waited for: 10 -> 12; matrix products, arithmetic and copies ran while one was open for 4% -> 3% of each run, Pallas kernels for 17% -> 13%
where the time goes in v4:
time: 201 us
  waiting for transfers between devices  101 us (50%)
  Pallas kernels  49 us (24%)
  starting transfers between devices  39.7 us (20%)
  other arithmetic  7.08 us (4%)
  local copies, waits for them, and re-layouts  2.56 us (1%)
    ppermute x29, waiting for transfers between devices, sent(): return lax.ppermute(value, axis, [(i, (i + step) % n) for i in range(n)])  101 us
    ppermute x29, starting transfers between devices, sent(): return lax.ppermute(value, axis, [(i, (i + step) % n) for i in range(n)])  39.7 us
    pallas_call x1, Pallas kernels, late(): pl.pallas_call(late_kernel, out_shape=shapes, in_specs=[SM] + [HB] * (4 +...  23.5 us
    pallas_call x1, Pallas kernels, middle(): pl.pallas_call(middle_kernel, out_shape=shapes, in_specs=[SM, HB, HB, HB,...  14.8 us
    pallas_call x1, Pallas kernels, early(): pl.pallas_call(early_kernel, out_shape=shapes, in_specs=[SM, VB, VB], out...  10.7 us
  transfers between devices with their start and end apart: 29, of which 12 were waited for; matrix products, arithmetic and copies ran while one was open for 3% of the time, Pallas kernels for 13%

profile of v4, /device:TPU:1, one launch (start us, length us, event | category | flops | bytes accessed | tf_op | source)
XLA Modules:
  0.0 200.6 jit_solution(10048308795011606735)
XLA Ops:
  0.6 1.1 exponential_convert_fusion
  1.7 2.1 %collective-permute-start = (bf16[12,64,128]{2,1,0:T(8,128)(2,1)S(1)}, bf16[12,64,128]{2,1,0:T(8,128)(2,1)S(1)}, u32[]{:S(2)}, u32[]{:S(2)}) collective-permute-start(bf16[12,64,128]{2,1,0:T(8,128)(2,1)S(1)} %exponential_convert_fusion), channel_id=1, source_target_pairs={{0,8},{8,16},{16,24},{24,0},{1,9},{9,17},{17,25},{25,1},{2,10},{10... | collective-permute-start | bytes 589832 | tf_op jit(solution)/shard_map/ppermute | solution.py:41
  3.8 2.5 %collective-permute-start.1 = (bf16[12,64,128]{2,1,0:T(8,128)(2,1)S(1)}, bf16[12,64,128]{2,1,0:T(8,128)(2,1)S(1)}, u32[]{:S(2)}, u32[]{:S(2)}) collective-permute-start(bf16[12,64,128]{2,1,0:T(8,128)(2,1)S(1)} %exponential_convert_fusion), channel_id=1, source_target_pairs={{0,16},{8,24},{16,0},{24,8},{1,17},{9,25},{17,1},{25,9},{2,18},{10... | collective-permute-start | bytes 589832 | tf_op jit(solution)/shard_map/ppermute | solution.py:41
  6.3 1.2 collective-permute-start.2
  7.4 1.1 fusion.19
  8.5 0.8 collective-permute-done
  9.3 5.5 %collective-permute-done.1 = bf16[12,64,128]{2,1,0:T(8,128)(2,1)S(1)} collective-permute-done((bf16[12,64,128]{2,1,0:T(8,128)(2,1)S(1)}, bf16[12,64,128]{2,1,0:T(8,128)(2,1)S(1)}, u32[]{:S(2)}, u32[]{:S(2)}) %collective-permute-start.1) | collective-permute-done | bytes 196640 | tf_op jit(solution)/shard_map/ppermute | solution.py:41
  14.9 1.7 collective-permute-start.3
  16.6 2.2 %collective-permute-start.5 = (bf16[4,12,64,128]{3,2,1,0:T(8,128)(2,1)S(1)}, bf16[4,12,64,128]{3,2,1,0:T(8,128)(2,1)S(1)}, u32[]{:S(2)}, u32[]{:S(2)}) collective-permute-start(bf16[4,12,64,128]{3,2,1,0:T(8,128)(2,1)S(1)} %pad_maximum_fusion.refs_0_), channel_id=1, source_target_pairs={{0,96},{32,0},{64,32},{96,64},{1,97},{33,1},{65,33},{97,65},{2,98}... | collective-permute-start | bytes 2359304 | tf_op jit(solution)/shard_map/ppermute | solution.py:41
  18.9 2.6 %collective-permute-start.8 = (bf16[12,64,128]{2,1,0:T(8,128)(2,1)S(1)}, bf16[12,64,128]{2,1,0:T(8,128)(2,1)S(1)}, u32[]{:S(2)}, u32[]{:S(2)}) collective-permute-start(bf16[12,64,128]{2,1,0:T(8,128)(2,1)S(1)} %copy-done.10), channel_id=1, source_target_pairs={{0,64},{32,96},{64,0},{96,32},{1,65},{33,97},{65,1},{97,33},{2,66}... | collective-permute-start | bytes 589832 | tf_op jit(solution)/shard_map/ppermute | solution.py:41
  21.4 0.7 collective-permute-start.9
  22.1 17.2 %collective-permute-done.7 = bf16[12,64,128]{2,1,0:T(8,128)(2,1)S(1)} collective-permute-done((bf16[12,64,128]{2,1,0:T(8,128)(2,1)S(1)}, bf16[12,64,128]{2,1,0:T(8,128)(2,1)S(1)}, u32[]{:S(2)}, u32[]{:S(2)}) %collective-permute-start.7) | collective-permute-done | bytes 196640 | tf_op jit(solution)/shard_map/ppermute | solution.py:41
  39.4 5.1 %collective-permute-done.8 = bf16[12,64,128]{2,1,0:T(8,128)(2,1)S(1)} collective-permute-done((bf16[12,64,128]{2,1,0:T(8,128)(2,1)S(1)}, bf16[12,64,128]{2,1,0:T(8,128)(2,1)S(1)}, u32[]{:S(2)}, u32[]{:S(2)}) %collective-permute-start.8) | collective-permute-done | bytes 196640 | tf_op jit(solution)/shard_map/ppermute | solution.py:41
  44.6 1.8 collective-permute-start.10
  46.4 2.9 %collective-permute-start.11 = (bf16[4,12,64,128]{3,2,1,0:T(8,128)(2,1)S(1)}, bf16[4,12,64,128]{3,2,1,0:T(8,128)(2,1)}, u32[]{:S(2)}, u32[]{:S(2)}) collective-permute-start(bf16[4,12,64,128]{3,2,1,0:T(8,128)(2,1)S(1)} %pad_maximum_fusion.1.refs_5_), channel_id=1, source_target_pairs={{0,16},{8,24},{16,0},{24,8},{1,17},{9,25},{17,1},{25,9},{2,18},{10... | collective-permute-start | bytes 2359304 | tf_op jit(solution)/shard_map/ppermute | solution.py:41
  49.4 0.8 slice.168
  50.2 0.8 slice.169
  51.0 2.7 %collective-permute-start.6 = (bf16[2,12,64,128]{3,2,1,0:T(8,128)(2,1)}, bf16[2,12,64,128]{3,2,1,0:T(8,128)(2,1)S(1)}, u32[]{:S(2)}, u32[]{:S(2)}) collective-permute-start(bf16[2,12,64,128]{3,2,1,0:T(8,128)(2,1)} %slice.169), channel_id=1, source_target_pairs={{0,96},{32,0},{64,32},{96,64},{1,97},{33,1},{65,33},{97,65},{2,98}... | collective-permute-start | bytes 1179656 | tf_op jit(solution)/shard_map/ppermute | solution.py:41
  53.7 10.7 %early.1 = (bf16[4,12,64,128]{3,2,1,0:T(8,128)(2,1)}, bf16[4,12,64,128]{3,2,1,0:T(8,128)(2,1)}, bf16[4,12,64,128]{3,2,1,0:T(8,128)(2,1)}, bf16[4,12,64,128]{3,2,...) custom-call(s32[8,12]{1,0:T(8,128)} %bitcast.47, bf16[512,4096]{1,0:T(8,128)(2,1)} %tok_in.1, ...), custom_call_target="tpu_custom_call" | custom-call | tf_op jit(solution)/shard_map/early/pallas_call | solution.py:187
  64.5 0.7 copy-done.6
  65.3 14.8 %middle.1 = (bf16[4,12,64,128]{3,2,1,0:T(8,128)(2,1)}, bf16[4,12,64,128]{3,2,1,0:T(8,128)(2,1)}, bf16[4,12,64,128]{3,2,1,0:T(8,128)(2,1)}, bf16[4,12,64,128]{3,2...) custom-call(s32[8,12]{1,0:T(8,128)} %bitcast.48, bf16[512,4096]{1,0:T(8,128)(2,1)} %get-tuple-element.23.sq_in, ...), custom_call_target="tpu_custom_call" | custom-call | tf_op jit(solution)/shard_map/middle/pallas_call | solution.py:277
  80.2 2.2 %collective-permute-done.11.refs_7_ = bf16[4,12,64,128]{3,2,1,0:T(8,128)(2,1)} collective-permute-done((bf16[4,12,64,128]{3,2,1,0:T(8,128)(2,1)S(1)}, bf16[4,12,64,128]{3,2,1,0:T(8,128)(2,1)}, u32[]{:S(2)}, u32[]{:S(2)}) %collective-permute-start.11) | collective-permute-done | bytes 786464 | tf_op jit(solution)/shard_map/ppermute | solution.py:41
  82.3 0.4 collective-permute-done.12.refs_8_
  82.7 23.5 %late.1 = (bf16[512,1536]{1,0:T(8,128)(2,1)}, bf16[4,512,512]{2,1,0:T(8,128)(2,1)}, bf16[4,512,512]{2,1,0:T(8,128)(2,1)}) custom-call(s32[8,12]{1,0:T(8,128)} %bitcast.49, bf16[512,4096]{1,0:T(8,128)(2,1)} %tok_in.1, bf16[512,1536]{1,0:T(8,128)(2,1)} %cot_in.3, bf16[512,1536]{1,0:T(8,128)(2,1)} %get-tuple-element.25.gv_in, ...), custom_call_target="tpu_custom_call" | custom-call | tf_op jit(solution)/shard_map/late/pallas_call | solution.py:376
  106.2 2.4 %collective-permute-start.13 = (bf16[4,512,512]{2,1,0:T(8,128)(2,1)}, bf16[4,512,512]{2,1,0:T(8,128)(2,1)S(1)}, u32[]{:S(2)}, u32[]{:S(2)}) collective-permute-start(bf16[4,512,512]{2,1,0:T(8,128)(2,1)} %get-tuple-element.29), channel_id=1, source_target_pairs={{0,1},{1,0},{2,3},{3,2},{4,5},{5,4},{6,7},{7,6},{8,9},{9,8},{10,11... | collective-permute-start | bytes 6291464 | tf_op jit(solution)/shard_map/ppermute | solution.py:41
  108.6 0.1 collective-permute-start.17
  108.7 2.9 %collective-permute-start.18 = (bf16[4,12,64,128]{3,2,1,0:T(8,128)(2,1)}, bf16[4,12,64,128]{3,2,1,0:T(8,128)(2,1)S(1)}, u32[]{:S(2)}, u32[]{:S(2)}) collective-permute-start(bf16[4,12,64,128]{3,2,1,0:T(8,128)(2,1)} %get-tuple-element.36), channel_id=1, source_target_pairs={{0,16},{8,24},{16,0},{24,8},{1,17},{9,25},{17,1},{25,9},{2,18},{10... | collective-permute-start | bytes 2359304 | tf_op jit(solution)/shard_map/ppermute | solution.py:41
  111.7 17.3 %collective-permute-done.17 = bf16[4,12,64,128]{3,2,1,0:T(8,128)(2,1)S(1)} collective-permute-done((bf16[4,12,64,128]{3,2,1,0:T(8,128)(2,1)}, bf16[4,12,64,128]{3,2,1,0:T(8,128)(2,1)S(1)}, u32[]{:S(2)}, u32[]{:S(2)}) %collective-permute-start.17) | collective-permute-done | bytes 786464 | tf_op jit(solution)/shard_map/ppermute | solution.py:41
  129.0 1.2 collective-permute-start.24
  130.3 16.0 %collective-permute-done.18 = bf16[4,12,64,128]{3,2,1,0:T(8,128)(2,1)S(1)} collective-permute-done((bf16[4,12,64,128]{3,2,1,0:T(8,128)(2,1)}, bf16[4,12,64,128]{3,2,1,0:T(8,128)(2,1)S(1)}, u32[]{:S(2)}, u32[]{:S(2)}) %collective-permute-start.18) | collective-permute-done | bytes 786464 | tf_op jit(solution)/shard_map/ppermute | solution.py:41
  146.3 1.6 collective-permute-start.25
  147.8 0.4 fusion.12
  148.4 1.2 collective-permute-start.21
  149.5 1.6 collective-permute-start.22
  151.1 13.9 %collective-permute-done.25 = bf16[4,12,64,128]{3,2,1,0:T(8,128)(2,1)S(1)} collective-permute-done((bf16[4,12,64,128]{3,2,1,0:T(8,128)(2,1)S(1)}, bf16[4,12,64,128]{3,2,1,0:T(8,128)(2,1)S(1)}, u32[]{:S(2)}, u32[]{:S(2)}) %collective-permute-start.25) | collective-permute-done | bytes 786464 | tf_op jit(solution)/shard_map/ppermute | solution.py:41
  165.0 0.4 fusion.16
  165.5 0.3 collective-permute-start.26
  165.8 2.9 %collective-permute-start.27 = (bf16[12,64,128]{2,1,0:T(8,128)(2,1)S(1)}, bf16[12,64,128]{2,1,0:T(8,128)(2,1)S(1)}, u32[]{:S(2)}, u32[]{:S(2)}) collective-permute-start(bf16[12,64,128]{2,1,0:T(8,128)(2,1)S(1)} %get-tuple-element.48), channel_id=1, source_target_pairs={{0,16},{8,24},{16,0},{24,8},{1,17},{9,25},{17,1},{25,9},{2,18},{10... | collective-permute-start | bytes 589832 | tf_op jit(solution)/shard_map/ppermute | solution.py:41
  168.7 0.7 fusion.3
  169.5 1.3 collective-permute-start.14
  170.8 2.7 %collective-permute-done.22 = bf16[12,64,128]{2,1,0:T(8,128)(2,1)S(1)} collective-permute-done((bf16[12,64,128]{2,1,0:T(8,128)(2,1)S(1)}, bf16[12,64,128]{2,1,0:T(8,128)(2,1)S(1)}, u32[]{:S(2)}, u32[]{:S(2)}) %collective-permute-start.22) | collective-permute-done | bytes 196640 | tf_op jit(solution)/shard_map/ppermute | solution.py:41
  173.5 3.0 %collective-permute-start.15 = (bf16[512,512]{1,0:T(8,128)(2,1)S(1)}, bf16[512,512]{1,0:T(8,128)(2,1)S(1)}, u32[]{:S(2)}, u32[]{:S(2)}) collective-permute-start(bf16[512,512]{1,0:T(8,128)(2,1)S(1)} %get-tuple-element.32), channel_id=1, source_target_pairs={{0,4},{2,6},{4,0},{6,2},{1,5},{3,7},{5,1},{7,3},{8,12},{10,14},{12... | collective-permute-start | bytes 1572872 | tf_op jit(solution)/shard_map/ppermute | solution.py:41
  176.5 0.7 collective-permute-start.16
  177.1 1.0 fusion.10
  178.1 1.0 fusion.7
  179.1 11.2 %collective-permute-done.15 = bf16[512,512]{1,0:T(8,128)(2,1)S(1)} collective-permute-done((bf16[512,512]{1,0:T(8,128)(2,1)S(1)}, bf16[512,512]{1,0:T(8,128)(2,1)S(1)}, u32[]{:S(2)}, u32[]{:S(2)}) %collective-permute-start.15) | collective-permute-done | bytes 524320 | tf_op jit(solution)/shard_map/ppermute | solution.py:41
  190.4 9.0 %collective-permute-done.16 = bf16[512,512]{1,0:T(8,128)(2,1)S(1)} collective-permute-done((bf16[512,512]{1,0:T(8,128)(2,1)S(1)}, bf16[512,512]{1,0:T(8,128)(2,1)S(1)}, u32[]{:S(2)}, u32[]{:S(2)}) %collective-permute-start.16) | collective-permute-done | bytes 524320 | tf_op jit(solution)/shard_map/ppermute | solution.py:41
  199.4 1.2 convert_add_fusion
  (55 shorter events, 0.7 us)
Async XLA Ops:
  0.6 18.2 %copy-start.10 = (bf16[12,64,128]{2,1,0:T(8,128)(2,1)S(1)}, bf16[12,64,128]{2,1,0:T(8,128)(2,1)}, u32[]{:S(2)}) copy-start(bf16[12,64,128]{2,1,0:T(8,128)(2,1)} %param.7) | copy-start | bytes 589828
  1.7 7.6 %collective-permute-start = (bf16[12,64,128]{2,1,0:T(8,128)(2,1)S(1)}, bf16[12,64,128]{2,1,0:T(8,128)(2,1)S(1)}, u32[]{:S(2)}, u32[]{:S(2)}) collective-permute-start(bf16[12,64,128]{2,1,0:T(8,128)(2,1)S(1)} %exponential_convert_fusion), channel_id=1, source_target_pairs={{0,8},{8,16},{16,24},{24,0},{1,9},{9,17},{17,25},{25,1},{2,10},{10... | collective-permute-start | bytes 589832 | tf_op jit(solution)/shard_map/ppermute | solution.py:41
  3.8 11.0 %collective-permute-start.1 = (bf16[12,64,128]{2,1,0:T(8,128)(2,1)S(1)}, bf16[12,64,128]{2,1,0:T(8,128)(2,1)S(1)}, u32[]{:S(2)}, u32[]{:S(2)}) collective-permute-start(bf16[12,64,128]{2,1,0:T(8,128)(2,1)S(1)} %exponential_convert_fusion), channel_id=1, source_target_pairs={{0,16},{8,24},{16,0},{24,8},{1,17},{9,25},{17,1},{25,9},{2,18},{10... | collective-permute-start | bytes 589832 | tf_op jit(solution)/shard_map/ppermute | solution.py:41
  6.3 8.5 %collective-permute-start.2 = (bf16[12,64,128]{2,1,0:T(8,128)(2,1)S(1)}, bf16[12,64,128]{2,1,0:T(8,128)(2,1)S(1)}, u32[]{:S(2)}, u32[]{:S(2)}) collective-permute-start(bf16[12,64,128]{2,1,0:T(8,128)(2,1)S(1)} %exponential_convert_fusion), channel_id=1, source_target_pairs={{0,24},{8,0},{16,8},{24,16},{1,25},{9,1},{17,9},{25,17},{2,26},{10... | collective-permute-start | bytes 589832 | tf_op jit(solution)/shard_map/ppermute | solution.py:41
  14.9 49.5 %copy-start = (bf16[4,12,64,128]{3,2,1,0:T(8,128)(2,1)}, bf16[4,12,64,128]{3,2,1,0:T(8,128)(2,1)S(1)}, u32[]{:S(2)}) copy-start(bf16[4,12,64,128]{3,2,1,0:T(8,128)(2,1)S(1)} %pad_maximum_fusion.refs_0_) | copy-start | bytes 2359300
  14.9 34.4 %collective-permute-start.3 = (bf16[4,12,64,128]{3,2,1,0:T(8,128)(2,1)S(1)}, bf16[4,12,64,128]{3,2,1,0:T(8,128)(2,1)S(1)}, u32[]{:S(2)}, u32[]{:S(2)}) collective-permute-start(bf16[4,12,64,128]{3,2,1,0:T(8,128)(2,1)S(1)} %pad_maximum_fusion.refs_0_), channel_id=1, source_target_pairs={{0,32},{32,64},{64,96},{96,0},{1,33},{33,65},{65,97},{97,1},{2,34}... | collective-permute-start | bytes 2359304 | tf_op jit(solution)/shard_map/ppermute | solution.py:41
  16.6 33.6 %collective-permute-start.5 = (bf16[4,12,64,128]{3,2,1,0:T(8,128)(2,1)S(1)}, bf16[4,12,64,128]{3,2,1,0:T(8,128)(2,1)S(1)}, u32[]{:S(2)}, u32[]{:S(2)}) collective-permute-start(bf16[4,12,64,128]{3,2,1,0:T(8,128)(2,1)S(1)} %pad_maximum_fusion.refs_0_), channel_id=1, source_target_pairs={{0,96},{32,0},{64,32},{96,64},{1,97},{33,1},{65,33},{97,65},{2,98}... | collective-permute-start | bytes 2359304 | tf_op jit(solution)/shard_map/ppermute | solution.py:41
  18.9 20.5 %collective-permute-start.7 = (bf16[12,64,128]{2,1,0:T(8,128)(2,1)S(1)}, bf16[12,64,128]{2,1,0:T(8,128)(2,1)S(1)}, u32[]{:S(2)}, u32[]{:S(2)}) collective-permute-start(bf16[12,64,128]{2,1,0:T(8,128)(2,1)S(1)} %copy-done.10), channel_id=1, source_target_pairs={{0,32},{32,64},{64,96},{96,0},{1,33},{33,65},{65,97},{97,1},{2,34}... | collective-permute-start | bytes 589832 | tf_op jit(solution)/shard_map/ppermute | solution.py:41
  18.9 25.6 %collective-permute-start.8 = (bf16[12,64,128]{2,1,0:T(8,128)(2,1)S(1)}, bf16[12,64,128]{2,1,0:T(8,128)(2,1)S(1)}, u32[]{:S(2)}, u32[]{:S(2)}) collective-permute-start(bf16[12,64,128]{2,1,0:T(8,128)(2,1)S(1)} %copy-done.10), channel_id=1, source_target_pairs={{0,64},{32,96},{64,0},{96,32},{1,65},{33,97},{65,1},{97,33},{2,66}... | collective-permute-start | bytes 589832 | tf_op jit(solution)/shard_map/ppermute | solution.py:41
  21.4 23.1 %collective-permute-start.9 = (bf16[12,64,128]{2,1,0:T(8,128)(2,1)S(1)}, bf16[12,64,128]{2,1,0:T(8,128)(2,1)S(1)}, u32[]{:S(2)}, u32[]{:S(2)}) collective-permute-start(bf16[12,64,128]{2,1,0:T(8,128)(2,1)S(1)} %copy-done.10), channel_id=1, source_target_pairs={{0,96},{32,0},{64,32},{96,64},{1,97},{33,1},{65,33},{97,65},{2,98}... | collective-permute-start | bytes 589832 | tf_op jit(solution)/shard_map/ppermute | solution.py:41
  44.6 19.8 %copy-start.4 = (bf16[4,12,64,128]{3,2,1,0:T(8,128)(2,1)}, bf16[4,12,64,128]{3,2,1,0:T(8,128)(2,1)S(1)}, u32[]{:S(2)}) copy-start(bf16[4,12,64,128]{3,2,1,0:T(8,128)(2,1)S(1)} %pad_maximum_fusion.1.refs_5_) | copy-start | bytes 2359300
  44.6 35.6 %collective-permute-start.10 = (bf16[4,12,64,128]{3,2,1,0:T(8,128)(2,1)S(1)}, bf16[4,12,64,128]{3,2,1,0:T(8,128)(2,1)}, u32[]{:S(2)}, u32[]{:S(2)}) collective-permute-start(bf16[4,12,64,128]{3,2,1,0:T(8,128)(2,1)S(1)} %pad_maximum_fusion.1.refs_5_), channel_id=1, source_target_pairs={{0,8},{8,16},{16,24},{24,0},{1,9},{9,17},{17,25},{25,1},{2,10},{10... | collective-permute-start | bytes 2359304 | tf_op jit(solution)/shard_map/ppermute | solution.py:41
  46.4 35.9 %collective-permute-start.11 = (bf16[4,12,64,128]{3,2,1,0:T(8,128)(2,1)S(1)}, bf16[4,12,64,128]{3,2,1,0:T(8,128)(2,1)}, u32[]{:S(2)}, u32[]{:S(2)}) collective-permute-start(bf16[4,12,64,128]{3,2,1,0:T(8,128)(2,1)S(1)} %pad_maximum_fusion.1.refs_5_), channel_id=1, source_target_pairs={{0,16},{8,24},{16,0},{24,8},{1,17},{9,25},{17,1},{25,9},{2,18},{10... | collective-permute-start | bytes 2359304 | tf_op jit(solution)/shard_map/ppermute | solution.py:41
  49.4 33.3 %collective-permute-start.12 = (bf16[4,12,64,128]{3,2,1,0:T(8,128)(2,1)S(1)}, bf16[4,12,64,128]{3,2,1,0:T(8,128)(2,1)}, u32[]{:S(2)}, u32[]{:S(2)}) collective-permute-start(bf16[4,12,64,128]{3,2,1,0:T(8,128)(2,1)S(1)} %pad_maximum_fusion.1.refs_5_), channel_id=1, source_target_pairs={{0,24},{8,0},{16,8},{24,16},{1,25},{9,1},{17,9},{25,17},{2,26},{10... | collective-permute-start | bytes 2359304 | tf_op jit(solution)/shard_map/ppermute | solution.py:41
  49.4 15.1 %copy-start.1 = (bf16[4,12,64,128]{3,2,1,0:T(8,128)(2,1)}, bf16[4,12,64,128]{3,2,1,0:T(8,128)(2,1)S(1)}, u32[]{:S(2)}) copy-start(bf16[4,12,64,128]{3,2,1,0:T(8,128)(2,1)S(1)} %collective-permute-done.3.refs_1_) | copy-start | bytes 2359300
  50.2 14.3 %collective-permute-start.4 = (bf16[2,12,64,128]{3,2,1,0:T(8,128)(2,1)}, bf16[2,12,64,128]{3,2,1,0:T(8,128)(2,1)S(1)}, u32[]{:S(2)}, u32[]{:S(2)}) collective-permute-start(bf16[2,12,64,128]{3,2,1,0:T(8,128)(2,1)} %slice.168), channel_id=1, source_target_pairs={{0,32},{32,64},{64,96},{96,0},{1,33},{33,65},{65,97},{97,1},{2,34}... | collective-permute-start | bytes 1179656 | tf_op jit(solution)/shard_map/ppermute | solution.py:41
  50.2 14.2 %copy-start.2 = (bf16[4,12,64,128]{3,2,1,0:T(8,128)(2,1)}, bf16[4,12,64,128]{3,2,1,0:T(8,128)(2,1)S(1)}, u32[]{:S(2)}) copy-start(bf16[4,12,64,128]{3,2,1,0:T(8,128)(2,1)S(1)} %collective-permute-done.5.refs_4_) | copy-start | bytes 2359300
  51.0 13.4 %collective-permute-start.6 = (bf16[2,12,64,128]{3,2,1,0:T(8,128)(2,1)}, bf16[2,12,64,128]{3,2,1,0:T(8,128)(2,1)S(1)}, u32[]{:S(2)}, u32[]{:S(2)}) collective-permute-start(bf16[2,12,64,128]{3,2,1,0:T(8,128)(2,1)} %slice.169), channel_id=1, source_target_pairs={{0,96},{32,0},{64,32},{96,64},{1,97},{33,1},{65,33},{97,65},{2,98}... | collective-permute-start | bytes 1179656 | tf_op jit(solution)/shard_map/ppermute | solution.py:41
  64.5 0.7 copy-start.6
  64.5 0.9 copy-start.7
  82.7 29.0 %copy-start.13 = (bf16[4,12,64,128]{3,2,1,0:T(8,128)(2,1)S(1)}, bf16[4,12,64,128]{3,2,1,0:T(8,128)(2,1)}, u32[]{:S(2)}) copy-start(bf16[4,12,64,128]{3,2,1,0:T(8,128)(2,1)} %get-tuple-element.37) | copy-start | bytes 2359300
  82.7 29.0 %copy-start.14 = (bf16[4,12,64,128]{3,2,1,0:T(8,128)(2,1)S(1)}, bf16[4,12,64,128]{3,2,1,0:T(8,128)(2,1)}, u32[]{:S(2)}) copy-start(bf16[4,12,64,128]{3,2,1,0:T(8,128)(2,1)} %get-tuple-element.39) | copy-start | bytes 2359300
  82.7 46.4 %copy-start.12 = (bf16[4,12,64,128]{3,2,1,0:T(8,128)(2,1)S(1)}, bf16[4,12,64,128]{3,2,1,0:T(8,128)(2,1)}, u32[]{:S(2)}) copy-start(bf16[4,12,64,128]{3,2,1,0:T(8,128)(2,1)} %get-tuple-element.40) | copy-start | bytes 2359300
  82.7 63.6 %copy-start.11 = (bf16[4,12,64,128]{3,2,1,0:T(8,128)(2,1)S(1)}, bf16[4,12,64,128]{3,2,1,0:T(8,128)(2,1)}, u32[]{:S(2)}) copy-start(bf16[4,12,64,128]{3,2,1,0:T(8,128)(2,1)} %get-tuple-element.41) | copy-start | bytes 2359300
  82.7 65.2 %copy-start.9 = (bf16[4,12,64,128]{3,2,1,0:T(8,128)(2,1)S(1)}, bf16[4,12,64,128]{3,2,1,0:T(8,128)(2,1)}, u32[]{:S(2)}) copy-start(bf16[4,12,64,128]{3,2,1,0:T(8,128)(2,1)} %get-tuple-element.34) | copy-start | bytes 2359300
  106.2 58.9 %copy-start.8 = (bf16[4,12,64,128]{3,2,1,0:T(8,128)(2,1)S(1)}, bf16[4,12,64,128]{3,2,1,0:T(8,128)(2,1)}, u32[]{:S(2)}) copy-start(bf16[4,12,64,128]{3,2,1,0:T(8,128)(2,1)} %get-tuple-element.38) | copy-start | bytes 2359300
  106.2 59.6 %collective-permute-start.13 = (bf16[4,512,512]{2,1,0:T(8,128)(2,1)}, bf16[4,512,512]{2,1,0:T(8,128)(2,1)S(1)}, u32[]{:S(2)}, u32[]{:S(2)}) collective-permute-start(bf16[4,512,512]{2,1,0:T(8,128)(2,1)} %get-tuple-element.29), channel_id=1, source_target_pairs={{0,1},{1,0},{2,3},{3,2},{4,5},{5,4},{6,7},{7,6},{8,9},{9,8},{10,11... | collective-permute-start | bytes 6291464 | tf_op jit(solution)/shard_map/ppermute | solution.py:41
  108.6 20.4 %collective-permute-start.17 = (bf16[4,12,64,128]{3,2,1,0:T(8,128)(2,1)}, bf16[4,12,64,128]{3,2,1,0:T(8,128)(2,1)S(1)}, u32[]{:S(2)}, u32[]{:S(2)}) collective-permute-start(bf16[4,12,64,128]{3,2,1,0:T(8,128)(2,1)} %get-tuple-element.35), channel_id=1, source_target_pairs={{0,8},{8,16},{16,24},{24,0},{1,9},{9,17},{17,25},{25,1},{2,10},{10... | collective-permute-start | bytes 2359304 | tf_op jit(solution)/shard_map/ppermute | solution.py:41
  108.7 37.5 %collective-permute-start.18 = (bf16[4,12,64,128]{3,2,1,0:T(8,128)(2,1)}, bf16[4,12,64,128]{3,2,1,0:T(8,128)(2,1)S(1)}, u32[]{:S(2)}, u32[]{:S(2)}) collective-permute-start(bf16[4,12,64,128]{3,2,1,0:T(8,128)(2,1)} %get-tuple-element.36), channel_id=1, source_target_pairs={{0,16},{8,24},{16,0},{24,8},{1,17},{9,25},{17,1},{25,9},{2,18},{10... | collective-permute-start | bytes 2359304 | tf_op jit(solution)/shard_map/ppermute | solution.py:41
  111.7 36.2 %collective-permute-start.19 = (bf16[4,12,64,128]{3,2,1,0:T(8,128)(2,1)S(1)}, bf16[4,12,64,128]{3,2,1,0:T(8,128)(2,1)S(1)}, u32[]{:S(2)}, u32[]{:S(2)}) collective-permute-start(bf16[4,12,64,128]{3,2,1,0:T(8,128)(2,1)S(1)} %copy-done.13), channel_id=1, source_target_pairs={{0,24},{8,0},{16,8},{24,16},{1,25},{9,1},{17,9},{25,17},{2,26},{10... | collective-permute-start | bytes 2359304 | tf_op jit(solution)/shard_map/ppermute | solution.py:41
  111.7 36.7 %collective-permute-start.23 = (bf16[4,12,64,128]{3,2,1,0:T(8,128)(2,1)S(1)}, bf16[4,12,64,128]{3,2,1,0:T(8,128)(2,1)S(1)}, u32[]{:S(2)}, u32[]{:S(2)}) collective-permute-start(bf16[4,12,64,128]{3,2,1,0:T(8,128)(2,1)S(1)} %copy-done.14), channel_id=1, source_target_pairs={{0,32},{32,64},{64,96},{96,0},{1,33},{33,65},{65,97},{97,1},{2,34}... | collective-permute-start | bytes 2359304 | tf_op jit(solution)/shard_map/ppermute | solution.py:41
  129.0 20.5 %collective-permute-start.24 = (bf16[4,12,64,128]{3,2,1,0:T(8,128)(2,1)S(1)}, bf16[4,12,64,128]{3,2,1,0:T(8,128)(2,1)S(1)}, u32[]{:S(2)}, u32[]{:S(2)}) collective-permute-start(bf16[4,12,64,128]{3,2,1,0:T(8,128)(2,1)S(1)} %copy-done.12), channel_id=1, source_target_pairs={{0,64},{32,96},{64,0},{96,32},{1,65},{33,97},{65,1},{97,33},{2,66}... | collective-permute-start | bytes 2359304 | tf_op jit(solution)/shard_map/ppermute | solution.py:41
  146.3 18.8 %collective-permute-start.25 = (bf16[4,12,64,128]{3,2,1,0:T(8,128)(2,1)S(1)}, bf16[4,12,64,128]{3,2,1,0:T(8,128)(2,1)S(1)}, u32[]{:S(2)}, u32[]{:S(2)}) collective-permute-start(bf16[4,12,64,128]{3,2,1,0:T(8,128)(2,1)S(1)} %copy-done.11), channel_id=1, source_target_pairs={{0,96},{32,0},{64,32},{96,64},{1,97},{33,1},{65,33},{97,65},{2,98}... | collective-permute-start | bytes 2359304 | tf_op jit(solution)/shard_map/ppermute | solution.py:41
  148.2 20.4 %copy-start.5 = (bf16[4,512,512]{2,1,0:T(8,128)(2,1)S(1)}, bf16[4,512,512]{2,1,0:T(8,128)(2,1)}, u32[]{:S(2)}) copy-start(bf16[4,512,512]{2,1,0:T(8,128)(2,1)} %get-tuple-element.28) | copy-start | bytes 6291460
  148.3 21.1 %collective-permute-start.20 = (bf16[12,64,128]{2,1,0:T(8,128)(2,1)S(1)}, bf16[12,64,128]{2,1,0:T(8,128)(2,1)S(1)}, u32[]{:S(2)}, u32[]{:S(2)}) collective-permute-start(bf16[12,64,128]{2,1,0:T(8,128)(2,1)S(1)} %get-tuple-element.49), channel_id=1, source_target_pairs={{0,32},{32,64},{64,96},{96,0},{1,33},{33,65},{65,97},{97,1},{2,34}... | collective-permute-start | bytes 589832 | tf_op jit(solution)/shard_map/ppermute | solution.py:41
  148.4 21.1 %collective-permute-start.21 = (bf16[12,64,128]{2,1,0:T(8,128)(2,1)S(1)}, bf16[12,64,128]{2,1,0:T(8,128)(2,1)S(1)}, u32[]{:S(2)}, u32[]{:S(2)}) collective-permute-start(bf16[12,64,128]{2,1,0:T(8,128)(2,1)S(1)} %get-tuple-element.51), channel_id=1, source_target_pairs={{0,64},{32,96},{64,0},{96,32},{1,65},{33,97},{65,1},{97,33},{2,66}... | collective-permute-start | bytes 589832 | tf_op jit(solution)/shard_map/ppermute | solution.py:41
  149.5 24.0 %collective-permute-start.22 = (bf16[12,64,128]{2,1,0:T(8,128)(2,1)S(1)}, bf16[12,64,128]{2,1,0:T(8,128)(2,1)S(1)}, u32[]{:S(2)}, u32[]{:S(2)}) collective-permute-start(bf16[12,64,128]{2,1,0:T(8,128)(2,1)S(1)} %get-tuple-element.50), channel_id=1, source_target_pairs={{0,96},{32,0},{64,32},{96,64},{1,97},{33,1},{65,33},{97,65},{2,98}... | collective-permute-start | bytes 589832 | tf_op jit(solution)/shard_map/ppermute | solution.py:41
  165.5 11.0 %collective-permute-start.26 = (bf16[12,64,128]{2,1,0:T(8,128)(2,1)S(1)}, bf16[12,64,128]{2,1,0:T(8,128)(2,1)S(1)}, u32[]{:S(2)}, u32[]{:S(2)}) collective-permute-start(bf16[12,64,128]{2,1,0:T(8,128)(2,1)S(1)} %get-tuple-element.46), channel_id=1, source_target_pairs={{0,8},{8,16},{16,24},{24,0},{1,9},{9,17},{17,25},{25,1},{2,10},{10... | collective-permute-start | bytes 589832 | tf_op jit(solution)/shard_map/ppermute | solution.py:41
  165.8 12.3 %collective-permute-start.27 = (bf16[12,64,128]{2,1,0:T(8,128)(2,1)S(1)}, bf16[12,64,128]{2,1,0:T(8,128)(2,1)S(1)}, u32[]{:S(2)}, u32[]{:S(2)}) collective-permute-start(bf16[12,64,128]{2,1,0:T(8,128)(2,1)S(1)} %get-tuple-element.48), channel_id=1, source_target_pairs={{0,16},{8,24},{16,0},{24,8},{1,17},{9,25},{17,1},{25,9},{2,18},{10... | collective-permute-start | bytes 589832 | tf_op jit(solution)/shard_map/ppermute | solution.py:41
  168.7 9.4 %copy-start.3 = (f32[12,64,128]{2,1,0:T(8,128)S(1)}, f32[12,64,128]{2,1,0:T(8,128)}, u32[]{:S(2)}) copy-start(f32[12,64,128]{2,1,0:T(8,128)} %param.8) | copy-start | bytes 1179652
  169.4 8.7 %collective-permute-start.28 = (bf16[12,64,128]{2,1,0:T(8,128)(2,1)S(1)}, bf16[12,64,128]{2,1,0:T(8,128)(2,1)S(1)}, u32[]{:S(2)}, u32[]{:S(2)}) collective-permute-start(bf16[12,64,128]{2,1,0:T(8,128)(2,1)S(1)} %get-tuple-element.47), channel_id=1, source_target_pairs={{0,24},{8,0},{16,8},{24,16},{1,25},{9,1},{17,9},{25,17},{2,26},{10... | collective-permute-start | bytes 589832 | tf_op jit(solution)/shard_map/ppermute | solution.py:41
  169.5 9.6 %collective-permute-start.14 = (bf16[512,512]{1,0:T(8,128)(2,1)S(1)}, bf16[512,512]{1,0:T(8,128)(2,1)S(1)}, u32[]{:S(2)}, u32[]{:S(2)}) collective-permute-start(bf16[512,512]{1,0:T(8,128)(2,1)S(1)} %get-tuple-element.31), channel_id=1, source_target_pairs={{0,2},{2,4},{4,6},{6,0},{1,3},{3,5},{5,7},{7,1},{8,10},{10,12},{12... | collective-permute-start | bytes 1572872 | tf_op jit(solution)/shard_map/ppermute | solution.py:41
  173.5 16.9 %collective-permute-start.15 = (bf16[512,512]{1,0:T(8,128)(2,1)S(1)}, bf16[512,512]{1,0:T(8,128)(2,1)S(1)}, u32[]{:S(2)}, u32[]{:S(2)}) collective-permute-start(bf16[512,512]{1,0:T(8,128)(2,1)S(1)} %get-tuple-element.32), channel_id=1, source_target_pairs={{0,4},{2,6},{4,0},{6,2},{1,5},{3,7},{5,1},{7,3},{8,12},{10,14},{12... | collective-permute-start | bytes 1572872 | tf_op jit(solution)/shard_map/ppermute | solution.py:41
  176.5 22.9 %collective-permute-start.16 = (bf16[512,512]{1,0:T(8,128)(2,1)S(1)}, bf16[512,512]{1,0:T(8,128)(2,1)S(1)}, u32[]{:S(2)}, u32[]{:S(2)}) collective-permute-start(bf16[512,512]{1,0:T(8,128)(2,1)S(1)} %get-tuple-element.33), channel_id=1, source_target_pairs={{0,6},{2,0},{4,2},{6,4},{1,7},{3,1},{5,3},{7,5},{8,14},{10,8},{12,... | collective-permute-start | bytes 1572872 | tf_op jit(solution)/shard_map/ppermute | solution.py:41

commit v5 on v4

--- a/solution.py
+++ b/solution.py
@@ -45,10 +45,6 @@
     return [sent(value, axis, k) for k in range(1, RING)]
 
 
-def steps_sent(values, axis):
-    return [values[0]] + [sent(values[k], axis, k) for k in range(1, RING)]
-
-
 def gather(pieces, paths):
     blocks = [jnp.stack([p] + steps_of(p, path[0])) for p, path in zip(pieces, paths)]
     return [[b] + steps_of(b, path[1]) for b, path in zip(blocks, paths)]
@@ -109,6 +105,7 @@
 
 EARLY_GROUPS, MIDDLE_GROUPS, LATE_GROUPS = 4, 2, 4
 SIGMA_PARTS = 5
+SLOTS = ((0, 0), (2, 1), (1, 3), (3, 2))
 
 
 def issue(copies):
@@ -357,12 +354,17 @@
     w = away_out.shape[2]
     core = place[PLACE["core"]]
     ends = []
+    mid = tok.shape[0] // 2
     for side, (ref, half) in enumerate(((away_out, 1 - core), (home_out, core))):
         for k in range(RING):
             y = (place[PLACE["y"]] + k) & 3
             both[side, k] = acc[:, pl.ds(pl.multiple_of((y * 2 + half) * w, w), w)].astype(bf16)
-            ends.append(pltpu.make_async_copy(both.at[side, k], ref.at[k], s_one.at[1 + side * RING + k]))
-            ends[-1].start()
+            for slot in range(RING):
+                for part in range(2):
+                    if SLOTS[slot][part] == k:
+                        r = slice(part * mid, (part + 1) * mid)
+                        pltpu.make_async_copy(both.at[side, k, r], ref.at[slot, r], s_one.at[1 + side]).start()
+        ends.append(pltpu.make_async_copy(both.at[side], both.at[side], s_one.at[1 + side]))
     for c in [save(g) for g in range(LATE_GROUPS)] + ends:
         c.wait()
 
@@ -417,8 +419,14 @@
     came = sent(away, "core", 1)
     pairs = [(home[k].astype(f32) + came[k].astype(f32)).astype(bf16) for k in range(RING)]
     pairs = lax.optimization_barrier(pairs)
-    arrived = steps_sent(pairs, "y")
-    grad_tokens = total_of(arrived)
+    mid = home.shape[1] // 2
+    below, above = sent(pairs[1], "y", 1), sent(pairs[3], "y", RING - 1)
+    up = (pairs[2][:mid].astype(f32) + below[:mid].astype(f32)).astype(bf16)
+    down = (pairs[2][mid:].astype(f32) + above[mid:].astype(f32)).astype(bf16)
+    below_far, above_far = sent(up, "y", 1), sent(down, "y", RING - 1)
+    top = total_of([pairs[0][:mid], below_far, above[:mid]])
+    bottom = total_of([pairs[0][mid:], below[mid:], above_far])
+    grad_tokens = jnp.concatenate([top, bottom], axis=0)
     return (output, grad_tokens, grad_theta, grad_logvar)
 
 

time: 201 us -> 197 us (0.980)
  waiting for transfers between devices: 101 us -> 95.3 us
    ppermute x29 -> x30, waiting for transfers between devices: 101 us -> 95.3 us  [sent(): return lax.ppermute(value, axis, [(i, (i + step) % n) for i in range(n)])]
    ppermute x29 -> x30, starting transfers between devices: 39.7 us -> 40.2 us  [sent(): return lax.ppermute(value, axis, [(i, (i + step) % n) for i in range(n)])]
  transfers between devices with their start and end apart: 29 -> 30, of which waited for: 12 -> 13; matrix products, arithmetic and copies ran while one was open for 3% -> 3% of each run, Pallas kernels for 13% -> 13%
where the time goes in v5:
time: 197 us; the launch traced here: 195 us
  waiting for transfers between devices  95.3 us (48%)
  Pallas kernels  49 us (25%)
  starting transfers between devices  40.2 us (20%)
  other arithmetic  7.18 us (4%)
  local copies, waits for them, and re-layouts  2.56 us (1%)
    ppermute x30, waiting for transfers between devices, sent(): return lax.ppermute(value, axis, [(i, (i + step) % n) for i in range(n)])  95.3 us
    ppermute x30, starting transfers between devices, sent(): return lax.ppermute(value, axis, [(i, (i + step) % n) for i in range(n)])  40.2 us
    pallas_call x1, Pallas kernels, late(): pl.pallas_call(late_kernel, out_shape=shapes, in_specs=[SM] + [HB] * (4 +...  23.5 us
    pallas_call x1, Pallas kernels, middle(): pl.pallas_call(middle_kernel, out_shape=shapes, in_specs=[SM, HB, HB, HB,...  14.8 us
    pallas_call x1, Pallas kernels, early(): pl.pallas_call(early_kernel, out_shape=shapes, in_specs=[SM, VB, VB], out...  10.7 us
  transfers between devices with their start and end apart: 30, of which 13 were waited for; matrix products, arithmetic and copies ran while one was open for 3% of the time, Pallas kernels for 13%

profile of v5, /device:TPU:1, one launch (start us, length us, event | category | flops | bytes accessed | tf_op | source)
XLA Modules:
  0.0 195.2 jit_solution(14359422999999174152)
XLA Ops:
  0.6 1.1 exponential_convert_fusion
  1.7 2.1 %collective-permute-start = (bf16[12,64,128]{2,1,0:T(8,128)(2,1)S(1)}, bf16[12,64,128]{2,1,0:T(8,128)(2,1)S(1)}, u32[]{:S(2)}, u32[]{:S(2)}) collective-permute-start(bf16[12,64,128]{2,1,0:T(8,128)(2,1)S(1)} %exponential_convert_fusion), channel_id=1, source_target_pairs={{0,8},{8,16},{16,24},{24,0},{1,9},{9,17},{17,25},{25,1},{2,10},{10... | collective-permute-start | bytes 589832 | tf_op jit(solution)/shard_map/ppermute | solution.py:41
  3.8 2.5 %collective-permute-start.1 = (bf16[12,64,128]{2,1,0:T(8,128)(2,1)S(1)}, bf16[12,64,128]{2,1,0:T(8,128)(2,1)S(1)}, u32[]{:S(2)}, u32[]{:S(2)}) collective-permute-start(bf16[12,64,128]{2,1,0:T(8,128)(2,1)S(1)} %exponential_convert_fusion), channel_id=1, source_target_pairs={{0,16},{8,24},{16,0},{24,8},{1,17},{9,25},{17,1},{25,9},{2,18},{10... | collective-permute-start | bytes 589832 | tf_op jit(solution)/shard_map/ppermute | solution.py:41
  6.3 1.2 collective-permute-start.2
  7.4 1.1 fusion.19
  8.5 0.8 collective-permute-done
  9.3 5.5 %collective-permute-done.1 = bf16[12,64,128]{2,1,0:T(8,128)(2,1)S(1)} collective-permute-done((bf16[12,64,128]{2,1,0:T(8,128)(2,1)S(1)}, bf16[12,64,128]{2,1,0:T(8,128)(2,1)S(1)}, u32[]{:S(2)}, u32[]{:S(2)}) %collective-permute-start.1) | collective-permute-done | bytes 196640 | tf_op jit(solution)/shard_map/ppermute | solution.py:41
  14.9 1.7 collective-permute-start.3
  16.6 2.2 %collective-permute-start.5 = (bf16[4,12,64,128]{3,2,1,0:T(8,128)(2,1)S(1)}, bf16[4,12,64,128]{3,2,1,0:T(8,128)(2,1)S(1)}, u32[]{:S(2)}, u32[]{:S(2)}) collective-permute-start(bf16[4,12,64,128]{3,2,1,0:T(8,128)(2,1)S(1)} %pad_maximum_fusion.1.refs_0_), channel_id=1, source_target_pairs={{0,96},{32,0},{64,32},{96,64},{1,97},{33,1},{65,33},{97,65},{2,98}... | collective-permute-start | bytes 2359304 | tf_op jit(solution)/shard_map/ppermute | solution.py:41
  18.9 2.6 %collective-permute-start.8 = (bf16[12,64,128]{2,1,0:T(8,128)(2,1)S(1)}, bf16[12,64,128]{2,1,0:T(8,128)(2,1)S(1)}, u32[]{:S(2)}, u32[]{:S(2)}) collective-permute-start(bf16[12,64,128]{2,1,0:T(8,128)(2,1)S(1)} %copy-done.10), channel_id=1, source_target_pairs={{0,64},{32,96},{64,0},{96,32},{1,65},{33,97},{65,1},{97,33},{2,66}... | collective-permute-start | bytes 589832 | tf_op jit(solution)/shard_map/ppermute | solution.py:41
  21.4 0.7 collective-permute-start.9
  22.1 17.2 %collective-permute-done.7 = bf16[12,64,128]{2,1,0:T(8,128)(2,1)S(1)} collective-permute-done((bf16[12,64,128]{2,1,0:T(8,128)(2,1)S(1)}, bf16[12,64,128]{2,1,0:T(8,128)(2,1)S(1)}, u32[]{:S(2)}, u32[]{:S(2)}) %collective-permute-start.7) | collective-permute-done | bytes 196640 | tf_op jit(solution)/shard_map/ppermute | solution.py:41
  39.4 5.1 %collective-permute-done.8 = bf16[12,64,128]{2,1,0:T(8,128)(2,1)S(1)} collective-permute-done((bf16[12,64,128]{2,1,0:T(8,128)(2,1)S(1)}, bf16[12,64,128]{2,1,0:T(8,128)(2,1)S(1)}, u32[]{:S(2)}, u32[]{:S(2)}) %collective-permute-start.8) | collective-permute-done | bytes 196640 | tf_op jit(solution)/shard_map/ppermute | solution.py:41
  44.6 1.8 collective-permute-start.10
  46.4 2.9 %collective-permute-start.11 = (bf16[4,12,64,128]{3,2,1,0:T(8,128)(2,1)S(1)}, bf16[4,12,64,128]{3,2,1,0:T(8,128)(2,1)}, u32[]{:S(2)}, u32[]{:S(2)}) collective-permute-start(bf16[4,12,64,128]{3,2,1,0:T(8,128)(2,1)S(1)} %pad_maximum_fusion.2.refs_5_), channel_id=1, source_target_pairs={{0,16},{8,24},{16,0},{24,8},{1,17},{9,25},{17,1},{25,9},{2,18},{10... | collective-permute-start | bytes 2359304 | tf_op jit(solution)/shard_map/ppermute | solution.py:41
  49.4 0.8 slice.200
  50.2 0.8 slice.201
  51.0 2.7 %collective-permute-start.6 = (bf16[2,12,64,128]{3,2,1,0:T(8,128)(2,1)}, bf16[2,12,64,128]{3,2,1,0:T(8,128)(2,1)S(1)}, u32[]{:S(2)}, u32[]{:S(2)}) collective-permute-start(bf16[2,12,64,128]{3,2,1,0:T(8,128)(2,1)} %slice.201), channel_id=1, source_target_pairs={{0,96},{32,0},{64,32},{96,64},{1,97},{33,1},{65,33},{97,65},{2,98}... | collective-permute-start | bytes 1179656 | tf_op jit(solution)/shard_map/ppermute | solution.py:41
  53.7 10.7 %early.1 = (bf16[4,12,64,128]{3,2,1,0:T(8,128)(2,1)}, bf16[4,12,64,128]{3,2,1,0:T(8,128)(2,1)}, bf16[4,12,64,128]{3,2,1,0:T(8,128)(2,1)}, bf16[4,12,64,128]{3,2,...) custom-call(s32[8,12]{1,0:T(8,128)} %bitcast.47, bf16[512,4096]{1,0:T(8,128)(2,1)} %tok_in.1, ...), custom_call_target="tpu_custom_call" | custom-call | tf_op jit(solution)/shard_map/early/pallas_call | solution.py:184
  64.5 0.7 copy-done.6
  65.4 14.8 %middle.1 = (bf16[4,12,64,128]{3,2,1,0:T(8,128)(2,1)}, bf16[4,12,64,128]{3,2,1,0:T(8,128)(2,1)}, bf16[4,12,64,128]{3,2,1,0:T(8,128)(2,1)}, bf16[4,12,64,128]{3,2...) custom-call(s32[8,12]{1,0:T(8,128)} %bitcast.48, bf16[512,4096]{1,0:T(8,128)(2,1)} %get-tuple-element.23.sq_in, ...), custom_call_target="tpu_custom_call" | custom-call | tf_op jit(solution)/shard_map/middle/pallas_call | solution.py:274
  80.1 2.2 %collective-permute-done.11.refs_7_ = bf16[4,12,64,128]{3,2,1,0:T(8,128)(2,1)} collective-permute-done((bf16[4,12,64,128]{3,2,1,0:T(8,128)(2,1)S(1)}, bf16[4,12,64,128]{3,2,1,0:T(8,128)(2,1)}, u32[]{:S(2)}, u32[]{:S(2)}) %collective-permute-start.11) | collective-permute-done | bytes 786464 | tf_op jit(solution)/shard_map/ppermute | solution.py:41
  82.3 0.4 collective-permute-done.12.refs_8_
  82.7 23.5 %late.1 = (bf16[512,1536]{1,0:T(8,128)(2,1)}, bf16[4,512,512]{2,1,0:T(8,128)(2,1)}, bf16[4,512,512]{2,1,0:T(8,128)(2,1)}) custom-call(s32[8,12]{1,0:T(8,128)} %bitcast.49, bf16[512,4096]{1,0:T(8,128)(2,1)} %tok_in.1, bf16[512,1536]{1,0:T(8,128)(2,1)} %cot_in.3, bf16[512,1536]{1,0:T(8,128)(2,1)} %get-tuple-element.25.gv_in, ...), custom_call_target="tpu_custom_call" | custom-call | tf_op jit(solution)/shard_map/late/pallas_call | solution.py:378
  106.2 2.4 %collective-permute-start.13 = (bf16[4,512,512]{2,1,0:T(8,128)(2,1)}, bf16[4,512,512]{2,1,0:T(8,128)(2,1)S(1)}, u32[]{:S(2)}, u32[]{:S(2)}) collective-permute-start(bf16[4,512,512]{2,1,0:T(8,128)(2,1)} %get-tuple-element.29), channel_id=1, source_target_pairs={{0,1},{1,0},{2,3},{3,2},{4,5},{5,4},{6,7},{7,6},{8,9},{9,8},{10,11... | collective-permute-start | bytes 6291464 | tf_op jit(solution)/shard_map/ppermute | solution.py:41
  108.8 2.9 %collective-permute-start.19 = (bf16[4,12,64,128]{3,2,1,0:T(8,128)(2,1)}, bf16[4,12,64,128]{3,2,1,0:T(8,128)(2,1)S(1)}, u32[]{:S(2)}, u32[]{:S(2)}) collective-permute-start(bf16[4,12,64,128]{3,2,1,0:T(8,128)(2,1)} %get-tuple-element.36), channel_id=1, source_target_pairs={{0,16},{8,24},{16,0},{24,8},{1,17},{9,25},{17,1},{25,9},{2,18},{10... | collective-permute-start | bytes 2359304 | tf_op jit(solution)/shard_map/ppermute | solution.py:41
  111.8 17.3 %collective-permute-done.18 = bf16[4,12,64,128]{3,2,1,0:T(8,128)(2,1)S(1)} collective-permute-done((bf16[4,12,64,128]{3,2,1,0:T(8,128)(2,1)}, bf16[4,12,64,128]{3,2,1,0:T(8,128)(2,1)S(1)}, u32[]{:S(2)}, u32[]{:S(2)}) %collective-permute-start.18) | collective-permute-done | bytes 786464 | tf_op jit(solution)/shard_map/ppermute | solution.py:41
  129.1 1.2 collective-permute-start.25
  130.3 16.0 %collective-permute-done.19 = bf16[4,12,64,128]{3,2,1,0:T(8,128)(2,1)S(1)} collective-permute-done((bf16[4,12,64,128]{3,2,1,0:T(8,128)(2,1)}, bf16[4,12,64,128]{3,2,1,0:T(8,128)(2,1)S(1)}, u32[]{:S(2)}, u32[]{:S(2)}) %collective-permute-start.19) | collective-permute-done | bytes 786464 | tf_op jit(solution)/shard_map/ppermute | solution.py:41
  146.3 1.6 collective-permute-start.26
  147.9 0.4 fusion.12
  148.3 6.4 %collective-permute-done.21 = bf16[12,64,128]{2,1,0:T(8,128)(2,1)S(1)} collective-permute-done((bf16[12,64,128]{2,1,0:T(8,128)(2,1)S(1)}, bf16[12,64,128]{2,1,0:T(8,128)(2,1)S(1)}, u32[]{:S(2)}, u32[]{:S(2)}) %collective-permute-start.21) | collective-permute-done | bytes 196640 | tf_op jit(solution)/shard_map/ppermute | solution.py:41
  154.8 1.3 collective-permute-start.23
  156.1 0.7 fusion.3
  156.8 4.0 %collective-permute-done.22 = bf16[12,64,128]{2,1,0:T(8,128)(2,1)S(1)} collective-permute-done((bf16[12,64,128]{2,1,0:T(8,128)(2,1)S(1)}, bf16[12,64,128]{2,1,0:T(8,128)(2,1)S(1)}, u32[]{:S(2)}, u32[]{:S(2)}) %collective-permute-start.22) | collective-permute-done | bytes 196640 | tf_op jit(solution)/shard_map/ppermute | solution.py:41
  160.8 1.2 collective-permute-start.14
  162.0 11.5 %collective-permute-done.23 = bf16[12,64,128]{2,1,0:T(8,128)(2,1)S(1)} collective-permute-done((bf16[12,64,128]{2,1,0:T(8,128)(2,1)S(1)}, bf16[12,64,128]{2,1,0:T(8,128)(2,1)S(1)}, u32[]{:S(2)}, u32[]{:S(2)}) %collective-permute-start.23) | collective-permute-done | bytes 196640 | tf_op jit(solution)/shard_map/ppermute | solution.py:41
  173.5 2.7 %collective-permute-start.16 = (bf16[512,512]{1,0:T(8,128)(2,1)S(1)}, bf16[512,512]{1,0:T(8,128)(2,1)S(1)}, u32[]{:S(2)}, u32[]{:S(2)}) collective-permute-start(bf16[512,512]{1,0:T(8,128)(2,1)S(1)} %get-tuple-element.33), channel_id=1, source_target_pairs={{0,6},{2,0},{4,2},{6,4},{1,7},{3,1},{5,3},{7,5},{8,14},{10,8},{12,... | collective-permute-start | bytes 1572872 | tf_op jit(solution)/shard_map/ppermute | solution.py:41
  176.2 1.0 fusion.10
  177.2 0.4 fusion.16
  177.7 1.8 collective-permute-start.28
  179.5 0.9 collective-permute-start.29
  180.4 5.6 %collective-permute-done.16 = bf16[512,512]{1,0:T(8,128)(2,1)S(1)} collective-permute-done((bf16[512,512]{1,0:T(8,128)(2,1)S(1)}, bf16[512,512]{1,0:T(8,128)(2,1)S(1)}, u32[]{:S(2)}, u32[]{:S(2)}) %collective-permute-start.16) | collective-permute-done | bytes 524320 | tf_op jit(solution)/shard_map/ppermute | solution.py:41
  186.1 0.8 collective-permute-start.15
  186.9 2.8 %collective-permute-start.17 = (bf16[256,512]{1,0:T(8,128)(2,1)S(1)}, bf16[256,512]{1,0:T(8,128)(2,1)S(1)}, u32[]{:S(2)}, u32[]{:S(2)}) collective-permute-start(bf16[256,512]{1,0:T(8,128)(2,1)S(1)} %get-tuple-element.55), channel_id=1, source_target_pairs={{0,6},{2,0},{4,2},{6,4},{1,7},{3,1},{5,3},{7,5},{8,14},{10,8},{12,... | collective-permute-start | bytes 786440 | tf_op jit(solution)/shard_map/ppermute | solution.py:41
  189.7 1.0 fusion.7
  190.7 3.2 %collective-permute-done.15 = bf16[256,512]{1,0:T(8,128)(2,1)S(1)} collective-permute-done((bf16[256,512]{1,0:T(8,128)(2,1)S(1)}, bf16[256,512]{1,0:T(8,128)(2,1)S(1)}, u32[]{:S(2)}, u32[]{:S(2)}) %collective-permute-start.15) | collective-permute-done | bytes 262176 | tf_op jit(solution)/shard_map/ppermute | solution.py:41
  194.1 1.0 pad_maximum_fusion
  (59 shorter events, 1.1 us)
Async XLA Ops:
  0.6 18.2 %copy-start.10 = (bf16[12,64,128]{2,1,0:T(8,128)(2,1)S(1)}, bf16[12,64,128]{2,1,0:T(8,128)(2,1)}, u32[]{:S(2)}) copy-start(bf16[12,64,128]{2,1,0:T(8,128)(2,1)} %param.7) | copy-start | bytes 589828
  1.7 7.6 %collective-permute-start = (bf16[12,64,128]{2,1,0:T(8,128)(2,1)S(1)}, bf16[12,64,128]{2,1,0:T(8,128)(2,1)S(1)}, u32[]{:S(2)}, u32[]{:S(2)}) collective-permute-start(bf16[12,64,128]{2,1,0:T(8,128)(2,1)S(1)} %exponential_convert_fusion), channel_id=1, source_target_pairs={{0,8},{8,16},{16,24},{24,0},{1,9},{9,17},{17,25},{25,1},{2,10},{10... | collective-permute-start | bytes 589832 | tf_op jit(solution)/shard_map/ppermute | solution.py:41
  3.8 11.0 %collective-permute-start.1 = (bf16[12,64,128]{2,1,0:T(8,128)(2,1)S(1)}, bf16[12,64,128]{2,1,0:T(8,128)(2,1)S(1)}, u32[]{:S(2)}, u32[]{:S(2)}) collective-permute-start(bf16[12,64,128]{2,1,0:T(8,128)(2,1)S(1)} %exponential_convert_fusion), channel_id=1, source_target_pairs={{0,16},{8,24},{16,0},{24,8},{1,17},{9,25},{17,1},{25,9},{2,18},{10... | collective-permute-start | bytes 589832 | tf_op jit(solution)/shard_map/ppermute | solution.py:41
  6.3 8.5 %collective-permute-start.2 = (bf16[12,64,128]{2,1,0:T(8,128)(2,1)S(1)}, bf16[12,64,128]{2,1,0:T(8,128)(2,1)S(1)}, u32[]{:S(2)}, u32[]{:S(2)}) collective-permute-start(bf16[12,64,128]{2,1,0:T(8,128)(2,1)S(1)} %exponential_convert_fusion), channel_id=1, source_target_pairs={{0,24},{8,0},{16,8},{24,16},{1,25},{9,1},{17,9},{25,17},{2,26},{10... | collective-permute-start | bytes 589832 | tf_op jit(solution)/shard_map/ppermute | solution.py:41
  14.9 49.5 %copy-start = (bf16[4,12,64,128]{3,2,1,0:T(8,128)(2,1)}, bf16[4,12,64,128]{3,2,1,0:T(8,128)(2,1)S(1)}, u32[]{:S(2)}) copy-start(bf16[4,12,64,128]{3,2,1,0:T(8,128)(2,1)S(1)} %pad_maximum_fusion.1.refs_0_) | copy-start | bytes 2359300
  14.9 34.4 %collective-permute-start.3 = (bf16[4,12,64,128]{3,2,1,0:T(8,128)(2,1)S(1)}, bf16[4,12,64,128]{3,2,1,0:T(8,128)(2,1)S(1)}, u32[]{:S(2)}, u32[]{:S(2)}) collective-permute-start(bf16[4,12,64,128]{3,2,1,0:T(8,128)(2,1)S(1)} %pad_maximum_fusion.1.refs_0_), channel_id=1, source_target_pairs={{0,32},{32,64},{64,96},{96,0},{1,33},{33,65},{65,97},{97,1},{2,34}... | collective-permute-start | bytes 2359304 | tf_op jit(solution)/shard_map/ppermute | solution.py:41
  16.6 33.6 %collective-permute-start.5 = (bf16[4,12,64,128]{3,2,1,0:T(8,128)(2,1)S(1)}, bf16[4,12,64,128]{3,2,1,0:T(8,128)(2,1)S(1)}, u32[]{:S(2)}, u32[]{:S(2)}) collective-permute-start(bf16[4,12,64,128]{3,2,1,0:T(8,128)(2,1)S(1)} %pad_maximum_fusion.1.refs_0_), channel_id=1, source_target_pairs={{0,96},{32,0},{64,32},{96,64},{1,97},{33,1},{65,33},{97,65},{2,98}... | collective-permute-start | bytes 2359304 | tf_op jit(solution)/shard_map/ppermute | solution.py:41
  18.9 20.5 %collective-permute-start.7 = (bf16[12,64,128]{2,1,0:T(8,128)(2,1)S(1)}, bf16[12,64,128]{2,1,0:T(8,128)(2,1)S(1)}, u32[]{:S(2)}, u32[]{:S(2)}) collective-permute-start(bf16[12,64,128]{2,1,0:T(8,128)(2,1)S(1)} %copy-done.10), channel_id=1, source_target_pairs={{0,32},{32,64},{64,96},{96,0},{1,33},{33,65},{65,97},{97,1},{2,34}... | collective-permute-start | bytes 589832 | tf_op jit(solution)/shard_map/ppermute | solution.py:41
  18.9 25.6 %collective-permute-start.8 = (bf16[12,64,128]{2,1,0:T(8,128)(2,1)S(1)}, bf16[12,64,128]{2,1,0:T(8,128)(2,1)S(1)}, u32[]{:S(2)}, u32[]{:S(2)}) collective-permute-start(bf16[12,64,128]{2,1,0:T(8,128)(2,1)S(1)} %copy-done.10), channel_id=1, source_target_pairs={{0,64},{32,96},{64,0},{96,32},{1,65},{33,97},{65,1},{97,33},{2,66}... | collective-permute-start | bytes 589832 | tf_op jit(solution)/shard_map/ppermute | solution.py:41
  21.4 23.1 %collective-permute-start.9 = (bf16[12,64,128]{2,1,0:T(8,128)(2,1)S(1)}, bf16[12,64,128]{2,1,0:T(8,128)(2,1)S(1)}, u32[]{:S(2)}, u32[]{:S(2)}) collective-permute-start(bf16[12,64,128]{2,1,0:T(8,128)(2,1)S(1)} %copy-done.10), channel_id=1, source_target_pairs={{0,96},{32,0},{64,32},{96,64},{1,97},{33,1},{65,33},{97,65},{2,98}... | collective-permute-start | bytes 589832 | tf_op jit(solution)/shard_map/ppermute | solution.py:41
  44.6 19.9 %copy-start.4 = (bf16[4,12,64,128]{3,2,1,0:T(8,128)(2,1)}, bf16[4,12,64,128]{3,2,1,0:T(8,128)(2,1)S(1)}, u32[]{:S(2)}) copy-start(bf16[4,12,64,128]{3,2,1,0:T(8,128)(2,1)S(1)} %pad_maximum_fusion.2.refs_5_) | copy-start | bytes 2359300
  44.6 35.5 %collective-permute-start.10 = (bf16[4,12,64,128]{3,2,1,0:T(8,128)(2,1)S(1)}, bf16[4,12,64,128]{3,2,1,0:T(8,128)(2,1)}, u32[]{:S(2)}, u32[]{:S(2)}) collective-permute-start(bf16[4,12,64,128]{3,2,1,0:T(8,128)(2,1)S(1)} %pad_maximum_fusion.2.refs_5_), channel_id=1, source_target_pairs={{0,8},{8,16},{16,24},{24,0},{1,9},{9,17},{17,25},{25,1},{2,10},{10... | collective-permute-start | bytes 2359304 | tf_op jit(solution)/shard_map/ppermute | solution.py:41
  46.4 35.9 %collective-permute-start.11 = (bf16[4,12,64,128]{3,2,1,0:T(8,128)(2,1)S(1)}, bf16[4,12,64,128]{3,2,1,0:T(8,128)(2,1)}, u32[]{:S(2)}, u32[]{:S(2)}) collective-permute-start(bf16[4,12,64,128]{3,2,1,0:T(8,128)(2,1)S(1)} %pad_maximum_fusion.2.refs_5_), channel_id=1, source_target_pairs={{0,16},{8,24},{16,0},{24,8},{1,17},{9,25},{17,1},{25,9},{2,18},{10... | collective-permute-start | bytes 2359304 | tf_op jit(solution)/shard_map/ppermute | solution.py:41
  49.4 33.3 %collective-permute-start.12 = (bf16[4,12,64,128]{3,2,1,0:T(8,128)(2,1)S(1)}, bf16[4,12,64,128]{3,2,1,0:T(8,128)(2,1)}, u32[]{:S(2)}, u32[]{:S(2)}) collective-permute-start(bf16[4,12,64,128]{3,2,1,0:T(8,128)(2,1)S(1)} %pad_maximum_fusion.2.refs_5_), channel_id=1, source_target_pairs={{0,24},{8,0},{16,8},{24,16},{1,25},{9,1},{17,9},{25,17},{2,26},{10... | collective-permute-start | bytes 2359304 | tf_op jit(solution)/shard_map/ppermute | solution.py:41
  49.4 15.1 %copy-start.1 = (bf16[4,12,64,128]{3,2,1,0:T(8,128)(2,1)}, bf16[4,12,64,128]{3,2,1,0:T(8,128)(2,1)S(1)}, u32[]{:S(2)}) copy-start(bf16[4,12,64,128]{3,2,1,0:T(8,128)(2,1)S(1)} %collective-permute-done.3.refs_1_) | copy-start | bytes 2359300
  50.2 14.3 %collective-permute-start.4 = (bf16[2,12,64,128]{3,2,1,0:T(8,128)(2,1)}, bf16[2,12,64,128]{3,2,1,0:T(8,128)(2,1)S(1)}, u32[]{:S(2)}, u32[]{:S(2)}) collective-permute-start(bf16[2,12,64,128]{3,2,1,0:T(8,128)(2,1)} %slice.200), channel_id=1, source_target_pairs={{0,32},{32,64},{64,96},{96,0},{1,33},{33,65},{65,97},{97,1},{2,34}... | collective-permute-start | bytes 1179656 | tf_op jit(solution)/shard_map/ppermute | solution.py:41
  50.2 14.2 %copy-start.2 = (bf16[4,12,64,128]{3,2,1,0:T(8,128)(2,1)}, bf16[4,12,64,128]{3,2,1,0:T(8,128)(2,1)S(1)}, u32[]{:S(2)}) copy-start(bf16[4,12,64,128]{3,2,1,0:T(8,128)(2,1)S(1)} %collective-permute-done.5.refs_4_) | copy-start | bytes 2359300
  51.0 13.5 %collective-permute-start.6 = (bf16[2,12,64,128]{3,2,1,0:T(8,128)(2,1)}, bf16[2,12,64,128]{3,2,1,0:T(8,128)(2,1)S(1)}, u32[]{:S(2)}, u32[]{:S(2)}) collective-permute-start(bf16[2,12,64,128]{3,2,1,0:T(8,128)(2,1)} %slice.201), channel_id=1, source_target_pairs={{0,96},{32,0},{64,32},{96,64},{1,97},{33,1},{65,33},{97,65},{2,98}... | collective-permute-start | bytes 1179656 | tf_op jit(solution)/shard_map/ppermute | solution.py:41
  64.5 0.7 copy-start.6
  64.5 0.9 copy-start.7
  82.7 29.0 %copy-start.14 = (bf16[4,12,64,128]{3,2,1,0:T(8,128)(2,1)S(1)}, bf16[4,12,64,128]{3,2,1,0:T(8,128)(2,1)}, u32[]{:S(2)}) copy-start(bf16[4,12,64,128]{3,2,1,0:T(8,128)(2,1)} %get-tuple-element.37) | copy-start | bytes 2359300
  82.7 29.0 %copy-start.13 = (bf16[4,12,64,128]{3,2,1,0:T(8,128)(2,1)S(1)}, bf16[4,12,64,128]{3,2,1,0:T(8,128)(2,1)}, u32[]{:S(2)}) copy-start(bf16[4,12,64,128]{3,2,1,0:T(8,128)(2,1)} %get-tuple-element.39) | copy-start | bytes 2359300
  82.7 46.4 %copy-start.12 = (bf16[4,12,64,128]{3,2,1,0:T(8,128)(2,1)S(1)}, bf16[4,12,64,128]{3,2,1,0:T(8,128)(2,1)}, u32[]{:S(2)}) copy-start(bf16[4,12,64,128]{3,2,1,0:T(8,128)(2,1)} %get-tuple-element.40) | copy-start | bytes 2359300
  82.7 63.6 %copy-start.11 = (bf16[4,12,64,128]{3,2,1,0:T(8,128)(2,1)S(1)}, bf16[4,12,64,128]{3,2,1,0:T(8,128)(2,1)}, u32[]{:S(2)}) copy-start(bf16[4,12,64,128]{3,2,1,0:T(8,128)(2,1)} %get-tuple-element.41) | copy-start | bytes 2359300
  82.7 65.2 %copy-start.9 = (bf16[4,12,64,128]{3,2,1,0:T(8,128)(2,1)S(1)}, bf16[4,12,64,128]{3,2,1,0:T(8,128)(2,1)}, u32[]{:S(2)}) copy-start(bf16[4,12,64,128]{3,2,1,0:T(8,128)(2,1)} %get-tuple-element.34) | copy-start | bytes 2359300
  106.2 49.9 %copy-start.5 = (bf16[4,512,512]{2,1,0:T(8,128)(2,1)S(1)}, bf16[4,512,512]{2,1,0:T(8,128)(2,1)}, u32[]{:S(2)}) copy-start(bf16[4,512,512]{2,1,0:T(8,128)(2,1)} %get-tuple-element.28) | copy-start | bytes 6291460
  106.2 48.6 %collective-permute-start.13 = (bf16[4,512,512]{2,1,0:T(8,128)(2,1)}, bf16[4,512,512]{2,1,0:T(8,128)(2,1)S(1)}, u32[]{:S(2)}, u32[]{:S(2)}) collective-permute-start(bf16[4,512,512]{2,1,0:T(8,128)(2,1)} %get-tuple-element.29), channel_id=1, source_target_pairs={{0,1},{1,0},{2,3},{3,2},{4,5},{5,4},{6,7},{7,6},{8,9},{9,8},{10,11... | collective-permute-start | bytes 6291464 | tf_op jit(solution)/shard_map/ppermute | solution.py:41
  108.6 20.4 %collective-permute-start.18 = (bf16[4,12,64,128]{3,2,1,0:T(8,128)(2,1)}, bf16[4,12,64,128]{3,2,1,0:T(8,128)(2,1)S(1)}, u32[]{:S(2)}, u32[]{:S(2)}) collective-permute-start(bf16[4,12,64,128]{3,2,1,0:T(8,128)(2,1)} %get-tuple-element.35), channel_id=1, source_target_pairs={{0,8},{8,16},{16,24},{24,0},{1,9},{9,17},{17,25},{25,1},{2,10},{10... | collective-permute-start | bytes 2359304 | tf_op jit(solution)/shard_map/ppermute | solution.py:41
  108.8 37.5 %collective-permute-start.19 = (bf16[4,12,64,128]{3,2,1,0:T(8,128)(2,1)}, bf16[4,12,64,128]{3,2,1,0:T(8,128)(2,1)S(1)}, u32[]{:S(2)}, u32[]{:S(2)}) collective-permute-start(bf16[4,12,64,128]{3,2,1,0:T(8,128)(2,1)} %get-tuple-element.36), channel_id=1, source_target_pairs={{0,16},{8,24},{16,0},{24,8},{1,17},{9,25},{17,1},{25,9},{2,18},{10... | collective-permute-start | bytes 2359304 | tf_op jit(solution)/shard_map/ppermute | solution.py:41
  111.7 36.2 %collective-permute-start.20 = (bf16[4,12,64,128]{3,2,1,0:T(8,128)(2,1)S(1)}, bf16[4,12,64,128]{3,2,1,0:T(8,128)(2,1)S(1)}, u32[]{:S(2)}, u32[]{:S(2)}) collective-permute-start(bf16[4,12,64,128]{3,2,1,0:T(8,128)(2,1)S(1)} %copy-done.14), channel_id=1, source_target_pairs={{0,24},{8,0},{16,8},{24,16},{1,25},{9,1},{17,9},{25,17},{2,26},{10... | collective-permute-start | bytes 2359304 | tf_op jit(solution)/shard_map/ppermute | solution.py:41
  111.7 65.5 %collective-permute-start.24 = (bf16[4,12,64,128]{3,2,1,0:T(8,128)(2,1)S(1)}, bf16[4,12,64,128]{3,2,1,0:T(8,128)(2,1)S(1)}, u32[]{:S(2)}, u32[]{:S(2)}) collective-permute-start(bf16[4,12,64,128]{3,2,1,0:T(8,128)(2,1)S(1)} %copy-done.13), channel_id=1, source_target_pairs={{0,32},{32,64},{64,96},{96,0},{1,33},{33,65},{65,97},{97,1},{2,34}... | collective-permute-start | bytes 2359304 | tf_op jit(solution)/shard_map/ppermute | solution.py:41
  129.1 48.1 %collective-permute-start.25 = (bf16[4,12,64,128]{3,2,1,0:T(8,128)(2,1)S(1)}, bf16[4,12,64,128]{3,2,1,0:T(8,128)(2,1)S(1)}, u32[]{:S(2)}, u32[]{:S(2)}) collective-permute-start(bf16[4,12,64,128]{3,2,1,0:T(8,128)(2,1)S(1)} %copy-done.12), channel_id=1, source_target_pairs={{0,64},{32,96},{64,0},{96,32},{1,65},{33,97},{65,1},{97,33},{2,66}... | collective-permute-start | bytes 2359304 | tf_op jit(solution)/shard_map/ppermute | solution.py:41
  146.3 30.9 %collective-permute-start.26 = (bf16[4,12,64,128]{3,2,1,0:T(8,128)(2,1)S(1)}, bf16[4,12,64,128]{3,2,1,0:T(8,128)(2,1)S(1)}, u32[]{:S(2)}, u32[]{:S(2)}) collective-permute-start(bf16[4,12,64,128]{3,2,1,0:T(8,128)(2,1)S(1)} %copy-done.11), channel_id=1, source_target_pairs={{0,96},{32,0},{64,32},{96,64},{1,97},{33,1},{65,33},{97,65},{2,98}... | collective-permute-start | bytes 2359304 | tf_op jit(solution)/shard_map/ppermute | solution.py:41
  148.3 6.5 %collective-permute-start.21 = (bf16[12,64,128]{2,1,0:T(8,128)(2,1)S(1)}, bf16[12,64,128]{2,1,0:T(8,128)(2,1)S(1)}, u32[]{:S(2)}, u32[]{:S(2)}) collective-permute-start(bf16[12,64,128]{2,1,0:T(8,128)(2,1)S(1)} %get-tuple-element.49), channel_id=1, source_target_pairs={{0,32},{32,64},{64,96},{96,0},{1,33},{33,65},{65,97},{97,1},{2,34}... | collective-permute-start | bytes 589832 | tf_op jit(solution)/shard_map/ppermute | solution.py:41
  154.8 6.0 %collective-permute-start.22 = (bf16[12,64,128]{2,1,0:T(8,128)(2,1)S(1)}, bf16[12,64,128]{2,1,0:T(8,128)(2,1)S(1)}, u32[]{:S(2)}, u32[]{:S(2)}) collective-permute-start(bf16[12,64,128]{2,1,0:T(8,128)(2,1)S(1)} %get-tuple-element.51), channel_id=1, source_target_pairs={{0,64},{32,96},{64,0},{96,32},{1,65},{33,97},{65,1},{97,33},{2,66}... | collective-permute-start | bytes 589832 | tf_op jit(solution)/shard_map/ppermute | solution.py:41
  154.8 18.7 %collective-permute-start.23 = (bf16[12,64,128]{2,1,0:T(8,128)(2,1)S(1)}, bf16[12,64,128]{2,1,0:T(8,128)(2,1)S(1)}, u32[]{:S(2)}, u32[]{:S(2)}) collective-permute-start(bf16[12,64,128]{2,1,0:T(8,128)(2,1)S(1)} %get-tuple-element.50), channel_id=1, source_target_pairs={{0,96},{32,0},{64,32},{96,64},{1,97},{33,1},{65,33},{97,65},{2,98}... | collective-permute-start | bytes 589832 | tf_op jit(solution)/shard_map/ppermute | solution.py:41
  156.8 20.4 %copy-start.8 = (bf16[4,12,64,128]{3,2,1,0:T(8,128)(2,1)S(1)}, bf16[4,12,64,128]{3,2,1,0:T(8,128)(2,1)}, u32[]{:S(2)}) copy-start(bf16[4,12,64,128]{3,2,1,0:T(8,128)(2,1)} %get-tuple-element.38) | copy-start | bytes 2359300
  160.8 19.6 %collective-permute-start.14 = (bf16[512,512]{1,0:T(8,128)(2,1)S(1)}, bf16[512,512]{1,0:T(8,128)(2,1)S(1)}, u32[]{:S(2)}, u32[]{:S(2)}) collective-permute-start(bf16[512,512]{1,0:T(8,128)(2,1)S(1)} %get-tuple-element.32), channel_id=1, source_target_pairs={{0,2},{2,4},{4,6},{6,0},{1,3},{3,5},{5,7},{7,1},{8,10},{10,12},{12... | collective-permute-start | bytes 1572872 | tf_op jit(solution)/shard_map/ppermute | solution.py:41
  173.5 12.5 %collective-permute-start.16 = (bf16[512,512]{1,0:T(8,128)(2,1)S(1)}, bf16[512,512]{1,0:T(8,128)(2,1)S(1)}, u32[]{:S(2)}, u32[]{:S(2)}) collective-permute-start(bf16[512,512]{1,0:T(8,128)(2,1)S(1)} %get-tuple-element.33), channel_id=1, source_target_pairs={{0,6},{2,0},{4,2},{6,4},{1,7},{3,1},{5,3},{7,5},{8,14},{10,8},{12,... | collective-permute-start | bytes 1572872 | tf_op jit(solution)/shard_map/ppermute | solution.py:41
  177.2 12.5 %copy-start.3 = (f32[12,64,128]{2,1,0:T(8,128)S(1)}, f32[12,64,128]{2,1,0:T(8,128)}, u32[]{:S(2)}) copy-start(f32[12,64,128]{2,1,0:T(8,128)} %param.8) | copy-start | bytes 1179652
  177.6 12.1 %collective-permute-start.27 = (bf16[12,64,128]{2,1,0:T(8,128)(2,1)S(1)}, bf16[12,64,128]{2,1,0:T(8,128)(2,1)S(1)}, u32[]{:S(2)}, u32[]{:S(2)}) collective-permute-start(bf16[12,64,128]{2,1,0:T(8,128)(2,1)S(1)} %get-tuple-element.46), channel_id=1, source_target_pairs={{0,8},{8,16},{16,24},{24,0},{1,9},{9,17},{17,25},{25,1},{2,10},{10... | collective-permute-start | bytes 589832 | tf_op jit(solution)/shard_map/ppermute | solution.py:41
  177.7 12.0 %collective-permute-start.28 = (bf16[12,64,128]{2,1,0:T(8,128)(2,1)S(1)}, bf16[12,64,128]{2,1,0:T(8,128)(2,1)S(1)}, u32[]{:S(2)}, u32[]{:S(2)}) collective-permute-start(bf16[12,64,128]{2,1,0:T(8,128)(2,1)S(1)} %get-tuple-element.48), channel_id=1, source_target_pairs={{0,16},{8,24},{16,0},{24,8},{1,17},{9,25},{17,1},{25,9},{2,18},{10... | collective-permute-start | bytes 589832 | tf_op jit(solution)/shard_map/ppermute | solution.py:41
  179.5 10.2 %collective-permute-start.29 = (bf16[12,64,128]{2,1,0:T(8,128)(2,1)S(1)}, bf16[12,64,128]{2,1,0:T(8,128)(2,1)S(1)}, u32[]{:S(2)}, u32[]{:S(2)}) collective-permute-start(bf16[12,64,128]{2,1,0:T(8,128)(2,1)S(1)} %get-tuple-element.47), channel_id=1, source_target_pairs={{0,24},{8,0},{16,8},{24,16},{1,25},{9,1},{17,9},{25,17},{2,26},{10... | collective-permute-start | bytes 589832 | tf_op jit(solution)/shard_map/ppermute | solution.py:41
  186.1 7.8 %collective-permute-start.15 = (bf16[256,512]{1,0:T(8,128)(2,1)S(1)}, bf16[256,512]{1,0:T(8,128)(2,1)S(1)}, u32[]{:S(2)}, u32[]{:S(2)}) collective-permute-start(bf16[256,512]{1,0:T(8,128)(2,1)S(1)} %get-tuple-element.54), channel_id=1, source_target_pairs={{0,2},{2,4},{4,6},{6,0},{1,3},{3,5},{5,7},{7,1},{8,10},{10,12},{12... | collective-permute-start | bytes 786440 | tf_op jit(solution)/shard_map/ppermute | solution.py:41
  186.9 7.0 %collective-permute-start.17 = (bf16[256,512]{1,0:T(8,128)(2,1)S(1)}, bf16[256,512]{1,0:T(8,128)(2,1)S(1)}, u32[]{:S(2)}, u32[]{:S(2)}) collective-permute-start(bf16[256,512]{1,0:T(8,128)(2,1)S(1)} %get-tuple-element.55), channel_id=1, source_target_pairs={{0,6},{2,0},{4,2},{6,4},{1,7},{3,1},{5,3},{7,5},{8,14},{10,8},{12,... | collective-permute-start | bytes 786440 | tf_op jit(solution)/shard_map/ppermute | solution.py:41
